TPU v7x, 32 devices: a whole 2x2x4 slice. The times are simulated.
32 devices in a mesh: scene: 4 (over z), tile: 8 (over y, x, core).
Axes of the slice: x: 2, y: 2, z: 4, core: 2. Of those that a mesh axis runs over, the one named last changes fastest.
Arguments:
- tokens: bfloat16 [32, 16, 128, 1024], P(('scene', 'tile')), may hold values from -40 to 40
- gain: bfloat16 [1024], replicated, may hold values from 0.5 to 1.5
- w_qkv: bfloat16 [1024, 3072], replicated, may hold values from -4 to 4
- w_proj: bfloat16 [1024, 1024], replicated, may hold values from -1 to 1
- scene_first: int32 [32], replicated, may hold values 0 or 1
- window_valid: int32 [32, 16], P(('scene', 'tile')), may hold values 0 or 1
- partner_tile: int32 [4, 8, 16, 1], P('scene'), may hold values from 0 to 7; in each aligned block of 16 rows (0 to 15, 16 to 31, ..., all dimensions but the last counted through in order) at most 4 rows name the same one
- partner_panel: int32 [4, 8, 16], P('scene'), may hold values from 0 to 15
Outputs:
- update: bfloat16 [32, 16, 128, 1024], P(('scene', 'tile'))
Inputs may be any that keep to these rules, and one draw needn't show every extreme that they name: `partner_tile`: among the 16 panels of one slab at most 4 name the same tile, and in every draw some slab names some tile exactly 4 times. `scene_first`: slab 0 opens a scene group whatever its entry.
All inputs are finite; a program needn't handle non-finite values. No bound on the sum of `window_valid` on one device may be relied on, other than what follows from the above.
Results may differ from a plain program's by a relative error of at most 0.009.
Values may be sent and summed in bfloat16 or wider, within the bound.
No kernel may reach another device: no remote copies, remote signals or barrier semaphores. Data moves between devices by JAX's collectives and lax.ppermute only.
A program may use at most 256 MiB of HBM per device.

v0:
```python
import jax
import jax.numpy as jnp
from jax import lax
from jax.sharding import PartitionSpec as P

HEADS = 16


NORM_EPS = 1e-05


def padded(block, sides, width):
    for axis, dim in sides:
        count = lax.axis_size(axis)
        forward = [(i, i + 1) for i in range(count - 1)]
        backward = [(target, source) for source, target in forward]
        low = lax.ppermute(
            lax.slice_in_dim(block, block.shape[dim] - width, None, axis=dim), axis, forward
        )
        high = lax.ppermute(lax.slice_in_dim(block, 0, width, axis=dim), axis, backward)
        block = jnp.concatenate([low, block, high], axis=dim)
    return block


def to_panels(grid_in):
    feat_dim = grid_in.shape[2]
    blocks = grid_in.shape[1] // 16
    return (
        grid_in.reshape(2, 8, blocks, 16, feat_dim)
        .transpose(0, 2, 1, 3, 4)
        .reshape(2 * blocks, 128, feat_dim)
    )


def from_panels(panel_in):
    feat_dim = panel_in.shape[2]
    blocks = panel_in.shape[0] // 2
    return (
        panel_in.reshape(2, blocks, 8, 16, feat_dim)
        .transpose(0, 2, 1, 3, 4)
        .reshape(16, blocks * 16, feat_dim)
    )


def attend_blocks(queries, pair_blocks, keep_blocks, head_count):
    panel_count, query_rows, feat_dim = queries.shape
    head_width = feat_dim // head_count
    query_heads = queries.reshape(panel_count, query_rows, head_count, head_width)
    score_list = []
    value_list = []
    for pair_rows, keep_rows in zip(pair_blocks, keep_blocks):
        key_length = pair_rows.shape[1]
        key_heads = pair_rows[:, :, :feat_dim].reshape(
            panel_count, key_length, head_count, head_width
        )
        value_list.append(
            pair_rows[:, :, feat_dim:].reshape(panel_count, key_length, head_count, head_width)
        )
        block_scores = jnp.einsum(
            "pqhd,pkhd->phqk", query_heads, key_heads, preferred_element_type=jnp.float32
        ) * head_width ** (-0.5)
        score_list.append(jnp.where(keep_rows[:, None, None, :], block_scores, -jnp.inf))
    scores = jnp.concatenate(score_list, axis=-1)
    row_max = jnp.max(scores, axis=-1, keepdims=True)
    exponent = jnp.exp(scores - row_max)
    weights = (exponent / jnp.sum(exponent, axis=-1, keepdims=True)).astype(jnp.bfloat16)
    mixed_out = jnp.zeros((panel_count, query_rows, head_count, head_width), jnp.float32)
    offset = 0
    for value_heads in value_list:
        width = value_heads.shape[1]
        mixed_out = mixed_out + jnp.einsum(
            "phqk,pkhd->pqhd",
            weights[..., offset : offset + width],
            value_heads,
            preferred_element_type=jnp.float32,
        )
        offset = offset + width
    return mixed_out.reshape(panel_count, query_rows, feat_dim)


def per_device(tokens, gain, w_qkv, w_proj, scene_first, window_valid, partner_tile, partner_panel):
    grid_in = tokens[0]
    tok_rows, tok_cols, feat_dim = grid_in.shape
    ordered = to_panels(grid_in)
    panel_count = ordered.shape[0]
    halfway = panel_count // 2
    values = ordered.reshape(panel_count * 128, feat_dim).astype(jnp.float32)
    centred = values - jnp.mean(values, axis=-1, keepdims=True)
    spread = jnp.mean(centred * centred, axis=-1, keepdims=True)
    normed = (centred * lax.rsqrt(spread + NORM_EPS) * gain.astype(jnp.float32)).astype(
        jnp.bfloat16
    )
    w_pairs = w_qkv[:, feat_dim:]
    queries = (
        jnp.dot(normed, w_qkv[:, :feat_dim], preferred_element_type=jnp.float32)
        .astype(jnp.bfloat16)
        .reshape(panel_count, 128, feat_dim)
    )
    pairs = (
        jnp.dot(normed, w_pairs, preferred_element_type=jnp.float32)
        .astype(jnp.bfloat16)
        .reshape(panel_count, 128, 2 * feat_dim)
    )
    extended = padded(pairs.reshape(2, halfway, 128, 2 * feat_dim), ((("scene", "tile"), 0),), 1)
    before = extended[0]
    after = extended[3]
    slab_count = scene_first.shape[0]
    slab_index = lax.axis_index(("scene", "tile"))
    after_index = jnp.minimum(slab_index + 1, slab_count - 1)
    own_first = jnp.logical_or(scene_first[slab_index] == 1, slab_index == 0)
    next_first = jnp.logical_or(scene_first[after_index] == 1, slab_index + 1 >= slab_count)
    always = jnp.ones((halfway, 128), dtype=bool)
    keep_before = jnp.broadcast_to(jnp.logical_not(own_first), (halfway, 128))
    keep_after = jnp.broadcast_to(jnp.logical_not(next_first), (halfway, 128))
    mix_upper = attend_blocks(
        queries[:halfway], (before, pairs[:halfway]), (keep_before, always), HEADS
    )
    mix_lower = attend_blocks(
        queries[halfway:], (pairs[halfway:], after), (always, keep_after), HEADS
    )
    own_mix = jnp.concatenate([mix_upper, mix_lower], axis=0)
    requests = partner_tile[0, :, :, 0]
    offsets = partner_panel[0]
    tile_count = requests.shape[0]
    capacity = 2 * max(1, panel_count // tile_count)
    panel_ids = jnp.arange(panel_count, dtype=jnp.int32)
    slot_ids = jnp.arange(capacity, dtype=jnp.int32)
    dest_ids = jnp.arange(tile_count, dtype=jnp.int32)
    same_dest = requests[:, :, None] == requests[:, None, :]
    earlier = panel_ids[:, None] < panel_ids[None, :]
    ranks = jnp.sum(jnp.logical_and(same_dest, earlier[None, :, :]).astype(jnp.int32), axis=1)
    tile_index = lax.axis_index("tile")
    own_dest = requests[tile_index]
    own_rank = ranks[tile_index]
    chooser = jnp.logical_and(
        own_dest[None, None, :] == dest_ids[:, None, None],
        own_rank[None, None, :] == slot_ids[None, :, None],
    ).astype(jnp.bfloat16)
    to_self = jnp.logical_and(
        (requests == tile_index)[:, :, None], ranks[:, :, None] == slot_ids[None, None, :]
    ).astype(jnp.float32)
    wanted = (offsets[:, :, None] == panel_ids[None, None, :]).astype(jnp.float32)
    server = jnp.einsum("upc,upj->ucj", to_self, wanted).astype(jnp.bfloat16)
    full_keep = jnp.ones((tile_count * capacity, 128), dtype=bool)
    served = jnp.einsum("ucj,jtf->uctf", server, pairs, preferred_element_type=jnp.float32).astype(
        jnp.bfloat16
    )
    outgoing = jnp.einsum(
        "dcp,ptf->dctf", chooser, queries, preferred_element_type=jnp.float32
    ).astype(jnp.bfloat16)
    asked = lax.all_to_all(outgoing, "tile", split_axis=0, concat_axis=0, tiled=True)
    flat_pairs = served.reshape(tile_count * capacity, 128, 2 * feat_dim)
    answer = attend_blocks(
        asked.reshape(tile_count * capacity, 128, feat_dim), (flat_pairs,), (full_keep,), HEADS
    ).astype(jnp.bfloat16)
    returned = lax.all_to_all(
        answer.reshape(tile_count, capacity, 128, feat_dim),
        "tile",
        split_axis=0,
        concat_axis=0,
        tiled=True,
    )
    cross_mix = jnp.einsum(
        "dcp,dctf->ptf", chooser, returned, preferred_element_type=jnp.float32
    ).astype(jnp.bfloat16)
    window_gate = window_valid[0].astype(jnp.float32)[:, None, None]
    blended = (window_gate * own_mix + cross_mix.astype(jnp.float32)).astype(jnp.bfloat16)
    result = jnp.dot(
        blended.reshape(-1, feat_dim), w_proj, preferred_element_type=jnp.float32
    ).astype(jnp.bfloat16)
    grid_out = from_panels(result.reshape(panel_count, 128, feat_dim))
    return grid_out.reshape(1, tok_rows, tok_cols, feat_dim)


def solution(mesh):
    in_specs = (
        P(("scene", "tile"), None, None, None),
        P(),
        P(),
        P(),
        P(),
        P(("scene", "tile"), None),
        P("scene", None, None, None),
        P("scene", None, None),
    )
    out_specs = P(("scene", "tile"), None, None, None)
    return jax.shard_map(
        per_device, mesh=mesh, in_specs=in_specs, out_specs=out_specs, check_vma=False
    )
```

profile of v0, /device:TPU:24, one launch (start us, length us, event | category | flops | bytes accessed | tf_op | source)
XLA Modules:
  0.0 419.4 jit_solution(993031663222207445)
XLA Ops:
  17.7 9.3 %convolution_convert_fusion.1 = bf16[2048,2048]{1,0:T(8,128)(2,1)S(1)} fusion(bf16[2048,1024]{1,0:T(8,128)(2,1)S(1)} %fusion.15, bf16[1024,3072]{1,0:T(8,128)(2,1)S(1)} %bitcast.132), kind=kOutput, calls=%fused_computation.32 | convolution fusion | flops 8594128896 | bytes 16777216 | tf_op jit(solution)/shard_map/dot_general | solution.py:100
  34.8 5.7 %collective-permute-start.1 = (bf16[1,8,128,2048]{3,2,1,0:T(8,128)(2,1)}, bf16[1,8,128,2048]{3,2,1,0:T(8,128)(2,1)}, u32[]{:S(2)}, u32[]{:S(2)}) collective-permute-start(bf16[1,8,128,2048]{3,2,1,0:T(8,128)(2,1)} %bitcast.19), channel_id=1, source_target_pairs={{1,0},{2,1},{3,2},{4,3},{5,4},{6,5},{7,6},{8,7},{9,8},{10,9},{11,1... | collective-permute-start | bytes 12582920 | tf_op jit(solution)/shard_map/ppermute | solution.py:20
  40.4 6.2 %convolution_convert_fusion.4 = bf16[2048,1024]{1,0:T(8,128)(2,1)} fusion(bf16[2048,1024]{1,0:T(8,128)(2,1)S(1)} %fusion.15, bf16[1024,3072]{1,0:T(8,128)(2,1)S(1)} %bitcast.132), kind=kOutput, calls=%fused_computation.50 | convolution fusion | flops 4297064448 | bytes 10485760 | tf_op jit(solution)/shard_map/dot_general | solution.py:95
  47.4 8.7 %convolution_convert_fusion.2 = bf16[8,4,128,1024]{3,0,2,1:T(8,128)(2,1)} fusion(bf16[16,128,1024]{2,1,0:T(8,128)(2,1)} %bitcast.112, pred[4,16]{1,0:T(4,128)(4,1)S(1)} %iota_compare_fusion.5, pred[8,16]{1,0:T(8,128)(4,1)S(1)} %iota_compare_fusion.4), kind=kOutput, calls=%fused_computation.33 | convolution fusion | flops 138412544 | bytes 12583104 | tf_op jit(solution)/shard_map/dcp,ptf->dctf/dot_general | solution.py:148
  56.1 11.3 %copy.159 = bf16[8,4,128,1024]{3,2,1,0:T(8,128)(2,1)} copy(bf16[8,4,128,1024]{3,0,2,1:T(8,128)(2,1)} %convolution_convert_fusion.2) | data formatting | bytes 16777216 | tf_op jit(solution)/shard_map/convert_element_type | solution.py:150
  78.8 6.4 %reshape.229 = bf16[8,128,16,64]{3,2,1,0:T(8,128)(2,1)} reshape(bf16[1024,1024]{1,0:T(8,128)(2,1)} %get-tuple-element.13) | data formatting | bytes 4194304 | tf_op jit(solution)/shard_map/reshape | solution.py:48
  85.2 5.8 %copy.137 = bf16[8,128,16,64]{1,3,2,0:T(8,128)(2,1)} copy(bf16[8,128,16,64]{3,2,1,0:T(8,128)(2,1)} %reshape.229) | data formatting | bytes 4194304 | tf_op jit(solution)/shard_map/reshape | solution.py:48
  104.2 6.5 %reshape.230 = bf16[8,128,16,64]{3,2,1,0:T(8,128)(2,1)} reshape(bf16[1024,1024]{1,0:T(8,128)(2,1)} %get-tuple-element.14) | data formatting | bytes 4194304 | tf_op jit(solution)/shard_map/reshape | solution.py:48
  110.6 5.8 %copy.146 = bf16[8,128,16,64]{1,3,2,0:T(8,128)(2,1)} copy(bf16[8,128,16,64]{3,2,1,0:T(8,128)(2,1)} %reshape.230) | data formatting | bytes 4194304 | tf_op jit(solution)/shard_map/reshape | solution.py:48
  129.3 25.4 %convolution_convert_fusion = bf16[8,4,128,2048]{3,0,2,1:T(8,128)(2,1)} fusion(bf16[16,128,2048]{2,1,0:T(8,128)(2,1)} %bitcast.111, bf16[8,4,16,1]{2,1,0,3:T(4,128)(2,1)S(1)} %fusion.43), kind=kOutput, calls=%fused_computation.13 | convolution fusion | flops 276824064 | bytes 25166848 | tf_op jit(solution)/shard_map/ucj,jtf->uctf/dot_general | solution.py:145
  154.7 15.0 %copy.156 = bf16[8,4,128,2048]{3,2,1,0:T(8,128)(2,1)S(1)} copy(bf16[8,4,128,2048]{3,0,2,1:T(8,128)(2,1)} %convolution_convert_fusion) | data formatting | bytes 33554432 | tf_op jit(solution)/shard_map/convert_element_type | solution.py:145
  169.7 6.5 %fusion.55 = (bf16[32,128,1024]{2,1,0:T(8,128)(2,1)}, bf16[32,128,1024]{2,1,0:T(8,128)(2,1)}) fusion(bf16[32,128,2048]{2,1,0:T(8,128)(2,1)S(1)} %bitcast.107), kind=kLoop, calls=%fused_computation.81 | loop fusion | bytes 33554432 | tf_op jit(solution)/shard_map/slice | solution.py:53
  176.2 11.9 %copy.161 = bf16[32,128,1024]{1,2,0:T(8,128)(2,1)} copy(bf16[32,128,1024]{2,1,0:T(8,128)(2,1)} %get-tuple-element.5) | data formatting | bytes 16777216 | tf_op jit(solution)/shard_map/slice | solution.py:53
  188.1 11.9 %copy.157 = bf16[32,128,1024]{1,2,0:T(8,128)(2,1)} copy(bf16[32,128,1024]{2,1,0:T(8,128)(2,1)} %get-tuple-element.6) | data formatting | bytes 16777216 | tf_op jit(solution)/shard_map/slice | solution.py:57
  200.1 7.1 %fusion.66 = (f32[8,16,128]{2,1,0:T(8,128)S(1)}, f32[8,16,128,128]{2,3,1,0:T(8,128)}) fusion(bf16[8,128,16,64]{1,3,2,0:T(8,128)(2,1)} %copy.137, bf16[8,128,16,64]{1,3,2,0:T(8,128)(2,1)} %bitcast.125), kind=kOutput, calls=%fused_computation.92 | convolution fusion | flops 272613376 | bytes 12648448 | tf_op jit(solution)/shard_map/pqhd,pkhd->phqk/dot_general | solution.py:59
  233.3 11.4 %copy.160 = bf16[8,4,128,1024]{2,3,1,0:T(8,128)(2,1)} copy(bf16[8,4,128,1024]{3,2,1,0:T(8,128)(2,1)} %all-to-all-done) | data formatting | bytes 16777216 | tf_op jit(solution)/shard_map/all_to_all | solution.py:151
  244.7 21.7 %fusion.67 = (f32[32,16,128]{2,1,0:T(8,128)S(1)}, f32[32,16,128,128]{2,3,1,0:T(8,128)}) fusion(bf16[32,128,16,64]{1,3,2,0:T(8,128)(2,1)} %bitcast.123, bf16[32,128,16,64]{1,3,2,0:T(8,128)(2,1)} %bitcast.122), kind=kOutput, calls=%fused_computation.93 | convolution fusion | flops 1098907776 | bytes 50593792 | tf_op jit(solution)/shard_map/sub | solution.py:65
  266.4 18.6 %fusion.19 = bf16[32,16,64,128]{3,2,1,0:T(8,128)(2,1)} fusion(bf16[32,128,16,64]{1,3,2,0:T(8,128)(2,1)} %bitcast.121, f32[32,16,128,128]{2,3,1,0:T(8,128)} %get-tuple-element.30, f32[32,16,128]{2,1,0:T(8,128)S(1)} %get-tuple-element.29), kind=kOutput, calls=%fused_computation.34 | convolution fusion | flops 1094713344 | bytes 50593792 | tf_op jit(solution)/shard_map/phqk,pkhd->pqhd/dot_general | solution.py:71
  285.0 14.7 %copy.163 = bf16[8,4,128,1024]{3,1,2,0:T(4,128)(2,1)} copy(bf16[8,4,128,1024]{2,3,1,0:T(8,128)(2,1)} %bitcast.124) | data formatting | bytes 16777216 | tf_op jit(solution)/shard_map/convert_element_type | solution.py:155
  304.6 10.1 %divide_convert_fusion.2 = bf16[8,16,128,256]{2,3,1,0:T(8,128)(2,1)} fusion(f32[8,16,128,128]{2,3,1,0:T(8,128)} %get-tuple-element.28, f32[8,16,128,128]{2,3,1,0:T(8,128)} %copy-done.1, f32[8,16,128]{2,1,0:T(8,128)S(1)} %fusion.9, f32[8,16,128]{2,1,0:T(8,128)S(1)} %reduce_max.51), kind=kLoop, calls=%fused_computation.11 | loop fusion | flops 16777216 | bytes 25296896 | tf_op jit(solution)/shard_map/convert_element_type | solution.py:66
  350.0 5.6 %fusion.8 = f32[8,16,128]{2,1,0:T(8,128)S(1)} fusion(f32[8,16,128,128]{2,3,1,0:T(8,128)S(1)} %get-tuple-element.24, f32[8,16,128,128]{2,3,1,0:T(8,128)} %get-tuple-element.22, f32[8,16,128]{2,1,0:T(8,128)S(1)} %reduce_max.54), kind=kLoop, calls=%fused_computation.14 | loop fusion | flops 12566528 | bytes 16908288 | tf_op jit(solution)/shard_map/reduce_sum | solution.py:66
  363.7 5.7 %copy.153 = f32[8,128,1024]{2,0,1:T(8,128)} copy(f32[8,128,1024]{1,2,0:T(8,128)} %bitcast.114) | data formatting | bytes 8388608 | tf_op jit(solution)/shard_map/reshape | solution.py:78
  369.4 29.2 %all-to-all-done.1 = bf16[8,4,128,1024]{3,1,2,0:T(4,128)(2,1)} async-done(((bf16[8,4,128,1024]{3,1,2,0:T(4,128)(2,1)}), bf16[8,4,128,1024]{3,1,2,0:T(4,128)(2,1)}, u32[]{:S(2)}, u32[]{:S(2)}) %all-to-all-start.1) | async-done | bytes 8388640 | tf_op jit(solution)/shard_map/all_to_all | solution.py:156
  398.7 10.8 %fusion.11 = bf16[16,128,1024]{2,0,1:T(8,128)(2,1)S(1)} fusion(f32[8,128,1024]{2,0,1:T(8,128)} %copy.153, f32[8,128,1024]{2,0,1:T(8,128)} %copy.152, f32[16]{0:T(128)S(1)} %convert_bitcast_fusion.1, bf16[8,4,128,1024]{3,1,2,0:T(4,128)(2,1)} %all-to-all-done.1, pred[4,16]{1,0:T(4,128)(4,1)S(1)} %copy-done.12, pred[8,16]{1,0:T(8,128)(4,1)S(1)} %copy-done.14), kind=kOutput, calls=%fused_computation.18 | convolution fusion | flops 146801152 | bytes 20971776 | tf_op jit(solution)/shard_map/dcp,dctf->ptf/dot_general | solution.py:163
  (105 shorter events, 146.1 us)
Async XLA Ops:
  0.0 411.7 %copy-start = (bf16[1024,1024]{1,0:T(8,128)(2,1)S(1)}, bf16[1024,1024]{1,0:T(8,128)(2,1)}, u32[]{:S(2)}) copy-start(bf16[1024,1024]{1,0:T(8,128)(2,1)} %param.11) | copy-start | bytes 6291460
  0.0 6.1 %copy-start.2 = (bf16[1,16,128,1024]{3,2,1,0:T(8,128)(2,1)S(1)}, bf16[1,16,128,1024]{3,2,1,0:T(8,128)(2,1)}, u32[]{:S(2)}) copy-start(bf16[1,16,128,1024]{3,2,1,0:T(8,128)(2,1)} %param.8) | copy-start | bytes 12582916
  10.6 4.3 %copy-start.15 = (bf16[1024]{0:T(1024)(128)(2,1)S(1)}, bf16[1024]{0:T(1024)(128)(2,1)}, u32[]{:S(2)}) copy-start(bf16[1024]{0:T(1024)(128)(2,1)} %param.9) | copy-start | bytes 6148
  14.9 2.2 slice-start.2
  14.9 2.9 slice-start.3
  27.1 5.7 %copy-start.4 = (bf16[2048,2048]{1,0:T(8,128)(2,1)}, bf16[2048,2048]{1,0:T(8,128)(2,1)S(1)}, u32[]{:S(2)}) copy-start(bf16[2048,2048]{1,0:T(8,128)(2,1)S(1)} %convolution_convert_fusion.1) | copy-start | bytes 25165828
  32.8 179.1 %collective-permute-start = (bf16[1,8,128,2048]{3,2,1,0:T(8,128)(2,1)}, bf16[1,8,128,2048]{3,2,1,0:T(8,128)(2,1)}, u32[]{:S(2)}, u32[]{:S(2)}) collective-permute-start(bf16[1,8,128,2048]{3,2,1,0:T(8,128)(2,1)} %bitcast.5), channel_id=1, source_target_pairs={{0,1},{1,2},{2,3},{3,4},{4,5},{5,6},{6,7},{7,8},{8,9},{9,10},{10,1... | collective-permute-start | bytes 12582920 | tf_op jit(solution)/shard_map/ppermute | solution.py:17
  34.8 298.4 %collective-permute-start.1 = (bf16[1,8,128,2048]{3,2,1,0:T(8,128)(2,1)}, bf16[1,8,128,2048]{3,2,1,0:T(8,128)(2,1)}, u32[]{:S(2)}, u32[]{:S(2)}) collective-permute-start(bf16[1,8,128,2048]{3,2,1,0:T(8,128)(2,1)} %bitcast.19), channel_id=1, source_target_pairs={{1,0},{2,1},{3,2},{4,3},{5,4},{6,5},{7,6},{8,7},{9,8},{10,9},{11,1... | collective-permute-start | bytes 12582920 | tf_op jit(solution)/shard_map/ppermute | solution.py:20
  40.4 6.3 %copy-start.10 = (s32[1,8,16,1]{2,3,1,0:T(1,128)S(1)}, s32[1,8,16,1]{2,3,1,0:T(1,128)}, u32[]{:S(2)}) copy-start(s32[1,8,16,1]{2,3,1,0:T(1,128)} %param.14) | copy-start | bytes 1540
  67.4 5.6 %copy-start.16 = (s32[32]{0:T(128)S(1)}, s32[32]{0:T(128)}, u32[]{:S(2)}) copy-start(s32[32]{0:T(128)} %param.12) | copy-start | bytes 388
  67.4 165.9 %all-to-all-start = ((bf16[8,4,128,1024]{3,2,1,0:T(8,128)(2,1)}), bf16[8,4,128,1024]{3,2,1,0:T(8,128)(2,1)}, u32[]{:S(2)}, u32[]{:S(2)}) async-start(bf16[8,4,128,1024]{3,2,1,0:T(8,128)(2,1)} %copy.159), calls=%async_computation | async-start | bytes 16777216 | tf_op jit(solution)/shard_map/all_to_all | solution.py:151
  116.4 12.7 %copy-start.17 = (s32[1,8,16]{2,1,0:T(8,128)S(1)}, s32[1,8,16]{2,1,0:T(8,128)}, u32[]{:S(2)}) copy-start(s32[1,8,16]{2,1,0:T(8,128)} %param.15) | copy-start | bytes 1540
  188.1 11.9 %copy-start.18 = (s32[1,16]{1,0:T(1,128)S(1)}, s32[1,16]{1,0:T(1,128)}, u32[]{:S(2)}) copy-start(s32[1,16]{1,0:T(1,128)} %param.13) | copy-start | bytes 196
  200.0 7.1 %copy-start.5 = (bf16[8,128,16,64]{1,3,2,0:T(8,128)(2,1)S(1)}, bf16[8,128,16,64]{1,3,2,0:T(8,128)(2,1)}, u32[]{:S(2)}) copy-start(bf16[8,128,16,64]{1,3,2,0:T(8,128)(2,1)} %copy.146) | copy-start | bytes 6291460
  200.0 7.1 %copy-start.9 = (bf16[8,128,1024]{1,2,0:T(8,128)(2,1)S(1)}, bf16[8,128,1024]{1,2,0:T(8,128)(2,1)}, u32[]{:S(2)}) copy-start(bf16[8,128,1024]{1,2,0:T(8,128)(2,1)} %copy.145) | copy-start | bytes 6291460
  224.6 3.2 copy-start.1
  299.6 99.0 %all-to-all-start.1 = ((bf16[8,4,128,1024]{3,1,2,0:T(4,128)(2,1)}), bf16[8,4,128,1024]{3,1,2,0:T(4,128)(2,1)}, u32[]{:S(2)}, u32[]{:S(2)}) async-start(bf16[8,4,128,1024]{3,1,2,0:T(4,128)(2,1)} %copy.163), calls=%async_computation.1 | async-start | bytes 16777216 | tf_op jit(solution)/shard_map/all_to_all | solution.py:156
  318.6 5.2 %copy-start.3 = (bf16[8,16,128,256]{2,3,1,0:T(8,128)(2,1)S(1)}, bf16[8,16,128,256]{2,3,1,0:T(8,128)(2,1)}, u32[]{:S(2)}) copy-start(bf16[8,16,128,256]{2,3,1,0:T(8,128)(2,1)} %divide_convert_fusion.2) | copy-start | bytes 25165828
  318.6 5.8 %copy-start.8 = (bf16[8,128,1024]{1,2,0:T(8,128)(2,1)S(1)}, bf16[8,128,1024]{1,2,0:T(8,128)(2,1)}, u32[]{:S(2)}) copy-start(bf16[8,128,1024]{1,2,0:T(8,128)(2,1)} %copy.134) | copy-start | bytes 6291460
  345.8 9.8 %slice-start = ((s8[8388608]{0:T(1024)(128)(4,1)}), s8[4194304]{0:T(1024)(128)(4,1)S(1)}, s32[]{:S(2)}) async-start(s8[8388608]{0:T(1024)(128)(4,1)} %bitcast.105), calls=%async_computation.2 | async-start | bytes 8388608
  350.0 5.6 %slice-start.1 = ((s8[8388608]{0:T(1024)(128)(4,1)}), s8[4194304]{0:T(1024)(128)(4,1)S(1)}, s32[]{:S(2)}) async-start(s8[8388608]{0:T(1024)(128)(4,1)} %bitcast.105), calls=%async_computation.3 | async-start | bytes 8388608
  355.6 3.3 copy-start.6
  360.5 38.2 %copy-start.12 = (pred[4,16]{1,0:T(4,128)(4,1)S(1)}, pred[4,16]{1,0:T(4,128)(4,1)}, u32[]{:S(2)}) copy-start(pred[4,16]{1,0:T(4,128)(4,1)} %copy-done.11) | copy-start | bytes 196
  360.5 38.2 %copy-start.14 = (pred[8,16]{1,0:T(8,128)(4,1)S(1)}, pred[8,16]{1,0:T(8,128)(4,1)}, u32[]{:S(2)}) copy-start(pred[8,16]{1,0:T(8,128)(4,1)} %copy-done.13) | copy-start | bytes 388
  (3 other events, 2.6 us)
where the time goes:
time: 427 us; the launch traced here: 419 us
  local copies, waits for them, and re-layouts  196 us (46%)
  matrix products  138 us (32%)
  other arithmetic  36.6 us (9%)
  waiting for transfers between devices  29.2 us (7%)
  starting transfers between devices  18.1 us (4%)
    slice x8, local copies, waits for them, and re-layouts, attend_blocks(): pair_rows[:, :, :feat_dim]  43.6 us
    slice x7, local copies, waits for them, and re-layouts, attend_blocks(): pair_rows[:, :, feat_dim:]  37.2 us
    dot_general x5, matrix products, attend_blocks(): jnp.einsum('phqk,pkhd->pqhd', weights[..., offset:offset + width], value_...  30.5 us
    all_to_all x1, waiting for transfers between devices, per_device(): lax.all_to_all(answer.reshape(tile_count, capacity, 128, feat_dim), 'tile...  29.2 us
    dot_general x1, matrix products, per_device(): jnp.einsum('ucj,jtf->uctf', server, pairs, preferred_element_type=jnp.flo...  25.4 us
    reshape x4, local copies, waits for them, and re-layouts, attend_blocks(): queries.reshape(panel_count, query_rows, head_count, head_width)  24.5 us
    sub x1, matrix products, attend_blocks(): exponent = jnp.exp(scores - row_max)  21.7 us
    dot_general x4, matrix products, attend_blocks(): jnp.einsum('pqhd,pkhd->phqk', query_heads, key_heads, preferred_element_t...  20 us
  transfers between devices with their start and end apart: 4, of which 1 were waited for; matrix products, arithmetic and copies ran while one was open for 74% of the time, Pallas kernels for 0%

commit v1 on v0

v1 whole, which is shorter than its diff:
```python
import functools

import jax
import jax.numpy as jnp
from jax import lax
from jax.experimental import pallas as pl
from jax.experimental.pallas import tpu as pltpu
from jax.sharding import PartitionSpec as P

HEADS = 16
NORM_EPS = 1e-05
LOG2E = 1.4426950408889634
VMEM_LIMIT = 56 * 1024 * 1024
GROUP = 4


def layer_norm(rows, gain_row):
    values = rows.astype(jnp.float32)
    centred = values - jnp.mean(values, axis=-1, keepdims=True)
    spread = jnp.mean(centred * centred, axis=-1, keepdims=True)
    return (centred * lax.rsqrt(spread + NORM_EPS) * gain_row.astype(jnp.float32)).astype(jnp.bfloat16)


def dot_f32(left, right):
    return jnp.dot(left, right, preferred_element_type=jnp.float32)


def dot_t(left, right):
    return lax.dot_general(left, right, (((1,), (1,)), ((), ())), preferred_element_type=jnp.float32)


def low_lanes(rows, width, head_width):
    return lax.broadcasted_iota(jnp.int32, (rows, width), 1) < head_width


def pack_kernel(tiles, panels, cap, me_ref, tile_ref, panel_ref, tok_ref, *rest):
    outs, sems = rest[: tiles - 1], rest[tiles - 1]
    me = me_ref[0]
    counts = []
    for r in range(1, tiles):
        asker = me ^ r
        out = outs[r - 1]

        def body(p, count, asker=asker, out=out, r=r):
            hit = jnp.logical_and(tile_ref[asker * panels + p] == me, count < cap)

            @pl.when(hit)
            def _():
                j = panel_ref[asker * panels + p]
                pltpu.make_async_copy(
                    tok_ref.at[j // (panels // 2), :, j % (panels // 2)], out.at[count], sems.at[r, count]
                ).start()

            return count + hit.astype(jnp.int32)

        counts.append(lax.fori_loop(0, panels, body, jnp.int32(0)))
    for r in range(1, tiles):
        for c in range(cap):

            @pl.when(c < counts[r - 1])
            def _(r=r, c=c):
                pltpu.make_async_copy(tok_ref.at[0, :, 0], outs[r - 1].at[c], sems.at[r, c]).wait()


def pack(me, tile_table, panel_table, tok, tiles, cap):
    panels = 2 * tok.shape[2]
    block = (cap, tok.shape[1], tok.shape[3], tok.shape[4])
    smem = pl.BlockSpec(memory_space=pltpu.SMEM)
    anym = pl.BlockSpec(memory_space=pl.ANY)
    return pl.pallas_call(
        functools.partial(pack_kernel, tiles, panels, cap),
        out_shape=[jax.ShapeDtypeStruct(block, tok.dtype)] * (tiles - 1),
        in_specs=[smem, smem, smem, anym],
        out_specs=[anym] * (tiles - 1),
        scratch_shapes=[pltpu.SemaphoreType.DMA((tiles, cap))],
        cost_estimate=pl.CostEstimate(flops=0, bytes_accessed=16 << 20, transcendentals=0),
    )(me, tile_table, panel_table, tok)


def qkv_kernel(tok_ref, gain_ref, w_ref, q_ref, kv_ref):
    dims = tok_ref.shape
    feat = dims[-1]
    rows = dims[1] * dims[2] * dims[3]
    normed = layer_norm(tok_ref[...].reshape(rows, feat), gain_ref[...])
    q_ref[...] = dot_f32(normed, w_ref[:, :feat]).astype(jnp.bfloat16).reshape(q_ref.shape)
    kv_ref[...] = dot_f32(normed, w_ref[:, feat:]).astype(jnp.bfloat16).reshape(kv_ref.shape)


def project_own(tok, gain_row, w_qkv):
    halves, deep, wide, run, feat = tok.shape
    step = deep // 2
    spec = lambda width: pl.BlockSpec((1, step, wide, run, width), lambda i: (i // 2, i % 2, 0, 0, 0))
    tokens = halves * deep * wide * run
    return pl.pallas_call(
        qkv_kernel,
        grid=(halves * 2,),
        out_shape=[
            jax.ShapeDtypeStruct((halves, deep, wide, run, feat), jnp.bfloat16),
            jax.ShapeDtypeStruct((halves, deep, wide, run, 2 * feat), jnp.bfloat16),
        ],
        in_specs=[
            spec(feat),
            pl.BlockSpec((1, feat), lambda i: (0, 0)),
            pl.BlockSpec((feat, 3 * feat), lambda i: (0, 0), pipeline_mode=pl.Buffered(1)),
        ],
        out_specs=[spec(feat), spec(2 * feat)],
        compiler_params=pltpu.CompilerParams(vmem_limit_bytes=VMEM_LIMIT),
        cost_estimate=pl.CostEstimate(
            flops=2 * tokens * feat * 3 * feat, bytes_accessed=tokens * feat * 8 + feat * feat * 6, transcendentals=0
        ),
    )(tok, gain_row, w_qkv)


def window_kernel(head_width, keep_ref, edge_ref, q_ref, kvo_ref, gain_ref, w_ref, mix_ref, kv_s):
    deep, group, run, feat = edge_ref.shape
    length = deep * run
    rows = edge_ref[...].reshape(deep * group * run, feat)
    normed = layer_norm(rows, gain_ref[...])
    kv_s[...] = dot_f32(normed, w_ref[:, feat:]).astype(jnp.bfloat16).reshape(kv_s.shape)
    pair = 2 * head_width
    scale = LOG2E * head_width ** (-0.5)
    bias = jnp.where(
        jnp.logical_and(keep_ref[0] == 0, lax.broadcasted_iota(jnp.int32, (1, 2 * length), 1) < length), -jnp.inf, 0.0
    )
    low = low_lanes(length, pair, head_width)
    ones = jnp.ones((2 * length, pair), jnp.bfloat16)
    zero = jnp.zeros((length, pair), jnp.bfloat16)
    for i in range(group):

        def body(g, carry, i=i):
            at = pl.ds(pl.multiple_of(g * pair, pair), pair)
            at_v = pl.ds(pl.multiple_of(feat + g * pair, pair), pair)
            q = q_ref[0, :, i, :, at].reshape(length, pair)
            qs = jnp.concatenate([jnp.where(low, q, zero), jnp.where(low, zero, q)], axis=0)
            keys = jnp.concatenate(
                [kv_s[:, i, :, at].reshape(length, pair), kvo_ref[0, :, i, :, at].reshape(length, pair)], axis=0
            )
            vals = jnp.concatenate(
                [kv_s[:, i, :, at_v].reshape(length, pair), kvo_ref[0, :, i, :, at_v].reshape(length, pair)], axis=0
            )
            scores = dot_t(qs, keys) + bias
            peak = jnp.max(scores, axis=1, keepdims=True)
            weights = jnp.exp2((scores - peak) * scale).astype(jnp.bfloat16)
            both = dot_f32(weights, jnp.concatenate([vals, ones], axis=1))
            mixed = both[:, :pair] / both[:, pair:]
            out = jnp.where(low, mixed[:length], mixed[length:])
            mix_ref[:, i, :, at] = out.astype(jnp.bfloat16).reshape(deep, run, pair)
            return carry

        lax.fori_loop(0, feat // pair, body, 0, unroll=2)


def window_mix(half, keep, edge, q, kv_own, gain_row, w_qkv):
    deep, wide, run, feat = edge.shape
    group = min(GROUP, wide)
    head_width = feat // HEADS
    own = lambda width: pl.BlockSpec((1, deep, group, run, width), lambda i: (half, 0, i, 0, 0))
    flat = pl.BlockSpec((deep, group, run, feat), lambda i: (0, i, 0, 0))
    tokens = deep * wide * run
    return pl.pallas_call(
        functools.partial(window_kernel, head_width),
        grid=(wide // group,),
        out_shape=jax.ShapeDtypeStruct(edge.shape, jnp.bfloat16),
        in_specs=[
            pl.BlockSpec(memory_space=pltpu.SMEM),
            flat,
            own(feat),
            own(2 * feat),
            pl.BlockSpec((1, feat), lambda i: (0, 0)),
            pl.BlockSpec((feat, 3 * feat), lambda i: (0, 0), pipeline_mode=pl.Buffered(1)),
        ],
        out_specs=flat,
        scratch_shapes=[pltpu.VMEM((deep, group, run, 2 * feat), jnp.bfloat16)],
        compiler_params=pltpu.CompilerParams(vmem_limit_bytes=VMEM_LIMIT),
        cost_estimate=pl.CostEstimate(
            flops=2 * tokens * feat * 2 * feat + 8 * tokens * 256 * feat,
            bytes_accessed=tokens * feat * 10 + feat * feat * 6,
            transcendentals=tokens * 256 * HEADS,
        ),
    )(keep, edge, q, kv_own, gain_row, w_qkv)


def cross_kernel(tiles, head_width, group, me_ref, tile_ref, panel_ref, valid_ref, tok_ref, *rest):
    recv = rest[: tiles - 1]
    q_ref, up_ref, down_ref, gain_ref, w_ref, wp_ref, out_ref, got, kv_s, mixed_s, seen, sems = rest[tiles - 1 :]
    panels, deep, run, feat = got.shape
    half = panels // 2
    length = deep * run
    step = pl.program_id(0)
    me = me_ref[0]

    @pl.when(step == 0)
    def _():
        for t in range(tiles):
            seen[t] = 0

        def body(p, carry):
            source = tile_ref[me * panels + p]
            slot = seen[source]
            seen[source] = slot + 1
            j = panel_ref[me * panels + p]
            r = source ^ me

            @pl.when(r == 0)
            def _():
                pltpu.make_async_copy(tok_ref.at[j // half, :, j % half], got.at[p], sems.at[p]).start()

            for k in range(1, tiles):

                @pl.when(r == k)
                def _(k=k):
                    pltpu.make_async_copy(recv[k - 1].at[slot], got.at[p], sems.at[p]).start()

            return carry

        lax.fori_loop(0, panels, body, 0)

    for i in range(group):
        pltpu.make_async_copy(tok_ref.at[0, :, 0], got.at[step * group + i], sems.at[step * group + i]).wait()
    rows = got[pl.ds(step * group, group)].reshape(group * length, feat)
    normed = layer_norm(rows, gain_ref[...])
    kv_s[...] = dot_f32(normed, w_ref[:, feat:]).astype(jnp.bfloat16)
    pair = 2 * head_width
    scale = LOG2E * head_width ** (-0.5)
    low = low_lanes(length, pair, head_width)
    zero = jnp.zeros((length, pair), jnp.bfloat16)
    one = jnp.ones((length, pair), jnp.bfloat16)
    marks = jnp.concatenate([jnp.where(low, one, zero), jnp.where(low, zero, one)], axis=0)
    upper = step < half // group
    for i in range(group):
        gate = valid_ref[step * group + i].astype(jnp.float32)

        def body(g, carry, i=i, gate=gate):
            at = pl.ds(pl.multiple_of(g * pair, pair), pair)
            at_v = pl.ds(pl.multiple_of(feat + g * pair, pair), pair)
            q = q_ref[0, :, i, :, at].reshape(length, pair)
            key = kv_s[i * length : (i + 1) * length, at]
            val = kv_s[i * length : (i + 1) * length, at_v]
            keys = jnp.concatenate([jnp.where(low, key, zero), jnp.where(low, zero, key)], axis=0)
            vals = jnp.concatenate([jnp.where(low, val, zero), jnp.where(low, zero, val)], axis=0)
            scores = dot_t(q, keys)
            parts = []
            for h in range(2):
                part = scores[:, h * length : (h + 1) * length]
                peak = jnp.max(part, axis=1, keepdims=True)
                parts.append(jnp.exp2((part - peak) * scale).astype(jnp.bfloat16))
            both = dot_f32(jnp.concatenate(parts, axis=1), jnp.concatenate([vals, marks], axis=1))
            cross = (both[:, :pair] / both[:, pair:]).astype(jnp.bfloat16)
            own = jnp.where(
                upper, up_ref[:, i, :, at].reshape(length, pair), down_ref[:, i, :, at].reshape(length, pair)
            )
            blended = gate * own.astype(jnp.float32) + cross.astype(jnp.float32)
            mixed_s[i * length : (i + 1) * length, at] = blended.astype(jnp.bfloat16)
            return carry

        lax.fori_loop(0, feat // pair, body, 0, unroll=2)
    result = dot_f32(mixed_s[...], wp_ref[...]).astype(jnp.bfloat16)
    for i in range(group):
        out_ref[0, :, i] = result[i * length : (i + 1) * length].reshape(deep, run, feat)


def cross_and_project(me, tile_table, panel_table, valid, tok, recv, q, mix_up, mix_down, gain_row, w_qkv, w_proj):
    halves, deep, wide, run, feat = tok.shape
    panels = halves * wide
    tiles = len(recv) + 1
    group = min(GROUP, wide)
    per_half = wide // group
    head_width = feat // HEADS
    length = deep * run
    smem = pl.BlockSpec(memory_space=pltpu.SMEM)
    anym = pl.BlockSpec(memory_space=pl.ANY)
    whole = pl.BlockSpec((1, deep, group, run, feat), lambda i: (i // per_half, 0, i % per_half, 0, 0))
    up = pl.BlockSpec((deep, group, run, feat), lambda i: (0, jnp.minimum(i, per_half - 1), 0, 0))
    down = pl.BlockSpec((deep, group, run, feat), lambda i: (0, jnp.maximum(i - per_half, 0), 0, 0))
    tokens = panels * length
    return pl.pallas_call(
        functools.partial(cross_kernel, tiles, head_width, group),
        grid=(panels // group,),
        out_shape=jax.ShapeDtypeStruct(tok.shape, jnp.bfloat16),
        in_specs=[smem, smem, smem, smem, anym]
        + [anym] * (tiles - 1)
        + [
            whole,
            up,
            down,
            pl.BlockSpec((1, feat), lambda i: (0, 0)),
            pl.BlockSpec((feat, 3 * feat), lambda i: (0, 0), pipeline_mode=pl.Buffered(1)),
            pl.BlockSpec((feat, feat), lambda i: (0, 0), pipeline_mode=pl.Buffered(1)),
        ],
        out_specs=whole,
        scratch_shapes=[
            pltpu.VMEM((panels, deep, run, feat), jnp.bfloat16),
            pltpu.VMEM((group * length, 2 * feat), jnp.bfloat16),
            pltpu.VMEM((group * length, feat), jnp.bfloat16),
            pltpu.SMEM((tiles,), jnp.int32),
            pltpu.SemaphoreType.DMA((panels,)),
        ],
        compiler_params=pltpu.CompilerParams(vmem_limit_bytes=VMEM_LIMIT),
        cost_estimate=pl.CostEstimate(
            flops=2 * tokens * feat * 3 * feat + 8 * tokens * 128 * feat,
            bytes_accessed=tokens * feat * 8 + feat * feat * 8,
            transcendentals=tokens * 128 * HEADS,
        ),
    )(me, tile_table, panel_table, valid, tok, *recv, q, mix_up, mix_down, gain_row, w_qkv, w_proj)


def per_device(tokens, gain, w_qkv, w_proj, scene_first, window_valid, partner_tile, partner_panel):
    _, tok_rows, tok_cols, feat = tokens.shape
    run = 16
    wide = tok_cols // run
    tok = tokens.reshape(2, tok_rows // 2, wide, run, feat)
    gain_row = gain.reshape(1, feat)
    tiles = partner_tile.shape[1]
    panels = partner_tile.shape[2]
    cap = 2 * max(1, panels // tiles)
    slab_count = scene_first.shape[0]
    forward = [(i, i + 1) for i in range(slab_count - 1)]
    backward = [(i + 1, i) for i in range(slab_count - 1)]
    before = lax.ppermute(tok[1], ("scene", "tile"), forward)
    after = lax.ppermute(tok[0], ("scene", "tile"), backward)

    me = lax.axis_index("tile").reshape(1).astype(jnp.int32)
    tile_table = partner_tile.reshape(tiles * panels)
    panel_table = partner_panel.reshape(tiles * panels)
    outgoing = pack(me, tile_table, panel_table, tok, tiles, cap)
    recv = [
        lax.ppermute(outgoing[r - 1], "tile", [(i, i ^ r) for i in range(tiles)]) for r in range(1, tiles)
    ]

    slab_index = lax.axis_index(("scene", "tile"))
    after_index = jnp.minimum(slab_index + 1, slab_count - 1)
    own_first = jnp.logical_or(scene_first[slab_index] == 1, slab_index == 0)
    next_first = jnp.logical_or(scene_first[after_index] == 1, slab_index + 1 >= slab_count)
    keep_before = jnp.logical_not(own_first).astype(jnp.int32).reshape(1)
    keep_after = jnp.logical_not(next_first).astype(jnp.int32).reshape(1)

    q, kv = project_own(tok, gain_row, w_qkv)
    mix_up = window_mix(0, keep_before, before, q, kv, gain_row, w_qkv)
    mix_down = window_mix(1, keep_after, after, q, kv, gain_row, w_qkv)
    valid = window_valid.reshape(panels)
    out = cross_and_project(
        me, tile_table, panel_table, valid, tok, recv, q, mix_up, mix_down, gain_row, w_qkv, w_proj
    )
    return out.reshape(tokens.shape)


def solution(mesh):
    in_specs = (
        P(("scene", "tile"), None, None, None),
        P(),
        P(),
        P(),
        P(),
        P(("scene", "tile"), None),
        P("scene", None, None, None),
        P("scene", None, None),
    )
    out_specs = P(("scene", "tile"), None, None, None)
    return jax.shard_map(per_device, mesh=mesh, in_specs=in_specs, out_specs=out_specs, check_vma=False)
```

time: 427 us -> 406 us (0.951)
  the two profiles are of different devices: /device:TPU:24 before, /device:TPU:11 now
where the time goes in v1:
time: 406 us; the launch traced here: 405 us
  Pallas kernels  238 us (59%)
  starting transfers between devices  122 us (30%)
  waiting for transfers between devices  34.9 us (9%)
  local copies, waits for them, and re-layouts  8.28 us (2%)
    ppermute x7, starting transfers between devices, per_device(): lax.ppermute(outgoing[r - 1], 'tile', [(i, i ^ r) for i in range(tiles)])  115 us
    pallas_call x1, Pallas kernels, pack(): pl.pallas_call(functools.partial(pack_kernel, tiles, panels, cap), out_sh...  114 us
    pallas_call x2, Pallas kernels, window_mix(): pl.pallas_call(functools.partial(window_kernel, head_width), grid=(wide /...  53.5 us
    pallas_call x1, Pallas kernels, cross_and_project(): pl.pallas_call(functools.partial(cross_kernel, tiles, head_width, group),...  50.6 us
    ppermute x7, waiting for transfers between devices, per_device(): lax.ppermute(outgoing[r - 1], 'tile', [(i, i ^ r) for i in range(tiles)])  34.8 us
    pallas_call x1, Pallas kernels, project_own(): pl.pallas_call(qkv_kernel, grid=(halves * 2,), out_shape=[jax.ShapeDtypeS...  20.3 us
  transfers between devices with their start and end apart: 9, of which 3 were waited for; matrix products, arithmetic and copies ran while one was open for 1% of the time, Pallas kernels for 46%

profile of v1, /device:TPU:11, one launch (start us, length us, event | category | flops | bytes accessed | tf_op | source)
XLA Modules:
  0.0 405.3 jit_solution(8777475893070786267)
XLA Ops:
  0.0 4.2 %fusion = (bf16[1,8,128,1024]{3,2,1,0:T(8,128)(2,1)}, bf16[1,8,128,1024]{3,2,1,0:T(8,128)(2,1)S(1)}) fusion(bf16[1,16,128,1024]{3,2,1,0:T(8,128)(2,1)} %param.8), kind=kLoop, calls=%fused_computation | loop fusion | bytes 8388608 | tf_op jit(solution)/shard_map/slice | solution.py:320
  4.2 2.6 collective-permute-start.8
  6.8 3.9 collective-permute-start.7
  10.6 0.6 broadcast.3
  11.2 0.7 reduce.3
  11.9 0.6 reshape.40.tile_ref
  12.6 0.6 reshape.41.panel_ref
  13.2 113.7 %shard_map.82 = (bf16[4,8,16,1024]{3,2,1,0:T(8,128)(2,1)}, bf16[4,8,16,1024]{3,2,1,0:T(8,128)(2,1)}, bf16[4,8,16,1024]{3,2,1,0:T(8,128)(2,1)}, bf16[4,8,16,1024]...) custom-call(s32[1]{0:T(128)} %bitcast.me_ref, ...), custom_call_target="tpu_custom_call" | custom-call | bytes 16777216 | tf_op jit(solution)/shard_map/pallas_call | solution.py:70
  126.9 109.5 %collective-permute-start = (bf16[4,8,16,1024]{3,2,1,0:T(8,128)(2,1)}, bf16[4,8,16,1024]{3,2,1,0:T(8,128)(2,1)S(1)}, u32[]{:S(2)}, u32[]{:S(2)}) collective-permute-start(bf16[4,8,16,1024]{3,2,1,0:T(8,128)(2,1)} %get-tuple-element.14), channel_id=1, source_target_pairs={{0,1},{1,0},{2,3},{3,2},{4,5},{5,4},{6,7},{7,6},{8,9},{9,8},{10,11... | collective-permute-start | bytes 3145736 | tf_op jit(solution)/shard_map/ppermute | solution.py:327
  236.4 1.7 collective-permute-start.2
  238.1 0.7 fusion.1
  239.5 0.6 reshape.44.gain_ref.rest_10_
  240.7 20.3 %shard_map.83 = (bf16[2,8,8,16,1024]{4,3,2,1,0:T(8,128)(2,1)}, bf16[2,8,8,16,2048]{4,3,2,1,0:T(8,128)(2,1)}) custom-call(bf16[2,8,8,16,1024]{4,3,2,1,0:T(8,128)(2,1)} %bitcast.12, bf16[1,1024]{1,0:T(2,128)(2,1)} %reshape.44.gain_ref.rest_10_, bf16[1024,3072]{1,0:T(8,128)(2,1)} %rest_11_.1), custom_call_target="tpu_custom_call" | custom-call | flops 12884901888 | bytes 23068672 | tf_op jit(solution)/shard_map/pallas_call | solution.py:94
  261.0 0.1 collective-permute-start.3
  261.1 0.3 collective-permute-done.1.rest_1_
  261.4 1.5 collective-permute-start.4
  262.9 0.7 collective-permute-start.5
  263.6 1.9 collective-permute-start.6
  265.5 26.8 %shard_map.85.rest_9_ = bf16[8,8,16,1024]{3,2,1,0:T(8,128)(2,1)} custom-call(s32[1]{0:T(128)} %bitcast.7.keep_ref, bf16[8,8,16,1024]{3,2,1,0:T(8,128)(2,1)} %collective-permute-done.8.edge_ref, bf16[2,8,8,16,1024]{4,3,2,1,0:T(8,128)(2,1)} %get-tuple-element.21.q_ref.rest_7_, bf16[2,8,8,16,2048]{4,3,2,1,0:T(8,128)(2,1)} %get-tuple-element.22.kvo_ref, ...), custom_call_target="tpu_custom_call" | custom-call | flops 6442450944 | bytes 16777216 | tf_op jit(solution)/shard_map/pallas_call | solution.py:160
  292.3 26.7 %shard_map.84.rest_8_ = bf16[8,8,16,1024]{3,2,1,0:T(8,128)(2,1)} custom-call(s32[1]{0:T(128)} %bitcast.4.keep_ref, bf16[8,8,16,1024]{3,2,1,0:T(8,128)(2,1)} %collective-permute-done.7.edge_ref, bf16[2,8,8,16,1024]{4,3,2,1,0:T(8,128)(2,1)} %get-tuple-element.21.q_ref.rest_7_, bf16[2,8,8,16,2048]{4,3,2,1,0:T(8,128)(2,1)} %get-tuple-element.22.kvo_ref, ...), custom_call_target="tpu_custom_call" | custom-call | flops 6442450944 | bytes 16777216 | tf_op jit(solution)/shard_map/pallas_call | solution.py:160
  319.0 11.8 %collective-permute-done.3.rest_3_ = bf16[4,8,16,1024]{3,2,1,0:T(8,128)(2,1)} collective-permute-done((bf16[4,8,16,1024]{3,2,1,0:T(8,128)(2,1)S(1)}, bf16[4,8,16,1024]{3,2,1,0:T(8,128)(2,1)}, u32[]{:S(2)}, u32[]{:S(2)}) %collective-permute-start.3) | collective-permute-done | bytes 1048608 | tf_op jit(solution)/shard_map/ppermute | solution.py:327
  330.8 22.8 %collective-permute-done.4.rest_4_ = bf16[4,8,16,1024]{3,2,1,0:T(8,128)(2,1)} collective-permute-done((bf16[4,8,16,1024]{3,2,1,0:T(8,128)(2,1)S(1)}, bf16[4,8,16,1024]{3,2,1,0:T(8,128)(2,1)}, u32[]{:S(2)}, u32[]{:S(2)}) %collective-permute-start.4) | collective-permute-done | bytes 1048608 | tf_op jit(solution)/shard_map/ppermute | solution.py:327
  353.5 1.0 copy-done.9
  354.5 50.6 %shard_map.86 = bf16[2,8,8,16,1024]{4,3,2,1,0:T(8,128)(2,1)} custom-call(s32[1]{0:T(128)} %bitcast.me_ref, s32[128]{0:T(128)} %reshape.40.tile_ref, s32[128]{0:T(128)} %reshape.41.panel_ref, s32[16]{0:T(128)} %bitcast.15, bf16[2,8,8,16,1024]{4,3,2,1,0:T(8,128)(2,1)} %bitcast.13, bf16[4,8,16,1024]{3,2,1,0:T(8,128)(2,1)} %copy-done.4, ...), custom_call_target="tpu_custom_call" | custom-call | flops 15032385536 | bytes 25165824 | tf_op jit(solution)/shard_map/pallas_call | solution.py:276
  (26 shorter events, 0.1 us)
Async XLA Ops:
  0.0 11.2 %copy-start.1 = (s32[1,8,16,1]{2,3,1,0:T(1,128)S(1)}, s32[1,8,16,1]{2,3,1,0:T(1,128)}, u32[]{:S(2)}) copy-start(s32[1,8,16,1]{2,3,1,0:T(1,128)} %param.14) | copy-start | bytes 1540
  0.0 12.6 %copy-start = (s32[1,8,16]{2,1,0:T(8,128)S(1)}, s32[1,8,16]{2,1,0:T(8,128)}, u32[]{:S(2)}) copy-start(s32[1,8,16]{2,1,0:T(8,128)} %param.15) | copy-start | bytes 1540
  4.2 258.7 %collective-permute-start.8 = (bf16[8,8,16,1024]{3,2,1,0:T(8,128)(2,1)}, bf16[8,8,16,1024]{3,2,1,0:T(8,128)(2,1)}, u32[]{:S(2)}, u32[]{:S(2)}) collective-permute-start(bf16[8,8,16,1024]{3,2,1,0:T(8,128)(2,1)} %bitcast.8), channel_id=1, source_target_pairs={{1,0},{2,1},{3,2},{4,3},{5,4},{6,5},{7,6},{8,7},{9,8},{10,9},{11,1... | collective-permute-start | bytes 6291464 | tf_op jit(solution)/shard_map/ppermute | solution.py:320
  6.8 256.9 %collective-permute-start.7 = (bf16[8,8,16,1024]{3,2,1,0:T(8,128)(2,1)S(1)}, bf16[8,8,16,1024]{3,2,1,0:T(8,128)(2,1)}, u32[]{:S(2)}, u32[]{:S(2)}) collective-permute-start(bf16[8,8,16,1024]{3,2,1,0:T(8,128)(2,1)S(1)} %bitcast.14), channel_id=1, source_target_pairs={{0,1},{1,2},{2,3},{3,4},{4,5},{5,6},{6,7},{7,8},{8,9},{9,10},{10,1... | collective-permute-start | bytes 6291464 | tf_op jit(solution)/shard_map/ppermute | solution.py:319
  13.2 224.9 %copy-start.3 = (s32[32]{0:T(128)S(1)}, s32[32]{0:T(128)}, u32[]{:S(2)}) copy-start(s32[32]{0:T(128)} %param.12) | copy-start | bytes 388
  13.2 226.3 %copy-start.2 = (bf16[1024]{0:T(1024)(128)(2,1)S(1)}, bf16[1024]{0:T(1024)(128)(2,1)}, u32[]{:S(2)}) copy-start(bf16[1024]{0:T(1024)(128)(2,1)} %param.9) | copy-start | bytes 6148
  126.9 134.1 %collective-permute-start = (bf16[4,8,16,1024]{3,2,1,0:T(8,128)(2,1)}, bf16[4,8,16,1024]{3,2,1,0:T(8,128)(2,1)S(1)}, u32[]{:S(2)}, u32[]{:S(2)}) collective-permute-start(bf16[4,8,16,1024]{3,2,1,0:T(8,128)(2,1)} %get-tuple-element.14), channel_id=1, source_target_pairs={{0,1},{1,0},{2,3},{3,2},{4,5},{5,4},{6,7},{7,6},{8,9},{9,8},{10,11... | collective-permute-start | bytes 3145736 | tf_op jit(solution)/shard_map/ppermute | solution.py:327
  236.4 25.1 %collective-permute-start.1 = (bf16[4,8,16,1024]{3,2,1,0:T(8,128)(2,1)}, bf16[4,8,16,1024]{3,2,1,0:T(8,128)(2,1)}, u32[]{:S(2)}, u32[]{:S(2)}) collective-permute-start(bf16[4,8,16,1024]{3,2,1,0:T(8,128)(2,1)} %get-tuple-element.15), channel_id=1, source_target_pairs={{0,2},{1,3},{2,0},{3,1},{4,6},{5,7},{6,4},{7,5},{8,10},{9,11},{10,... | collective-permute-start | bytes 3145736 | tf_op jit(solution)/shard_map/ppermute | solution.py:327
  236.4 82.6 %collective-permute-start.2 = (bf16[4,8,16,1024]{3,2,1,0:T(8,128)(2,1)}, bf16[4,8,16,1024]{3,2,1,0:T(8,128)(2,1)}, u32[]{:S(2)}, u32[]{:S(2)}) collective-permute-start(bf16[4,8,16,1024]{3,2,1,0:T(8,128)(2,1)} %get-tuple-element.16), channel_id=1, source_target_pairs={{0,3},{1,2},{2,1},{3,0},{4,7},{5,6},{6,5},{7,4},{8,11},{9,10},{10,... | collective-permute-start | bytes 3145736 | tf_op jit(solution)/shard_map/ppermute | solution.py:327
  240.7 20.4 %copy-start.8 = (bf16[4,8,16,1024]{3,2,1,0:T(8,128)(2,1)S(1)}, bf16[4,8,16,1024]{3,2,1,0:T(8,128)(2,1)}, u32[]{:S(2)}) copy-start(bf16[4,8,16,1024]{3,2,1,0:T(8,128)(2,1)} %get-tuple-element.17) | copy-start | bytes 3145732
  240.7 20.8 %copy-start.7 = (bf16[4,8,16,1024]{3,2,1,0:T(8,128)(2,1)S(1)}, bf16[4,8,16,1024]{3,2,1,0:T(8,128)(2,1)}, u32[]{:S(2)}) copy-start(bf16[4,8,16,1024]{3,2,1,0:T(8,128)(2,1)} %get-tuple-element.18) | copy-start | bytes 3145732
  240.7 22.2 %copy-start.6 = (bf16[4,8,16,1024]{3,2,1,0:T(8,128)(2,1)S(1)}, bf16[4,8,16,1024]{3,2,1,0:T(8,128)(2,1)}, u32[]{:S(2)}) copy-start(bf16[4,8,16,1024]{3,2,1,0:T(8,128)(2,1)} %get-tuple-element.19) | copy-start | bytes 3145732
  240.7 22.9 %copy-start.5 = (bf16[4,8,16,1024]{3,2,1,0:T(8,128)(2,1)S(1)}, bf16[4,8,16,1024]{3,2,1,0:T(8,128)(2,1)}, u32[]{:S(2)}) copy-start(bf16[4,8,16,1024]{3,2,1,0:T(8,128)(2,1)} %get-tuple-element.20) | copy-start | bytes 3145732
  261.0 31.3 %copy-start.4 = (bf16[4,8,16,1024]{3,2,1,0:T(8,128)(2,1)}, bf16[4,8,16,1024]{3,2,1,0:T(8,128)(2,1)S(1)}, u32[]{:S(2)}) copy-start(bf16[4,8,16,1024]{3,2,1,0:T(8,128)(2,1)S(1)} %collective-permute-done.rest_0_) | copy-start | bytes 3145732
  261.0 69.7 %collective-permute-start.3 = (bf16[4,8,16,1024]{3,2,1,0:T(8,128)(2,1)S(1)}, bf16[4,8,16,1024]{3,2,1,0:T(8,128)(2,1)}, u32[]{:S(2)}, u32[]{:S(2)}) collective-permute-start(bf16[4,8,16,1024]{3,2,1,0:T(8,128)(2,1)S(1)} %copy-done.8), channel_id=1, source_target_pairs={{0,4},{1,5},{2,6},{3,7},{4,0},{5,1},{6,2},{7,3},{8,12},{9,13},{10,... | collective-permute-start | bytes 3145736 | tf_op jit(solution)/shard_map/ppermute | solution.py:327
  261.4 92.1 %collective-permute-start.4 = (bf16[4,8,16,1024]{3,2,1,0:T(8,128)(2,1)S(1)}, bf16[4,8,16,1024]{3,2,1,0:T(8,128)(2,1)}, u32[]{:S(2)}, u32[]{:S(2)}) collective-permute-start(bf16[4,8,16,1024]{3,2,1,0:T(8,128)(2,1)S(1)} %copy-done.7), channel_id=1, source_target_pairs={{0,5},{1,4},{2,7},{3,6},{4,1},{5,0},{6,3},{7,2},{8,13},{9,12},{10,... | collective-permute-start | bytes 3145736 | tf_op jit(solution)/shard_map/ppermute | solution.py:327
  262.9 90.6 %collective-permute-start.5 = (bf16[4,8,16,1024]{3,2,1,0:T(8,128)(2,1)S(1)}, bf16[4,8,16,1024]{3,2,1,0:T(8,128)(2,1)}, u32[]{:S(2)}, u32[]{:S(2)}) collective-permute-start(bf16[4,8,16,1024]{3,2,1,0:T(8,128)(2,1)S(1)} %copy-done.6), channel_id=1, source_target_pairs={{0,6},{1,7},{2,4},{3,5},{4,2},{5,3},{6,0},{7,1},{8,14},{9,15},{10,... | collective-permute-start | bytes 3145736 | tf_op jit(solution)/shard_map/ppermute | solution.py:327
  263.6 89.9 %collective-permute-start.6 = (bf16[4,8,16,1024]{3,2,1,0:T(8,128)(2,1)S(1)}, bf16[4,8,16,1024]{3,2,1,0:T(8,128)(2,1)S(1)}, u32[]{:S(2)}, u32[]{:S(2)}) collective-permute-start(bf16[4,8,16,1024]{3,2,1,0:T(8,128)(2,1)S(1)} %copy-done.5), channel_id=1, source_target_pairs={{0,7},{1,6},{2,5},{3,4},{4,3},{5,2},{6,1},{7,0},{8,15},{9,14},{10,... | collective-permute-start | bytes 3145736 | tf_op jit(solution)/shard_map/ppermute | solution.py:327
  353.5 1.0 copy-start.9

commit v2 on v1

--- a/solution.py
+++ b/solution.py
@@ -29,13 +29,24 @@
     return lax.dot_general(left, right, (((1,), (1,)), ((), ())), preferred_element_type=jnp.float32)
 
 
+def staged(count, first, second):
+    held = first(0)
+    for g in range(count):
+        coming = first(g + 1) if g + 1 < count else None
+        second(g, held)
+        held = coming
+
+
 def low_lanes(rows, width, head_width):
     return lax.broadcasted_iota(jnp.int32, (rows, width), 1) < head_width
 
 
 def pack_kernel(tiles, panels, cap, me_ref, tile_ref, panel_ref, tok_ref, *rest):
-    outs, sems = rest[: tiles - 1], rest[tiles - 1]
+    outs, slab, sem, sems = rest[: tiles - 1], rest[tiles - 1], rest[tiles], rest[tiles + 1]
     me = me_ref[0]
+    load = pltpu.make_async_copy(tok_ref, slab, sem)
+    load.start()
+    load.wait()
     counts = []
     for r in range(1, tiles):
         asker = me ^ r
@@ -48,7 +59,7 @@
             def _():
                 j = panel_ref[asker * panels + p]
                 pltpu.make_async_copy(
-                    tok_ref.at[j // (panels // 2), :, j % (panels // 2)], out.at[count], sems.at[r, count]
+                    slab.at[j // (panels // 2), :, j % (panels // 2)], out.at[count], sems.at[r, count]
                 ).start()
 
             return count + hit.astype(jnp.int32)
@@ -59,7 +70,7 @@
 
             @pl.when(c < counts[r - 1])
             def _(r=r, c=c):
-                pltpu.make_async_copy(tok_ref.at[0, :, 0], outs[r - 1].at[c], sems.at[r, c]).wait()
+                pltpu.make_async_copy(slab.at[0, :, 0], outs[r - 1].at[c], sems.at[r, c]).wait()
 
 
 def pack(me, tile_table, panel_table, tok, tiles, cap):
@@ -72,7 +83,11 @@
         out_shape=[jax.ShapeDtypeStruct(block, tok.dtype)] * (tiles - 1),
         in_specs=[smem, smem, smem, anym],
         out_specs=[anym] * (tiles - 1),
-        scratch_shapes=[pltpu.SemaphoreType.DMA((tiles, cap))],
+        scratch_shapes=[
+            pltpu.VMEM(tok.shape, tok.dtype),
+            pltpu.SemaphoreType.DMA,
+            pltpu.SemaphoreType.DMA((tiles, cap)),
+        ],
         cost_estimate=pl.CostEstimate(flops=0, bytes_accessed=16 << 20, transcendentals=0),
     )(me, tile_table, panel_table, tok)
 
@@ -125,29 +140,32 @@
     low = low_lanes(length, pair, head_width)
     ones = jnp.ones((2 * length, pair), jnp.bfloat16)
     zero = jnp.zeros((length, pair), jnp.bfloat16)
-    for i in range(group):
-
-        def body(g, carry, i=i):
-            at = pl.ds(pl.multiple_of(g * pair, pair), pair)
-            at_v = pl.ds(pl.multiple_of(feat + g * pair, pair), pair)
+    def panel(i, carry):
+        def score(g):
+            at = slice(g * pair, (g + 1) * pair)
             q = q_ref[0, :, i, :, at].reshape(length, pair)
             qs = jnp.concatenate([jnp.where(low, q, zero), jnp.where(low, zero, q)], axis=0)
             keys = jnp.concatenate(
                 [kv_s[:, i, :, at].reshape(length, pair), kvo_ref[0, :, i, :, at].reshape(length, pair)], axis=0
             )
+            return dot_t(qs, keys) + bias
+
+        def mix(g, scores):
+            at_v = slice(feat + g * pair, feat + (g + 1) * pair)
             vals = jnp.concatenate(
                 [kv_s[:, i, :, at_v].reshape(length, pair), kvo_ref[0, :, i, :, at_v].reshape(length, pair)], axis=0
             )
-            scores = dot_t(qs, keys) + bias
             peak = jnp.max(scores, axis=1, keepdims=True)
             weights = jnp.exp2((scores - peak) * scale).astype(jnp.bfloat16)
             both = dot_f32(weights, jnp.concatenate([vals, ones], axis=1))
             mixed = both[:, :pair] / both[:, pair:]
             out = jnp.where(low, mixed[:length], mixed[length:])
-            mix_ref[:, i, :, at] = out.astype(jnp.bfloat16).reshape(deep, run, pair)
-            return carry
-
-        lax.fori_loop(0, feat // pair, body, 0, unroll=2)
+            mix_ref[:, i, :, g * pair : (g + 1) * pair] = out.astype(jnp.bfloat16).reshape(deep, run, pair)
+
+        staged(feat // pair, score, mix)
+        return carry
+
+    lax.fori_loop(0, group, panel, 0)
 
 
 def window_mix(half, keep, edge, q, kv_own, gain_row, w_qkv):
@@ -227,18 +245,21 @@
     one = jnp.ones((length, pair), jnp.bfloat16)
     marks = jnp.concatenate([jnp.where(low, one, zero), jnp.where(low, zero, one)], axis=0)
     upper = step < half // group
-    for i in range(group):
+    def panel(i, carry):
         gate = valid_ref[step * group + i].astype(jnp.float32)
-
-        def body(g, carry, i=i, gate=gate):
-            at = pl.ds(pl.multiple_of(g * pair, pair), pair)
-            at_v = pl.ds(pl.multiple_of(feat + g * pair, pair), pair)
+        rows_i = pl.ds(pl.multiple_of(i * length, length), length)
+
+        def score(g):
+            at = slice(g * pair, (g + 1) * pair)
             q = q_ref[0, :, i, :, at].reshape(length, pair)
-            key = kv_s[i * length : (i + 1) * length, at]
-            val = kv_s[i * length : (i + 1) * length, at_v]
+            key = kv_s[rows_i, at]
             keys = jnp.concatenate([jnp.where(low, key, zero), jnp.where(low, zero, key)], axis=0)
+            return dot_t(q, keys)
+
+        def mix(g, scores):
+            at = slice(g * pair, (g + 1) * pair)
+            val = kv_s[rows_i, feat + g * pair : feat + (g + 1) * pair]
             vals = jnp.concatenate([jnp.where(low, val, zero), jnp.where(low, zero, val)], axis=0)
-            scores = dot_t(q, keys)
             parts = []
             for h in range(2):
                 part = scores[:, h * length : (h + 1) * length]
@@ -250,10 +271,12 @@
                 upper, up_ref[:, i, :, at].reshape(length, pair), down_ref[:, i, :, at].reshape(length, pair)
             )
             blended = gate * own.astype(jnp.float32) + cross.astype(jnp.float32)
-            mixed_s[i * length : (i + 1) * length, at] = blended.astype(jnp.bfloat16)
-            return carry
-
-        lax.fori_loop(0, feat // pair, body, 0, unroll=2)
+            mixed_s[rows_i, at] = blended.astype(jnp.bfloat16)
+
+        staged(feat // pair, score, mix)
+        return carry
+
+    lax.fori_loop(0, group, panel, 0)
     result = dot_f32(mixed_s[...], wp_ref[...]).astype(jnp.bfloat16)
     for i in range(group):
         out_ref[0, :, i] = result[i * length : (i + 1) * length].reshape(deep, run, feat)

time: 406 us -> 184 us (0.45)
  Pallas kernels: 238 us -> 94.3 us
  starting transfers between devices: 122 us -> 12.3 us
  waiting for transfers between devices: 34.9 us -> 67.1 us
    ppermute x7, starting transfers between devices: 115 us -> 5.82 us  [per_device(): lax.ppermute(outgoing[r - 1], 'tile', [(i, i ^ r) for i in range(tiles)])]
    pallas_call x1, Pallas kernels: 114 us -> 4.51 us  [pack(): pl.pallas_call(functools.partial(pack_kernel, tiles, panels, cap), out_sh...]
    ppermute x7, waiting for transfers between devices: 34.8 us -> 67.1 us  [per_device(): lax.ppermute(outgoing[r - 1], 'tile', [(i, i ^ r) for i in range(tiles)])]
    pallas_call x2, Pallas kernels: 53.5 us -> 35.7 us  [window_mix(): pl.pallas_call(functools.partial(window_kernel, head_width), grid=(wide /...]
    pallas_call x1, Pallas kernels: 50.6 us -> 33.8 us  [cross_and_project(): pl.pallas_call(functools.partial(cross_kernel, tiles, head_width, group),...]
  transfers between devices with their start and end apart: 9 -> 9, of which waited for: 3 -> 2; matrix products, arithmetic and copies ran while one was open for 1% -> 2% of each run, Pallas kernels for 46% -> 33%
where the time goes in v2:
time: 184 us
  Pallas kernels  94.3 us (51%)
  waiting for transfers between devices  67.1 us (36%)
  starting transfers between devices  12.3 us (7%)
  local copies, waits for them, and re-layouts  8.28 us (4%)
    ppermute x7, waiting for transfers between devices, per_device(): lax.ppermute(outgoing[r - 1], 'tile', [(i, i ^ r) for i in range(tiles)])  67.1 us
    pallas_call x2, Pallas kernels, window_mix(): pl.pallas_call(functools.partial(window_kernel, head_width), grid=(wide /...  35.7 us
    pallas_call x1, Pallas kernels, cross_and_project(): pl.pallas_call(functools.partial(cross_kernel, tiles, head_width, group),...  33.8 us
    pallas_call x1, Pallas kernels, project_own(): pl.pallas_call(qkv_kernel, grid=(halves * 2,), out_shape=[jax.ShapeDtypeS...  20.3 us
    ppermute x7, starting transfers between devices, per_device(): lax.ppermute(outgoing[r - 1], 'tile', [(i, i ^ r) for i in range(tiles)])  5.82 us
    pallas_call x1, Pallas kernels, pack(): pl.pallas_call(functools.partial(pack_kernel, tiles, panels, cap), out_sh...  4.51 us
    slice x1, local copies, waits for them, and re-layouts, per_device(): after = lax.ppermute(tok[0], ('scene', 'tile'), backward)  4.17 us
    ppermute x1, starting transfers between devices, per_device(): before = lax.ppermute(tok[1], ('scene', 'tile'), forward)  3.88 us
  transfers between devices with their start and end apart: 9, of which 2 were waited for; matrix products, arithmetic and copies ran while one was open for 2% of the time, Pallas kernels for 33%

profile of v2, /device:TPU:11, one launch (start us, length us, event | category | flops | bytes accessed | tf_op | source)
XLA Modules:
  0.0 184.2 jit_solution(4305094420242511010)
XLA Ops:
  0.0 4.2 %fusion = (bf16[1,8,128,1024]{3,2,1,0:T(8,128)(2,1)}, bf16[1,8,128,1024]{3,2,1,0:T(8,128)(2,1)S(1)}) fusion(bf16[1,16,128,1024]{3,2,1,0:T(8,128)(2,1)} %param.8), kind=kLoop, calls=%fused_computation | loop fusion | bytes 8388608 | tf_op jit(solution)/shard_map/slice | solution.py:343
  4.2 2.6 %collective-permute-start.8 = (bf16[8,8,16,1024]{3,2,1,0:T(8,128)(2,1)}, bf16[8,8,16,1024]{3,2,1,0:T(8,128)(2,1)}, u32[]{:S(2)}, u32[]{:S(2)}) collective-permute-start(bf16[8,8,16,1024]{3,2,1,0:T(8,128)(2,1)} %bitcast.8), channel_id=1, source_target_pairs={{1,0},{2,1},{3,2},{4,3},{5,4},{6,5},{7,6},{8,7},{9,8},{10,9},{11,1... | collective-permute-start | bytes 6291464 | tf_op jit(solution)/shard_map/ppermute | solution.py:343
  6.8 3.9 %collective-permute-start.7 = (bf16[8,8,16,1024]{3,2,1,0:T(8,128)(2,1)S(1)}, bf16[8,8,16,1024]{3,2,1,0:T(8,128)(2,1)}, u32[]{:S(2)}, u32[]{:S(2)}) collective-permute-start(bf16[8,8,16,1024]{3,2,1,0:T(8,128)(2,1)S(1)} %bitcast.14), channel_id=1, source_target_pairs={{0,1},{1,2},{2,3},{3,4},{4,5},{5,6},{6,7},{7,8},{8,9},{9,10},{10,1... | collective-permute-start | bytes 6291464 | tf_op jit(solution)/shard_map/ppermute | solution.py:342
  10.6 0.6 broadcast.3
  11.2 0.7 reduce.3
  11.9 0.6 reshape.40.tile_ref
  12.6 0.6 reshape.41.panel_ref
  13.2 4.5 %shard_map.82 = (bf16[4,8,16,1024]{3,2,1,0:T(8,128)(2,1)}, bf16[4,8,16,1024]{3,2,1,0:T(8,128)(2,1)}, bf16[4,8,16,1024]{3,2,1,0:T(8,128)(2,1)}, bf16[4,8,16,1024]...) custom-call(s32[1]{0:T(128)} %bitcast.me_ref, ...), custom_call_target="tpu_custom_call" | custom-call | bytes 16777216 | tf_op jit(solution)/shard_map/pallas_call | solution.py:81
  17.7 0.1 collective-permute-start
  17.8 0.7 collective-permute-start.1
  18.5 1.4 collective-permute-start.2
  19.9 0.7 fusion.1
  21.3 0.6 reshape.44.gain_ref.rest_10_
  22.5 20.3 %shard_map.83 = (bf16[2,8,8,16,1024]{4,3,2,1,0:T(8,128)(2,1)}, bf16[2,8,8,16,2048]{4,3,2,1,0:T(8,128)(2,1)}) custom-call(bf16[2,8,8,16,1024]{4,3,2,1,0:T(8,128)(2,1)} %bitcast.12, bf16[1,1024]{1,0:T(2,128)(2,1)} %reshape.44.gain_ref.rest_10_, bf16[1024,3072]{1,0:T(8,128)(2,1)} %rest_11_.1), custom_call_target="tpu_custom_call" | custom-call | flops 12884901888 | bytes 23068672 | tf_op jit(solution)/shard_map/pallas_call | solution.py:109
  42.8 0.0 collective-permute-done.rest_0_
  42.9 2.8 %collective-permute-start.3 = (bf16[4,8,16,1024]{3,2,1,0:T(8,128)(2,1)S(1)}, bf16[4,8,16,1024]{3,2,1,0:T(8,128)(2,1)}, u32[]{:S(2)}, u32[]{:S(2)}) collective-permute-start(bf16[4,8,16,1024]{3,2,1,0:T(8,128)(2,1)S(1)} %copy-done.8), channel_id=1, source_target_pairs={{0,4},{1,5},{2,6},{3,7},{4,0},{5,1},{6,2},{7,3},{8,12},{9,13},{10,... | collective-permute-start | bytes 3145736 | tf_op jit(solution)/shard_map/ppermute | solution.py:350
  45.7 44.3 %collective-permute-done.1.rest_1_ = bf16[4,8,16,1024]{3,2,1,0:T(8,128)(2,1)} collective-permute-done((bf16[4,8,16,1024]{3,2,1,0:T(8,128)(2,1)}, bf16[4,8,16,1024]{3,2,1,0:T(8,128)(2,1)}, u32[]{:S(2)}, u32[]{:S(2)}) %collective-permute-start.1) | collective-permute-done | bytes 1048608 | tf_op jit(solution)/shard_map/ppermute | solution.py:350
  90.0 0.1 collective-permute-start.5
  90.1 0.7 collective-permute-start.6
  90.8 17.8 %shard_map.85.rest_9_ = bf16[8,8,16,1024]{3,2,1,0:T(8,128)(2,1)} custom-call(s32[1]{0:T(128)} %bitcast.7.keep_ref, bf16[8,8,16,1024]{3,2,1,0:T(8,128)(2,1)} %collective-permute-done.8.edge_ref, bf16[2,8,8,16,1024]{4,3,2,1,0:T(8,128)(2,1)} %get-tuple-element.21.q_ref.rest_7_, bf16[2,8,8,16,2048]{4,3,2,1,0:T(8,128)(2,1)} %get-tuple-element.22.kvo_ref, ...), custom_call_target="tpu_custom_call" | custom-call | flops 6442450944 | bytes 16777216 | tf_op jit(solution)/shard_map/pallas_call | solution.py:178
  108.7 17.8 %shard_map.84.rest_8_ = bf16[8,8,16,1024]{3,2,1,0:T(8,128)(2,1)} custom-call(s32[1]{0:T(128)} %bitcast.4.keep_ref, bf16[8,8,16,1024]{3,2,1,0:T(8,128)(2,1)} %collective-permute-done.7.edge_ref, bf16[2,8,8,16,1024]{4,3,2,1,0:T(8,128)(2,1)} %get-tuple-element.21.q_ref.rest_7_, bf16[2,8,8,16,2048]{4,3,2,1,0:T(8,128)(2,1)} %get-tuple-element.22.kvo_ref, ...), custom_call_target="tpu_custom_call" | custom-call | flops 6442450944 | bytes 16777216 | tf_op jit(solution)/shard_map/pallas_call | solution.py:178
  126.5 22.8 %collective-permute-done.4.rest_4_ = bf16[4,8,16,1024]{3,2,1,0:T(8,128)(2,1)} collective-permute-done((bf16[4,8,16,1024]{3,2,1,0:T(8,128)(2,1)S(1)}, bf16[4,8,16,1024]{3,2,1,0:T(8,128)(2,1)}, u32[]{:S(2)}, u32[]{:S(2)}) %collective-permute-start.4) | collective-permute-done | bytes 1048608 | tf_op jit(solution)/shard_map/ppermute | solution.py:350
  149.3 1.0 copy-done.9
  150.3 33.8 %shard_map.86 = bf16[2,8,8,16,1024]{4,3,2,1,0:T(8,128)(2,1)} custom-call(s32[1]{0:T(128)} %bitcast.me_ref, s32[128]{0:T(128)} %reshape.40.tile_ref, s32[128]{0:T(128)} %reshape.41.panel_ref, s32[16]{0:T(128)} %bitcast.15, bf16[2,8,8,16,1024]{4,3,2,1,0:T(8,128)(2,1)} %bitcast.13, bf16[4,8,16,1024]{3,2,1,0:T(8,128)(2,1)} %copy-done.4, ...), custom_call_target="tpu_custom_call" | custom-call | flops 15032385536 | bytes 25165824 | tf_op jit(solution)/shard_map/pallas_call | solution.py:299
  (26 shorter events, 0.1 us)
Async XLA Ops:
  0.0 11.2 %copy-start.1 = (s32[1,8,16,1]{2,3,1,0:T(1,128)S(1)}, s32[1,8,16,1]{2,3,1,0:T(1,128)}, u32[]{:S(2)}) copy-start(s32[1,8,16,1]{2,3,1,0:T(1,128)} %param.14) | copy-start | bytes 1540
  0.0 12.6 %copy-start = (s32[1,8,16]{2,1,0:T(8,128)S(1)}, s32[1,8,16]{2,1,0:T(8,128)}, u32[]{:S(2)}) copy-start(s32[1,8,16]{2,1,0:T(8,128)} %param.15) | copy-start | bytes 1540
  4.2 85.8 %collective-permute-start.8 = (bf16[8,8,16,1024]{3,2,1,0:T(8,128)(2,1)}, bf16[8,8,16,1024]{3,2,1,0:T(8,128)(2,1)}, u32[]{:S(2)}, u32[]{:S(2)}) collective-permute-start(bf16[8,8,16,1024]{3,2,1,0:T(8,128)(2,1)} %bitcast.8), channel_id=1, source_target_pairs={{1,0},{2,1},{3,2},{4,3},{5,4},{6,5},{7,6},{8,7},{9,8},{10,9},{11,1... | collective-permute-start | bytes 6291464 | tf_op jit(solution)/shard_map/ppermute | solution.py:343
  6.8 83.4 %collective-permute-start.7 = (bf16[8,8,16,1024]{3,2,1,0:T(8,128)(2,1)S(1)}, bf16[8,8,16,1024]{3,2,1,0:T(8,128)(2,1)}, u32[]{:S(2)}, u32[]{:S(2)}) collective-permute-start(bf16[8,8,16,1024]{3,2,1,0:T(8,128)(2,1)S(1)} %bitcast.14), channel_id=1, source_target_pairs={{0,1},{1,2},{2,3},{3,4},{4,5},{5,6},{6,7},{7,8},{8,9},{9,10},{10,1... | collective-permute-start | bytes 6291464 | tf_op jit(solution)/shard_map/ppermute | solution.py:342
  13.2 6.7 %copy-start.3 = (s32[32]{0:T(128)S(1)}, s32[32]{0:T(128)}, u32[]{:S(2)}) copy-start(s32[32]{0:T(128)} %param.12) | copy-start | bytes 388
  13.2 8.1 %copy-start.2 = (bf16[1024]{0:T(1024)(128)(2,1)S(1)}, bf16[1024]{0:T(1024)(128)(2,1)}, u32[]{:S(2)}) copy-start(bf16[1024]{0:T(1024)(128)(2,1)} %param.9) | copy-start | bytes 6148
  17.7 25.1 %collective-permute-start = (bf16[4,8,16,1024]{3,2,1,0:T(8,128)(2,1)}, bf16[4,8,16,1024]{3,2,1,0:T(8,128)(2,1)S(1)}, u32[]{:S(2)}, u32[]{:S(2)}) collective-permute-start(bf16[4,8,16,1024]{3,2,1,0:T(8,128)(2,1)} %get-tuple-element.14), channel_id=1, source_target_pairs={{0,1},{1,0},{2,3},{3,2},{4,5},{5,4},{6,7},{7,6},{8,9},{9,8},{10,11... | collective-permute-start | bytes 3145736 | tf_op jit(solution)/shard_map/ppermute | solution.py:350
  17.8 72.2 %collective-permute-start.1 = (bf16[4,8,16,1024]{3,2,1,0:T(8,128)(2,1)}, bf16[4,8,16,1024]{3,2,1,0:T(8,128)(2,1)}, u32[]{:S(2)}, u32[]{:S(2)}) collective-permute-start(bf16[4,8,16,1024]{3,2,1,0:T(8,128)(2,1)} %get-tuple-element.15), channel_id=1, source_target_pairs={{0,2},{1,3},{2,0},{3,1},{4,6},{5,7},{6,4},{7,5},{8,10},{9,11},{10,... | collective-permute-start | bytes 3145736 | tf_op jit(solution)/shard_map/ppermute | solution.py:350
  18.5 108.0 %collective-permute-start.2 = (bf16[4,8,16,1024]{3,2,1,0:T(8,128)(2,1)}, bf16[4,8,16,1024]{3,2,1,0:T(8,128)(2,1)}, u32[]{:S(2)}, u32[]{:S(2)}) collective-permute-start(bf16[4,8,16,1024]{3,2,1,0:T(8,128)(2,1)} %get-tuple-element.16), channel_id=1, source_target_pairs={{0,3},{1,2},{2,1},{3,0},{4,7},{5,6},{6,5},{7,4},{8,11},{9,10},{10,... | collective-permute-start | bytes 3145736 | tf_op jit(solution)/shard_map/ppermute | solution.py:350
  22.5 20.4 %copy-start.8 = (bf16[4,8,16,1024]{3,2,1,0:T(8,128)(2,1)S(1)}, bf16[4,8,16,1024]{3,2,1,0:T(8,128)(2,1)}, u32[]{:S(2)}) copy-start(bf16[4,8,16,1024]{3,2,1,0:T(8,128)(2,1)} %get-tuple-element.17) | copy-start | bytes 3145732
  22.5 67.5 %copy-start.7 = (bf16[4,8,16,1024]{3,2,1,0:T(8,128)(2,1)S(1)}, bf16[4,8,16,1024]{3,2,1,0:T(8,128)(2,1)}, u32[]{:S(2)}) copy-start(bf16[4,8,16,1024]{3,2,1,0:T(8,128)(2,1)} %get-tuple-element.18) | copy-start | bytes 3145732
  22.5 67.5 %copy-start.6 = (bf16[4,8,16,1024]{3,2,1,0:T(8,128)(2,1)S(1)}, bf16[4,8,16,1024]{3,2,1,0:T(8,128)(2,1)}, u32[]{:S(2)}) copy-start(bf16[4,8,16,1024]{3,2,1,0:T(8,128)(2,1)} %get-tuple-element.19) | copy-start | bytes 3145732
  22.5 67.6 %copy-start.5 = (bf16[4,8,16,1024]{3,2,1,0:T(8,128)(2,1)S(1)}, bf16[4,8,16,1024]{3,2,1,0:T(8,128)(2,1)}, u32[]{:S(2)}) copy-start(bf16[4,8,16,1024]{3,2,1,0:T(8,128)(2,1)} %get-tuple-element.20) | copy-start | bytes 3145732
  42.8 65.8 %copy-start.4 = (bf16[4,8,16,1024]{3,2,1,0:T(8,128)(2,1)}, bf16[4,8,16,1024]{3,2,1,0:T(8,128)(2,1)S(1)}, u32[]{:S(2)}) copy-start(bf16[4,8,16,1024]{3,2,1,0:T(8,128)(2,1)S(1)} %collective-permute-done.rest_0_) | copy-start | bytes 3145732
  42.9 83.7 %collective-permute-start.3 = (bf16[4,8,16,1024]{3,2,1,0:T(8,128)(2,1)S(1)}, bf16[4,8,16,1024]{3,2,1,0:T(8,128)(2,1)}, u32[]{:S(2)}, u32[]{:S(2)}) collective-permute-start(bf16[4,8,16,1024]{3,2,1,0:T(8,128)(2,1)S(1)} %copy-done.8), channel_id=1, source_target_pairs={{0,4},{1,5},{2,6},{3,7},{4,0},{5,1},{6,2},{7,3},{8,12},{9,13},{10,... | collective-permute-start | bytes 3145736 | tf_op jit(solution)/shard_map/ppermute | solution.py:350
  90.0 59.3 %collective-permute-start.4 = (bf16[4,8,16,1024]{3,2,1,0:T(8,128)(2,1)S(1)}, bf16[4,8,16,1024]{3,2,1,0:T(8,128)(2,1)}, u32[]{:S(2)}, u32[]{:S(2)}) collective-permute-start(bf16[4,8,16,1024]{3,2,1,0:T(8,128)(2,1)S(1)} %copy-done.7), channel_id=1, source_target_pairs={{0,5},{1,4},{2,7},{3,6},{4,1},{5,0},{6,3},{7,2},{8,13},{9,12},{10,... | collective-permute-start | bytes 3145736 | tf_op jit(solution)/shard_map/ppermute | solution.py:350
  90.0 59.3 %collective-permute-start.5 = (bf16[4,8,16,1024]{3,2,1,0:T(8,128)(2,1)S(1)}, bf16[4,8,16,1024]{3,2,1,0:T(8,128)(2,1)}, u32[]{:S(2)}, u32[]{:S(2)}) collective-permute-start(bf16[4,8,16,1024]{3,2,1,0:T(8,128)(2,1)S(1)} %copy-done.6), channel_id=1, source_target_pairs={{0,6},{1,7},{2,4},{3,5},{4,2},{5,3},{6,0},{7,1},{8,14},{9,15},{10,... | collective-permute-start | bytes 3145736 | tf_op jit(solution)/shard_map/ppermute | solution.py:350
  90.1 59.2 %collective-permute-start.6 = (bf16[4,8,16,1024]{3,2,1,0:T(8,128)(2,1)S(1)}, bf16[4,8,16,1024]{3,2,1,0:T(8,128)(2,1)S(1)}, u32[]{:S(2)}, u32[]{:S(2)}) collective-permute-start(bf16[4,8,16,1024]{3,2,1,0:T(8,128)(2,1)S(1)} %copy-done.5), channel_id=1, source_target_pairs={{0,7},{1,6},{2,5},{3,4},{4,3},{5,2},{6,1},{7,0},{8,15},{9,14},{10,... | collective-permute-start | bytes 3145736 | tf_op jit(solution)/shard_map/ppermute | solution.py:350
  149.3 1.0 copy-start.9

commit v3 on v2

--- a/solution.py
+++ b/solution.py
@@ -198,67 +198,97 @@
     )(keep, edge, q, kv_own, gain_row, w_qkv)
 
 
-def cross_kernel(tiles, head_width, group, me_ref, tile_ref, panel_ref, valid_ref, tok_ref, *rest):
-    recv = rest[: tiles - 1]
-    q_ref, up_ref, down_ref, gain_ref, w_ref, wp_ref, out_ref, got, kv_s, mixed_s, seen, sems = rest[tiles - 1 :]
+def cross_kernel(tiles, head_width, wanted, own_halves, refs):
+    me_ref, tile_ref, panel_ref, valid_ref, tok_ref = refs[:5]
+    recv = refs[5 : 4 + tiles]
+    q_ref, mix_a, mix_b, gain_ref, wqkv_ref, wproj_ref = refs[4 + tiles : 10 + tiles]
+    out_ref, got, q_s, own_s, res_s, wkv_s, wp_s, kv_s, mixed_s, seen, ids, w_sem, sems = refs[-13:]
     panels, deep, run, feat = got.shape
     half = panels // 2
     length = deep * run
-    step = pl.program_id(0)
     me = me_ref[0]
-
-    @pl.when(step == 0)
-    def _():
-        for t in range(tiles):
-            seen[t] = 0
-
-        def body(p, carry):
-            source = tile_ref[me * panels + p]
-            slot = seen[source]
-            seen[source] = slot + 1
+    for t in range(tiles):
+        seen[t] = 0
+
+    def fetch(p, count):
+        source = tile_ref[me * panels + p]
+        slot = seen[source]
+        seen[source] = slot + 1
+        r = source ^ me
+        hit = ((wanted >> r) & 1) == 1
+
+        @pl.when(hit)
+        def _():
+            ids[count] = p
             j = panel_ref[me * panels + p]
-            r = source ^ me
 
             @pl.when(r == 0)
             def _():
-                pltpu.make_async_copy(tok_ref.at[j // half, :, j % half], got.at[p], sems.at[p]).start()
+                pltpu.make_async_copy(tok_ref.at[j // half, :, j % half], got.at[count], sems.at[0, count]).start()
 
             for k in range(1, tiles):
-
-                @pl.when(r == k)
-                def _(k=k):
-                    pltpu.make_async_copy(recv[k - 1].at[slot], got.at[p], sems.at[p]).start()
-
-            return carry
-
-        lax.fori_loop(0, panels, body, 0)
-
-    for i in range(group):
-        pltpu.make_async_copy(tok_ref.at[0, :, 0], got.at[step * group + i], sems.at[step * group + i]).wait()
-    rows = got[pl.ds(step * group, group)].reshape(group * length, feat)
-    normed = layer_norm(rows, gain_ref[...])
-    kv_s[...] = dot_f32(normed, w_ref[:, feat:]).astype(jnp.bfloat16)
+                if (wanted >> k) & 1:
+
+                    @pl.when(r == k)
+                    def _(k=k):
+                        pltpu.make_async_copy(recv[k - 1].at[slot], got.at[count], sems.at[0, count]).start()
+
+            u = p // half
+            w = p % half
+            pltpu.make_async_copy(q_ref.at[u, :, w], q_s.at[count], sems.at[1, count]).start()
+
+            @pl.when(u == own_halves[0])
+            def _():
+                pltpu.make_async_copy(mix_a.at[:, w], own_s.at[count], sems.at[2, count]).start()
+
+            @pl.when(u == own_halves[1])
+            def _():
+                pltpu.make_async_copy(mix_b.at[:, w], own_s.at[count], sems.at[2, count]).start()
+
+        return count + hit.astype(jnp.int32)
+
+    load_wkv = pltpu.make_async_copy(wqkv_ref.at[:, feat:], wkv_s, w_sem.at[0])
+    load_wp = pltpu.make_async_copy(wproj_ref, wp_s, w_sem.at[1])
+    load_wkv.start()
+    total = lax.fori_loop(0, panels, fetch, jnp.int32(0))
+    load_wp.start()
+    load_wkv.wait()
+    load_wp.wait()
+
     pair = 2 * head_width
     scale = LOG2E * head_width ** (-0.5)
     low = low_lanes(length, pair, head_width)
     zero = jnp.zeros((length, pair), jnp.bfloat16)
     one = jnp.ones((length, pair), jnp.bfloat16)
     marks = jnp.concatenate([jnp.where(low, one, zero), jnp.where(low, zero, one)], axis=0)
-    upper = step < half // group
-    def panel(i, carry):
-        gate = valid_ref[step * group + i].astype(jnp.float32)
-        rows_i = pl.ds(pl.multiple_of(i * length, length), length)
-
-        def score(g):
+    pairs = feat // pair
+
+    def unit(n, carry):
+        first = 2 * n
+        for i in range(2):
+
+            @pl.when(first + i < total)
+            def _(i=i):
+                for k, place in enumerate((got, q_s, own_s)):
+                    pltpu.make_async_copy(tok_ref.at[0, :, 0], place.at[first + i], sems.at[k, first + i]).wait()
+
+        rows = got[pl.ds(first, 2)].reshape(2 * length, feat)
+        normed = layer_norm(rows, gain_ref[...])
+        kv_s[...] = dot_f32(normed, wkv_s[...]).astype(jnp.bfloat16)
+        gates = [valid_ref[ids[jnp.minimum(first + i, total - 1)]].astype(jnp.float32) for i in range(2)]
+
+        def score(t):
+            i, g = t // pairs, t % pairs
             at = slice(g * pair, (g + 1) * pair)
-            q = q_ref[0, :, i, :, at].reshape(length, pair)
-            key = kv_s[rows_i, at]
+            q = q_s[first + i, :, :, at].reshape(length, pair)
+            key = kv_s[i * length : (i + 1) * length, at]
             keys = jnp.concatenate([jnp.where(low, key, zero), jnp.where(low, zero, key)], axis=0)
             return dot_t(q, keys)
 
-        def mix(g, scores):
+        def mix(t, scores):
+            i, g = t // pairs, t % pairs
             at = slice(g * pair, (g + 1) * pair)
-            val = kv_s[rows_i, feat + g * pair : feat + (g + 1) * pair]
+            val = kv_s[i * length : (i + 1) * length, feat + g * pair : feat + (g + 1) * pair]
             vals = jnp.concatenate([jnp.where(low, val, zero), jnp.where(low, zero, val)], axis=0)
             parts = []
             for h in range(2):
@@ -267,64 +297,81 @@
                 parts.append(jnp.exp2((part - peak) * scale).astype(jnp.bfloat16))
             both = dot_f32(jnp.concatenate(parts, axis=1), jnp.concatenate([vals, marks], axis=1))
             cross = (both[:, :pair] / both[:, pair:]).astype(jnp.bfloat16)
-            own = jnp.where(
-                upper, up_ref[:, i, :, at].reshape(length, pair), down_ref[:, i, :, at].reshape(length, pair)
-            )
-            blended = gate * own.astype(jnp.float32) + cross.astype(jnp.float32)
-            mixed_s[rows_i, at] = blended.astype(jnp.bfloat16)
-
-        staged(feat // pair, score, mix)
+            own = own_s[first + i, :, :, at].reshape(length, pair)
+            blended = gates[i] * own.astype(jnp.float32) + cross.astype(jnp.float32)
+            mixed_s[i * length : (i + 1) * length, at] = blended.astype(jnp.bfloat16)
+
+        staged(2 * pairs, score, mix)
+        res_s[pl.ds(first, 2)] = dot_f32(mixed_s[...], wp_s[...]).astype(jnp.bfloat16).reshape(2, deep, run, feat)
+        for i in range(2):
+
+            @pl.when(first + i < total)
+            def _(i=i):
+                p = ids[first + i]
+                pltpu.make_async_copy(
+                    res_s.at[first + i], out_ref.at[p // half, :, p % half], sems.at[3, first + i]
+                ).start()
+
         return carry
 
-    lax.fori_loop(0, group, panel, 0)
-    result = dot_f32(mixed_s[...], wp_ref[...]).astype(jnp.bfloat16)
-    for i in range(group):
-        out_ref[0, :, i] = result[i * length : (i + 1) * length].reshape(deep, run, feat)
-
-
-def cross_and_project(me, tile_table, panel_table, valid, tok, recv, q, mix_up, mix_down, gain_row, w_qkv, w_proj):
+    lax.fori_loop(0, (total + 1) // 2, unit, 0)
+
+    def finish(n, carry):
+        pltpu.make_async_copy(res_s.at[n], out_ref.at[0, :, 0], sems.at[3, n]).wait()
+        return carry
+
+    lax.fori_loop(0, total, finish, 0)
+
+
+def cross_and_project(wanted, me, tile_table, panel_table, valid, tok, recv, q, mixes, gain_row, w_qkv, w_proj, earlier):
     halves, deep, wide, run, feat = tok.shape
     panels = halves * wide
     tiles = len(recv) + 1
-    group = min(GROUP, wide)
-    per_half = wide // group
     head_width = feat // HEADS
     length = deep * run
     smem = pl.BlockSpec(memory_space=pltpu.SMEM)
     anym = pl.BlockSpec(memory_space=pl.ANY)
-    whole = pl.BlockSpec((1, deep, group, run, feat), lambda i: (i // per_half, 0, i % per_half, 0, 0))
-    up = pl.BlockSpec((deep, group, run, feat), lambda i: (0, jnp.minimum(i, per_half - 1), 0, 0))
-    down = pl.BlockSpec((deep, group, run, feat), lambda i: (0, jnp.maximum(i - per_half, 0), 0, 0))
-    tokens = panels * length
+    share = bin(wanted).count("1") / tiles
+    tokens = int(panels * length * share)
+    many = pltpu.VMEM((panels, deep, run, feat), jnp.bfloat16)
+    operands = [me, tile_table, panel_table, valid, tok, *recv, q, *mixes, gain_row, w_qkv, w_proj]
+    specs = [smem] * 4 + [anym] * (tiles + 3) + [pl.BlockSpec((1, feat), lambda: (0, 0))] + [anym] * 2
+    aliases = {}
+    if earlier is not None:
+        aliases = {len(operands): 0}
+        operands.append(earlier)
+        specs.append(anym)
+
+    def kernel(*refs):
+        cross_kernel(tiles, head_width, wanted, (0, 1), refs)
+
     return pl.pallas_call(
-        functools.partial(cross_kernel, tiles, head_width, group),
-        grid=(panels // group,),
+        kernel,
         out_shape=jax.ShapeDtypeStruct(tok.shape, jnp.bfloat16),
-        in_specs=[smem, smem, smem, smem, anym]
-        + [anym] * (tiles - 1)
-        + [
-            whole,
-            up,
-            down,
-            pl.BlockSpec((1, feat), lambda i: (0, 0)),
-            pl.BlockSpec((feat, 3 * feat), lambda i: (0, 0), pipeline_mode=pl.Buffered(1)),
-            pl.BlockSpec((feat, feat), lambda i: (0, 0), pipeline_mode=pl.Buffered(1)),
+        in_specs=specs,
+        out_specs=anym,
+        scratch_shapes=[
+            many,
+            many,
+            many,
+            many,
+            pltpu.VMEM((feat, 2 * feat), jnp.bfloat16),
+            pltpu.VMEM((feat, feat), jnp.bfloat16),
+            pltpu.VMEM((2 * length, 2 * feat), jnp.bfloat16),
+            pltpu.VMEM((2 * length, feat), jnp.bfloat16),
+            pltpu.SMEM((tiles,), jnp.int32),
+            pltpu.SMEM((panels,), jnp.int32),
+            pltpu.SemaphoreType.DMA((2,)),
+            pltpu.SemaphoreType.DMA((4, panels)),
         ],
-        out_specs=whole,
-        scratch_shapes=[
-            pltpu.VMEM((panels, deep, run, feat), jnp.bfloat16),
-            pltpu.VMEM((group * length, 2 * feat), jnp.bfloat16),
-            pltpu.VMEM((group * length, feat), jnp.bfloat16),
-            pltpu.SMEM((tiles,), jnp.int32),
-            pltpu.SemaphoreType.DMA((panels,)),
-        ],
+        input_output_aliases=aliases,
         compiler_params=pltpu.CompilerParams(vmem_limit_bytes=VMEM_LIMIT),
         cost_estimate=pl.CostEstimate(
             flops=2 * tokens * feat * 3 * feat + 8 * tokens * 128 * feat,
-            bytes_accessed=tokens * feat * 8 + feat * feat * 8,
+            bytes_accessed=tokens * feat * 8 + feat * feat * 6,
             transcendentals=tokens * 128 * HEADS,
         ),
-    )(me, tile_table, panel_table, valid, tok, *recv, q, mix_up, mix_down, gain_row, w_qkv, w_proj)
+    )(*operands)
 
 
 def per_device(tokens, gain, w_qkv, w_proj, scene_first, window_valid, partner_tile, partner_panel):
@@ -361,9 +408,13 @@
     mix_up = window_mix(0, keep_before, before, q, kv, gain_row, w_qkv)
     mix_down = window_mix(1, keep_after, after, q, kv, gain_row, w_qkv)
     valid = window_valid.reshape(panels)
-    out = cross_and_project(
-        me, tile_table, panel_table, valid, tok, recv, q, mix_up, mix_down, gain_row, w_qkv, w_proj
-    )
+    out = None
+    late = (1 << tiles) - (1 << (tiles - tiles // 4))
+    for wanted in ((1 << tiles) - 1 - late, late):
+        parts = [block if (wanted >> r) & 1 else tok for r, block in enumerate(recv, 1)]
+        out = cross_and_project(
+            wanted, me, tile_table, panel_table, valid, tok, parts, q, (mix_up, mix_down), gain_row, w_qkv, w_proj, out
+        )
     return out.reshape(tokens.shape)
 
 

time: 184 us -> 173 us (0.940)
  the two profiles are of different devices: /device:TPU:11 before, /device:TPU:16 now
where the time goes in v3:
time: 173 us; the launch traced here: 172 us
  Pallas kernels  99.8 us (58%)
  starting transfers between devices  45.4 us (26%)
  waiting for transfers between devices  15.5 us (9%)
  local copies, waits for them, and re-layouts  9.24 us (5%)
    ppermute x7, starting transfers between devices, per_device(): lax.ppermute(outgoing[r - 1], 'tile', [(i, i ^ r) for i in range(tiles)])  39.8 us
    pallas_call x2, Pallas kernels, cross_and_project(): pl.pallas_call(kernel, out_shape=jax.ShapeDtypeStruct(tok.shape, jnp.bflo...  37.5 us
    pallas_call x2, Pallas kernels, window_mix(): pl.pallas_call(functools.partial(window_kernel, head_width), grid=(wide /...  35.8 us
    pallas_call x1, Pallas kernels, project_own(): pl.pallas_call(qkv_kernel, grid=(halves * 2,), out_shape=[jax.ShapeDtypeS...  20.3 us
    ppermute x7, waiting for transfers between devices, per_device(): lax.ppermute(outgoing[r - 1], 'tile', [(i, i ^ r) for i in range(tiles)])  15.5 us
    pallas_call x1, Pallas kernels, pack(): pl.pallas_call(functools.partial(pack_kernel, tiles, panels, cap), out_sh...  6.24 us
    slice x1, local copies, waits for them, and re-layouts, per_device(): after = lax.ppermute(tok[0], ('scene', 'tile'), backward)  4.22 us
    ppermute x1, starting transfers between devices, per_device(): after = lax.ppermute(tok[0], ('scene', 'tile'), backward)  3.67 us
  transfers between devices with their start and end apart: 9, of which 1 were waited for; matrix products, arithmetic and copies ran while one was open for 2% of the time, Pallas kernels for 51%

profile of v3, /device:TPU:16, one launch (start us, length us, event | category | flops | bytes accessed | tf_op | source)
XLA Modules:
  0.0 172.2 jit_solution(17754670016150996422)
XLA Ops:
  0.0 4.2 %fusion = (bf16[1,8,128,1024]{3,2,1,0:T(8,128)(2,1)}, bf16[1,8,128,1024]{3,2,1,0:T(8,128)(2,1)S(1)}) fusion(bf16[1,16,128,1024]{3,2,1,0:T(8,128)(2,1)} %param.8), kind=kLoop, calls=%fused_computation | loop fusion | bytes 8388608 | tf_op jit(solution)/shard_map/slice | solution.py:390
  4.2 3.7 %collective-permute-start.3 = (bf16[8,8,16,1024]{3,2,1,0:T(8,128)(2,1)}, bf16[8,8,16,1024]{3,2,1,0:T(8,128)(2,1)}, u32[]{:S(2)}, u32[]{:S(2)}) collective-permute-start(bf16[8,8,16,1024]{3,2,1,0:T(8,128)(2,1)} %bitcast.8), channel_id=1, source_target_pairs={{1,0},{2,1},{3,2},{4,3},{5,4},{6,5},{7,6},{8,7},{9,8},{10,9},{11,1... | collective-permute-start | bytes 6291464 | tf_op jit(solution)/shard_map/ppermute | solution.py:390
  7.9 1.9 %collective-permute-start.2 = (bf16[8,8,16,1024]{3,2,1,0:T(8,128)(2,1)S(1)}, bf16[8,8,16,1024]{3,2,1,0:T(8,128)(2,1)}, u32[]{:S(2)}, u32[]{:S(2)}) collective-permute-start(bf16[8,8,16,1024]{3,2,1,0:T(8,128)(2,1)S(1)} %bitcast.22), channel_id=1, source_target_pairs={{0,1},{1,2},{2,3},{3,4},{4,5},{5,6},{6,7},{7,8},{8,9},{9,10},{10,1... | collective-permute-start | bytes 6291464 | tf_op jit(solution)/shard_map/ppermute | solution.py:389
  9.8 0.5 broadcast.3
  10.4 0.6 reduce.3
  10.9 0.6 reshape.40.tile_ref.refs_1_
  11.5 0.6 reshape.41.panel_ref.refs_2_
  12.2 6.2 %shard_map.82 = (bf16[4,8,16,1024]{3,2,1,0:T(8,128)(2,1)}, bf16[4,8,16,1024]{3,2,1,0:T(8,128)(2,1)}, bf16[4,8,16,1024]{3,2,1,0:T(8,128)(2,1)}, bf16[4,8,16,1024]...) custom-call(s32[1]{0:T(128)} %bitcast.me_ref.refs_0_, ...), custom_call_target="tpu_custom_call" | custom-call | bytes 16777216 | tf_op jit(solution)/shard_map/pallas_call | solution.py:81
  18.4 0.1 collective-permute-start.4
  18.5 1.1 collective-permute-start.5
  19.6 0.8 collective-permute-start.6
  20.4 0.6 fusion.1
  21.7 0.6 reshape.44.gain_ref.refs_15_
  22.9 20.3 %shard_map.83 = (bf16[2,8,8,16,1024]{4,3,2,1,0:T(8,128)(2,1)}, bf16[2,8,8,16,2048]{4,3,2,1,0:T(8,128)(2,1)}) custom-call(bf16[2,8,8,16,1024]{4,3,2,1,0:T(8,128)(2,1)} %bitcast.12, bf16[1,1024]{1,0:T(2,128)(2,1)} %reshape.44.gain_ref.refs_15_, bf16[1024,3072]{1,0:T(8,128)(2,1)} %refs_16_.3), custom_call_target="tpu_custom_call" | custom-call | flops 12884901888 | bytes 23068672 | tf_op jit(solution)/shard_map/pallas_call | solution.py:109
  43.2 9.8 %collective-permute-start.7 = (bf16[4,8,16,1024]{3,2,1,0:T(8,128)(2,1)}, bf16[4,8,16,1024]{3,2,1,0:T(8,128)(2,1)}, u32[]{:S(2)}, u32[]{:S(2)}) collective-permute-start(bf16[4,8,16,1024]{3,2,1,0:T(8,128)(2,1)} %get-tuple-element.21), channel_id=1, source_target_pairs={{0,4},{1,5},{2,6},{3,7},{4,0},{5,1},{6,2},{7,3},{8,12},{9,13},{10,... | collective-permute-start | bytes 3145736 | tf_op jit(solution)/shard_map/ppermute | solution.py:397
  53.0 20.7 %collective-permute-start.8 = (bf16[4,8,16,1024]{3,2,1,0:T(8,128)(2,1)S(1)}, bf16[4,8,16,1024]{3,2,1,0:T(8,128)(2,1)S(1)}, u32[]{:S(2)}, u32[]{:S(2)}) collective-permute-start(bf16[4,8,16,1024]{3,2,1,0:T(8,128)(2,1)S(1)} %copy-done.8), channel_id=1, source_target_pairs={{0,5},{1,4},{2,7},{3,6},{4,1},{5,0},{6,3},{7,2},{8,13},{9,12},{10,... | collective-permute-start | bytes 3145736 | tf_op jit(solution)/shard_map/ppermute | solution.py:397
  73.8 17.8 %shard_map.85.refs_14_ = bf16[8,8,16,1024]{3,2,1,0:T(8,128)(2,1)} custom-call(s32[1]{0:T(128)} %bitcast.7.keep_ref, bf16[8,8,16,1024]{3,2,1,0:T(8,128)(2,1)} %collective-permute-done.3.edge_ref, bf16[2,8,8,16,1024]{4,3,2,1,0:T(8,128)(2,1)} %get-tuple-element.16.q_ref.refs_12_, bf16[2,8,8,16,2048]{4,3,2,1,0:T(8,128)(2,1)} %get-tuple-element.17.kvo_ref, ...), custom_call_target="tpu_custom_call" | custom-call | flops 6442450944 | bytes 16777216 | tf_op jit(solution)/shard_map/pallas_call | solution.py:178
  91.6 18.0 %shard_map.84.refs_13_ = bf16[8,8,16,1024]{3,2,1,0:T(8,128)(2,1)} custom-call(s32[1]{0:T(128)} %bitcast.4.keep_ref, bf16[8,8,16,1024]{3,2,1,0:T(8,128)(2,1)} %collective-permute-done.2.edge_ref, bf16[2,8,8,16,1024]{4,3,2,1,0:T(8,128)(2,1)} %get-tuple-element.16.q_ref.refs_12_, bf16[2,8,8,16,2048]{4,3,2,1,0:T(8,128)(2,1)} %get-tuple-element.17.kvo_ref, ...), custom_call_target="tpu_custom_call" | custom-call | flops 6442450944 | bytes 16777216 | tf_op jit(solution)/shard_map/pallas_call | solution.py:178
  109.7 7.3 %collective-permute-start.1 = (bf16[4,8,16,1024]{3,2,1,0:T(8,128)(2,1)S(1)}, bf16[4,8,16,1024]{3,2,1,0:T(8,128)(2,1)S(1)}, u32[]{:S(2)}, u32[]{:S(2)}) collective-permute-start(bf16[4,8,16,1024]{3,2,1,0:T(8,128)(2,1)S(1)} %copy-done.6), channel_id=1, source_target_pairs={{0,7},{1,6},{2,5},{3,4},{4,3},{5,2},{6,1},{7,0},{8,15},{9,14},{10,... | collective-permute-start | bytes 3145736 | tf_op jit(solution)/shard_map/ppermute | solution.py:397
  117.0 1.0 copy-done.9
  118.0 25.5 %shard_map.86.refs_18_ = bf16[2,8,8,16,1024]{4,3,2,1,0:T(8,128)(2,1)} custom-call(s32[1]{0:T(128)} %bitcast.me_ref.refs_0_, s32[128]{0:T(128)} %reshape.40.tile_ref.refs_1_, s32[128]{0:T(128)} %reshape.41.panel_ref.refs_2_, s32[16]{0:T(128)} %bitcast.23, bf16[2,8,8,16,1024]{4,3,2,1,0:T(8,128)(2,1)} %bitcast.13, ...), custom_call_target="tpu_custom_call" | custom-call | flops 11274289152 | bytes 18874368 | tf_op jit(solution)/shard_map/pallas_call | solution.py:348
  143.6 15.5 %collective-permute-done.1.refs_11_ = bf16[4,8,16,1024]{3,2,1,0:T(8,128)(2,1)S(1)} collective-permute-done((bf16[4,8,16,1024]{3,2,1,0:T(8,128)(2,1)S(1)}, bf16[4,8,16,1024]{3,2,1,0:T(8,128)(2,1)S(1)}, u32[]{:S(2)}, u32[]{:S(2)}) %collective-permute-start.1) | collective-permute-done | bytes 1048608 | tf_op jit(solution)/shard_map/ppermute | solution.py:397
  159.0 1.0 copy-done.1
  160.0 12.0 %shard_map.87 = bf16[2,8,8,16,1024]{4,3,2,1,0:T(8,128)(2,1)} custom-call(s32[1]{0:T(128)} %bitcast.me_ref.refs_0_, s32[128]{0:T(128)} %reshape.40.tile_ref.refs_1_, s32[128]{0:T(128)} %reshape.41.panel_ref.refs_2_, s32[16]{0:T(128)} %bitcast.24, bf16[2,8,8,16,1024]{4,3,2,1,0:T(8,128)(2,1)} %bitcast.16, ...), custom_call_target="tpu_custom_call", output_to_operand_aliasing={{}: (18, {})} | custom-call | flops 3758096384 | bytes 10485760 | tf_op jit(solution)/shard_map/pallas_call | solution.py:348
  (27 shorter events, 0.1 us)
Async XLA Ops:
  0.0 10.4 %copy-start.3 = (s32[1,8,16,1]{2,3,1,0:T(1,128)S(1)}, s32[1,8,16,1]{2,3,1,0:T(1,128)}, u32[]{:S(2)}) copy-start(s32[1,8,16,1]{2,3,1,0:T(1,128)} %param.14) | copy-start | bytes 1540
  0.0 11.5 %copy-start.2 = (s32[1,8,16]{2,1,0:T(8,128)S(1)}, s32[1,8,16]{2,1,0:T(8,128)}, u32[]{:S(2)}) copy-start(s32[1,8,16]{2,1,0:T(8,128)} %param.15) | copy-start | bytes 1540
  4.2 39.0 %collective-permute-start.3 = (bf16[8,8,16,1024]{3,2,1,0:T(8,128)(2,1)}, bf16[8,8,16,1024]{3,2,1,0:T(8,128)(2,1)}, u32[]{:S(2)}, u32[]{:S(2)}) collective-permute-start(bf16[8,8,16,1024]{3,2,1,0:T(8,128)(2,1)} %bitcast.8), channel_id=1, source_target_pairs={{1,0},{2,1},{3,2},{4,3},{5,4},{6,5},{7,6},{8,7},{9,8},{10,9},{11,1... | collective-permute-start | bytes 6291464 | tf_op jit(solution)/shard_map/ppermute | solution.py:390
  7.9 45.1 %collective-permute-start.2 = (bf16[8,8,16,1024]{3,2,1,0:T(8,128)(2,1)S(1)}, bf16[8,8,16,1024]{3,2,1,0:T(8,128)(2,1)}, u32[]{:S(2)}, u32[]{:S(2)}) collective-permute-start(bf16[8,8,16,1024]{3,2,1,0:T(8,128)(2,1)S(1)} %bitcast.22), channel_id=1, source_target_pairs={{0,1},{1,2},{2,3},{3,4},{4,5},{5,6},{6,7},{7,8},{8,9},{9,10},{10,1... | collective-permute-start | bytes 6291464 | tf_op jit(solution)/shard_map/ppermute | solution.py:389
  12.2 8.2 %copy-start.5 = (s32[32]{0:T(128)S(1)}, s32[32]{0:T(128)}, u32[]{:S(2)}) copy-start(s32[32]{0:T(128)} %param.12) | copy-start | bytes 388
  12.2 9.5 %copy-start.4 = (bf16[1024]{0:T(1024)(128)(2,1)S(1)}, bf16[1024]{0:T(1024)(128)(2,1)}, u32[]{:S(2)}) copy-start(bf16[1024]{0:T(1024)(128)(2,1)} %param.9) | copy-start | bytes 6148
  18.4 91.1 %collective-permute-start.4 = (bf16[4,8,16,1024]{3,2,1,0:T(8,128)(2,1)}, bf16[4,8,16,1024]{3,2,1,0:T(8,128)(2,1)}, u32[]{:S(2)}, u32[]{:S(2)}) collective-permute-start(bf16[4,8,16,1024]{3,2,1,0:T(8,128)(2,1)} %get-tuple-element.18), channel_id=1, source_target_pairs={{0,1},{1,0},{2,3},{3,2},{4,5},{5,4},{6,7},{7,6},{8,9},{9,8},{10,11... | collective-permute-start | bytes 3145736 | tf_op jit(solution)/shard_map/ppermute | solution.py:397
  18.5 91.2 %collective-permute-start.5 = (bf16[4,8,16,1024]{3,2,1,0:T(8,128)(2,1)}, bf16[4,8,16,1024]{3,2,1,0:T(8,128)(2,1)}, u32[]{:S(2)}, u32[]{:S(2)}) collective-permute-start(bf16[4,8,16,1024]{3,2,1,0:T(8,128)(2,1)} %get-tuple-element.19), channel_id=1, source_target_pairs={{0,2},{1,3},{2,0},{3,1},{4,6},{5,7},{6,4},{7,5},{8,10},{9,11},{10,... | collective-permute-start | bytes 3145736 | tf_op jit(solution)/shard_map/ppermute | solution.py:397
  19.6 97.4 %collective-permute-start.6 = (bf16[4,8,16,1024]{3,2,1,0:T(8,128)(2,1)}, bf16[4,8,16,1024]{3,2,1,0:T(8,128)(2,1)}, u32[]{:S(2)}, u32[]{:S(2)}) collective-permute-start(bf16[4,8,16,1024]{3,2,1,0:T(8,128)(2,1)} %get-tuple-element.20), channel_id=1, source_target_pairs={{0,3},{1,2},{2,1},{3,0},{4,7},{5,6},{6,5},{7,4},{8,11},{9,10},{10,... | collective-permute-start | bytes 3145736 | tf_op jit(solution)/shard_map/ppermute | solution.py:397
  22.9 30.1 %copy-start.8 = (bf16[4,8,16,1024]{3,2,1,0:T(8,128)(2,1)S(1)}, bf16[4,8,16,1024]{3,2,1,0:T(8,128)(2,1)}, u32[]{:S(2)}) copy-start(bf16[4,8,16,1024]{3,2,1,0:T(8,128)(2,1)} %get-tuple-element.22) | copy-start | bytes 3145732
  43.2 73.7 %collective-permute-start.7 = (bf16[4,8,16,1024]{3,2,1,0:T(8,128)(2,1)}, bf16[4,8,16,1024]{3,2,1,0:T(8,128)(2,1)}, u32[]{:S(2)}, u32[]{:S(2)}) collective-permute-start(bf16[4,8,16,1024]{3,2,1,0:T(8,128)(2,1)} %get-tuple-element.21), channel_id=1, source_target_pairs={{0,4},{1,5},{2,6},{3,7},{4,0},{5,1},{6,2},{7,3},{8,12},{9,13},{10,... | collective-permute-start | bytes 3145736 | tf_op jit(solution)/shard_map/ppermute | solution.py:397
  53.0 64.0 %collective-permute-start.8 = (bf16[4,8,16,1024]{3,2,1,0:T(8,128)(2,1)S(1)}, bf16[4,8,16,1024]{3,2,1,0:T(8,128)(2,1)S(1)}, u32[]{:S(2)}, u32[]{:S(2)}) collective-permute-start(bf16[4,8,16,1024]{3,2,1,0:T(8,128)(2,1)S(1)} %copy-done.8), channel_id=1, source_target_pairs={{0,5},{1,4},{2,7},{3,6},{4,1},{5,0},{6,3},{7,2},{8,13},{9,12},{10,... | collective-permute-start | bytes 3145736 | tf_op jit(solution)/shard_map/ppermute | solution.py:397
  91.6 18.0 %copy-start.7 = (bf16[4,8,16,1024]{3,2,1,0:T(8,128)(2,1)S(1)}, bf16[4,8,16,1024]{3,2,1,0:T(8,128)(2,1)}, u32[]{:S(2)}) copy-start(bf16[4,8,16,1024]{3,2,1,0:T(8,128)(2,1)} %get-tuple-element.14) | copy-start | bytes 3145732
  91.6 18.1 %copy-start.6 = (bf16[4,8,16,1024]{3,2,1,0:T(8,128)(2,1)S(1)}, bf16[4,8,16,1024]{3,2,1,0:T(8,128)(2,1)}, u32[]{:S(2)}) copy-start(bf16[4,8,16,1024]{3,2,1,0:T(8,128)(2,1)} %get-tuple-element.15) | copy-start | bytes 3145732
  109.6 34.0 %collective-permute-start = (bf16[4,8,16,1024]{3,2,1,0:T(8,128)(2,1)S(1)}, bf16[4,8,16,1024]{3,2,1,0:T(8,128)(2,1)S(1)}, u32[]{:S(2)}, u32[]{:S(2)}) collective-permute-start(bf16[4,8,16,1024]{3,2,1,0:T(8,128)(2,1)S(1)} %copy-done.7), channel_id=1, source_target_pairs={{0,6},{1,7},{2,4},{3,5},{4,2},{5,3},{6,0},{7,1},{8,14},{9,15},{10,... | collective-permute-start | bytes 3145736 | tf_op jit(solution)/shard_map/ppermute | solution.py:397
  109.7 49.4 %collective-permute-start.1 = (bf16[4,8,16,1024]{3,2,1,0:T(8,128)(2,1)S(1)}, bf16[4,8,16,1024]{3,2,1,0:T(8,128)(2,1)S(1)}, u32[]{:S(2)}, u32[]{:S(2)}) collective-permute-start(bf16[4,8,16,1024]{3,2,1,0:T(8,128)(2,1)S(1)} %copy-done.6), channel_id=1, source_target_pairs={{0,7},{1,6},{2,5},{3,4},{4,3},{5,2},{6,1},{7,0},{8,15},{9,14},{10,... | collective-permute-start | bytes 3145736 | tf_op jit(solution)/shard_map/ppermute | solution.py:397
  117.0 1.0 copy-start.9
  143.5 15.5 %copy-start = (bf16[4,8,16,1024]{3,2,1,0:T(8,128)(2,1)}, bf16[4,8,16,1024]{3,2,1,0:T(8,128)(2,1)S(1)}, u32[]{:S(2)}) copy-start(bf16[4,8,16,1024]{3,2,1,0:T(8,128)(2,1)S(1)} %collective-permute-done.refs_10_) | copy-start | bytes 3145732
  159.0 1.0 copy-start.1

commit v4 on v3

--- a/solution.py
+++ b/solution.py
@@ -90,6 +90,224 @@
         ],
         cost_estimate=pl.CostEstimate(flops=0, bytes_accessed=16 << 20, transcendentals=0),
     )(me, tile_table, panel_table, tok)
+
+
+def copy_through(pairs, bounce, sems):
+    loads = [pltpu.make_async_copy(src, bounce.at[k], sems.at[0, k]) for k, (src, _) in enumerate(pairs)]
+    for load in loads:
+        load.start()
+    stores = []
+    for k, (_, dst) in enumerate(pairs):
+        loads[k].wait()
+        store = pltpu.make_async_copy(bounce.at[k], dst, sems.at[1, k])
+        store.start()
+        stores.append(store)
+    for store in stores:
+        store.wait()
+
+
+def halves_kernel(tok_ref, first_ref, second_ref, bounce, sems):
+    deep = first_ref.shape[1]
+    pairs = []
+    for u in range(2):
+        pairs.append((tok_ref.at[u, :deep], first_ref.at[u]))
+        pairs.append((tok_ref.at[u, deep:], second_ref.at[u]))
+    copy_through(pairs, bounce, sems)
+
+
+def split_halves(tok):
+    halves, deep, wide, run, feat = tok.shape
+    part = (halves, deep // 2, wide, run, feat)
+    anym = pl.BlockSpec(memory_space=pl.ANY)
+    return pl.pallas_call(
+        halves_kernel,
+        out_shape=[jax.ShapeDtypeStruct(part, tok.dtype)] * 2,
+        in_specs=[anym],
+        out_specs=[anym] * 2,
+        scratch_shapes=[pltpu.VMEM((4,) + part[1:], tok.dtype), pltpu.SemaphoreType.DMA((2, 4))],
+        cost_estimate=pl.CostEstimate(flops=0, bytes_accessed=16 << 20, transcendentals=0),
+    )(tok)
+
+
+def near_kernel(cap, me_ref, tile_ref, panel_ref, tok_ref, out_ref, bounce, sems, slots, slot_sems):
+    halves, deep, wide, run, feat = tok_ref.shape
+    panels = halves * wide
+    me = me_ref[0]
+    asker = me ^ 1
+    part = 1 - (me & 1)
+
+    def body(p, count):
+        hit = jnp.logical_and(tile_ref[asker * panels + p] == me, count < cap)
+
+        @pl.when(hit)
+        def _():
+            j = panel_ref[asker * panels + p]
+            pltpu.make_async_copy(tok_ref.at[j // wide, :, j % wide], slots.at[count], slot_sems.at[0, count]).start()
+
+        return count + hit.astype(jnp.int32)
+
+    total = lax.fori_loop(0, panels, body, jnp.int32(0))
+    copy_through([(tok_ref.at[part, 2 * k : 2 * k + 2], out_ref.at[2 * k : 2 * k + 2]) for k in range(deep // 2)], bounce, sems)
+    for c in range(cap):
+
+        @pl.when(c < total)
+        def _(c=c):
+            pltpu.make_async_copy(tok_ref.at[0, :, 0], slots.at[c], slot_sems.at[0, c]).wait()
+            pltpu.make_async_copy(slots.at[c], out_ref.at[deep + c], slot_sems.at[1, c]).start()
+
+    for c in range(cap):
+
+        @pl.when(c < total)
+        def _(c=c):
+            pltpu.make_async_copy(slots.at[c], out_ref.at[deep + c], slot_sems.at[1, c]).wait()
+
+
+def pack_near(me, tile_table, panel_table, tok, cap):
+    halves, deep, wide, run, feat = tok.shape
+    smem = pl.BlockSpec(memory_space=pltpu.SMEM)
+    anym = pl.BlockSpec(memory_space=pl.ANY)
+    return pl.pallas_call(
+        functools.partial(near_kernel, cap),
+        out_shape=jax.ShapeDtypeStruct((deep + cap, wide, run, feat), tok.dtype),
+        in_specs=[smem, smem, smem, anym],
+        out_specs=anym,
+        scratch_shapes=[
+            pltpu.VMEM((deep // 2, 2, wide, run, feat), tok.dtype),
+            pltpu.SemaphoreType.DMA((2, deep // 2)),
+            pltpu.VMEM((cap, deep, run, feat), tok.dtype),
+            pltpu.SemaphoreType.DMA((2, cap)),
+        ],
+        cost_estimate=pl.CostEstimate(flops=0, bytes_accessed=6 << 20, transcendentals=0),
+    )(me, tile_table, panel_table, tok)
+
+
+def rim_kernel(me_ref, tok_ref, first_ref, second_ref, out_a, out_b, bounce, sems):
+    deep = out_a.shape[0]
+    me = me_ref[0]
+    part = me & 1
+    held = jnp.logical_or(me % 4 == 1, me % 4 == 2)
+    bite = deep // 2
+    spots = [pl.ds(k * bite, bite) for k in range(2)]
+    for k in range(2):
+        pltpu.make_async_copy(first_ref.at[part, spots[k]], bounce.at[k], sems.at[0, k]).start()
+
+        @pl.when(held)
+        def _(k=k):
+            pltpu.make_async_copy(
+                tok_ref.at[part, pl.ds(deep + k * bite, bite)], bounce.at[2 + k], sems.at[0, 2 + k]
+            ).start()
+
+        @pl.when(jnp.logical_not(held))
+        def _(k=k):
+            pltpu.make_async_copy(second_ref.at[part, spots[k]], bounce.at[2 + k], sems.at[0, 2 + k]).start()
+
+    stores = []
+    for k in range(4):
+        pltpu.make_async_copy(first_ref.at[0, spots[0]], bounce.at[k], sems.at[0, k]).wait()
+        store = pltpu.make_async_copy(bounce.at[k], (out_a if k < 2 else out_b).at[spots[k % 2]], sems.at[1, k])
+        store.start()
+        stores.append(store)
+    for store in stores:
+        store.wait()
+
+
+def pack_rim(me, tok, first, second):
+    halves, deep, wide, run, feat = first.shape
+    anym = pl.BlockSpec(memory_space=pl.ANY)
+    return pl.pallas_call(
+        rim_kernel,
+        out_shape=[jax.ShapeDtypeStruct(first.shape[1:], tok.dtype)] * 2,
+        in_specs=[pl.BlockSpec(memory_space=pltpu.SMEM), anym, anym, anym],
+        out_specs=[anym] * 2,
+        scratch_shapes=[pltpu.VMEM((4, deep // 2, wide, run, feat), tok.dtype), pltpu.SemaphoreType.DMA((2, 4))],
+        cost_estimate=pl.CostEstimate(flops=0, bytes_accessed=4 << 20, transcendentals=0),
+    )(me, tok, first, second)
+
+
+def far_kernel(cap, me_ref, tile_ref, panel_ref, tok_ref, first_ref, second_ref, *rest):
+    outs, slab, got_a, got_b, sem, sems = rest[:5], *rest[5:]
+    halves, deep, wide, run, feat = tok_ref.shape
+    panels = halves * wide
+    cut = deep // 2
+    me = me_ref[0]
+    loads = [
+        pltpu.make_async_copy(src, dst, sem.at[k])
+        for k, (src, dst) in enumerate(((tok_ref, slab), (first_ref, got_a), (second_ref, got_b)))
+    ]
+    for load in loads:
+        load.start()
+    for load in loads:
+        load.wait()
+    totals = []
+    for k, (bits, relay) in enumerate(((2, 4), (3, 4), (4, 2), (5, 2))):
+        asker = me ^ bits
+        buffer, rows = (got_b, slice(cut, deep)) if relay == 4 else (got_a, slice(0, cut))
+
+        def body(p, count, k=k, asker=asker, relay=relay, buffer=buffer, rows=rows):
+            named = tile_ref[asker * panels + p]
+            own = named == me
+            hit = jnp.logical_and(jnp.logical_or(own, named == me ^ relay), count < 2 * cap)
+            j = panel_ref[asker * panels + p]
+
+            @pl.when(jnp.logical_and(hit, own))
+            def _():
+                pltpu.make_async_copy(slab.at[j // wide, rows, j % wide], outs[k].at[count], sems.at[k, count]).start()
+
+            @pl.when(jnp.logical_and(hit, jnp.logical_not(own)))
+            def _():
+                pltpu.make_async_copy(buffer.at[j // wide, :, j % wide], outs[k].at[count], sems.at[k, count]).start()
+
+            return count + hit.astype(jnp.int32)
+
+        totals.append(lax.fori_loop(0, panels, body, jnp.int32(0)))
+
+    asker = me ^ 1
+
+    def near(p, counts):
+        named = tile_ref[asker * panels + p]
+        j = panel_ref[asker * panels + p]
+        fresh = []
+        for k, (relay, buffer) in enumerate(((2, got_a), (4, got_b))):
+            hit = jnp.logical_and(named == me ^ relay, counts[k] < cap)
+
+            @pl.when(hit)
+            def _(k=k, buffer=buffer):
+                spot = k * cap + counts[k]
+                pltpu.make_async_copy(buffer.at[j // wide, :, j % wide], outs[4].at[spot], sems.at[4, spot]).start()
+
+            fresh.append(counts[k] + hit.astype(jnp.int32))
+        return tuple(fresh)
+
+    near_totals = lax.fori_loop(0, panels, near, (jnp.int32(0), jnp.int32(0)))
+    for k in range(5):
+        for c in range(2 * cap):
+            used = c < totals[k] if k < 4 else c % cap < near_totals[c // cap]
+
+            @pl.when(used)
+            def _(k=k, c=c):
+                pltpu.make_async_copy(got_a.at[0, :, 0], outs[k].at[c], sems.at[k, c]).wait()
+
+
+def pack_far(me, tile_table, panel_table, tok, first, second, cap):
+    halves, deep, wide, run, feat = tok.shape
+    smem = pl.BlockSpec(memory_space=pltpu.SMEM)
+    anym = pl.BlockSpec(memory_space=pl.ANY)
+    block = (2 * cap, deep // 2, run, feat)
+    return pl.pallas_call(
+        functools.partial(far_kernel, cap),
+        out_shape=[jax.ShapeDtypeStruct(block, tok.dtype)] * 5,
+        in_specs=[smem, smem, smem, anym, anym, anym],
+        out_specs=[anym] * 5,
+        scratch_shapes=[
+            pltpu.VMEM(tok.shape, tok.dtype),
+            pltpu.VMEM(first.shape, tok.dtype),
+            pltpu.VMEM(second.shape, tok.dtype),
+            pltpu.SemaphoreType.DMA((3,)),
+            pltpu.SemaphoreType.DMA((5, 2 * cap)),
+        ],
+        compiler_params=pltpu.CompilerParams(vmem_limit_bytes=VMEM_LIMIT),
+        cost_estimate=pl.CostEstimate(flops=0, bytes_accessed=14 << 20, transcendentals=0),
+    )(me, tile_table, panel_table, tok, first, second)
 
 
 def qkv_kernel(tok_ref, gain_ref, w_ref, q_ref, kv_ref):
@@ -126,16 +344,16 @@
     )(tok, gain_row, w_qkv)
 
 
-def window_kernel(head_width, keep_ref, edge_ref, q_ref, kvo_ref, gain_ref, w_ref, mix_ref, kv_s):
-    deep, group, run, feat = edge_ref.shape
+def window_kernel(head_width, half_ref, top_ref, low_ref, q_ref, kvo_ref, gain_ref, w_ref, mix_ref, kv_s):
+    deep, group, run, feat = mix_ref.shape
     length = deep * run
-    rows = edge_ref[...].reshape(deep * group * run, feat)
+    rows = jnp.concatenate([top_ref[...], low_ref[...]], axis=0).reshape(deep * group * run, feat)
     normed = layer_norm(rows, gain_ref[...])
     kv_s[...] = dot_f32(normed, w_ref[:, feat:]).astype(jnp.bfloat16).reshape(kv_s.shape)
     pair = 2 * head_width
     scale = LOG2E * head_width ** (-0.5)
     bias = jnp.where(
-        jnp.logical_and(keep_ref[0] == 0, lax.broadcasted_iota(jnp.int32, (1, 2 * length), 1) < length), -jnp.inf, 0.0
+        jnp.logical_and(half_ref[1] == 0, lax.broadcasted_iota(jnp.int32, (1, 2 * length), 1) < length), -jnp.inf, 0.0
     )
     low = low_lanes(length, pair, head_width)
     ones = jnp.ones((2 * length, pair), jnp.bfloat16)
@@ -168,83 +386,115 @@
     lax.fori_loop(0, group, panel, 0)
 
 
-def window_mix(half, keep, edge, q, kv_own, gain_row, w_qkv):
-    deep, wide, run, feat = edge.shape
+def window_mix(half_keep, edges, spots, q, kv_own, gain_row, w_qkv):
+    _, deep, wide, run, feat = q.shape
     group = min(GROUP, wide)
     head_width = feat // HEADS
-    own = lambda width: pl.BlockSpec((1, deep, group, run, width), lambda i: (half, 0, i, 0, 0))
-    flat = pl.BlockSpec((deep, group, run, feat), lambda i: (0, i, 0, 0))
+    own = lambda width: pl.BlockSpec((1, deep, group, run, width), lambda i, hk: (hk[0], 0, i, 0, 0))
+    side = lambda spot: pl.BlockSpec((deep // 2, group, run, feat), lambda i, hk: (spot, i, 0, 0))
+    flat = pl.BlockSpec((deep, group, run, feat), lambda i, hk: (0, i, 0, 0))
     tokens = deep * wide * run
     return pl.pallas_call(
         functools.partial(window_kernel, head_width),
-        grid=(wide // group,),
-        out_shape=jax.ShapeDtypeStruct(edge.shape, jnp.bfloat16),
-        in_specs=[
-            pl.BlockSpec(memory_space=pltpu.SMEM),
-            flat,
-            own(feat),
-            own(2 * feat),
-            pl.BlockSpec((1, feat), lambda i: (0, 0)),
-            pl.BlockSpec((feat, 3 * feat), lambda i: (0, 0), pipeline_mode=pl.Buffered(1)),
-        ],
-        out_specs=flat,
-        scratch_shapes=[pltpu.VMEM((deep, group, run, 2 * feat), jnp.bfloat16)],
+        out_shape=jax.ShapeDtypeStruct((deep, wide, run, feat), jnp.bfloat16),
+        grid_spec=pltpu.PrefetchScalarGridSpec(
+            num_scalar_prefetch=1,
+            grid=(wide // group,),
+            in_specs=[
+                side(spots[0]),
+                side(spots[1]),
+                own(feat),
+                own(2 * feat),
+                pl.BlockSpec((1, feat), lambda i, hk: (0, 0)),
+                pl.BlockSpec((feat, 3 * feat), lambda i, hk: (0, 0), pipeline_mode=pl.Buffered(1)),
+            ],
+            out_specs=flat,
+            scratch_shapes=[pltpu.VMEM((deep, group, run, 2 * feat), jnp.bfloat16)],
+        ),
         compiler_params=pltpu.CompilerParams(vmem_limit_bytes=VMEM_LIMIT),
         cost_estimate=pl.CostEstimate(
             flops=2 * tokens * feat * 2 * feat + 8 * tokens * 256 * feat,
             bytes_accessed=tokens * feat * 10 + feat * feat * 6,
             transcendentals=tokens * 256 * HEADS,
         ),
-    )(keep, edge, q, kv_own, gain_row, w_qkv)
-
-
-def cross_kernel(tiles, head_width, wanted, own_halves, refs):
-    me_ref, tile_ref, panel_ref, valid_ref, tok_ref = refs[:5]
-    recv = refs[5 : 4 + tiles]
-    q_ref, mix_a, mix_b, gain_ref, wqkv_ref, wproj_ref = refs[4 + tiles : 10 + tiles]
+    )(half_keep, edges[0], edges[1], q, kv_own, gain_row, w_qkv)
+
+
+def direct_parts(recv, tok_ref, tiles, wanted, cap):
+    cut = tok_ref.shape[1] // 2
+    wide = tok_ref.shape[2]
+
+    def own(j, seen):
+        return tok_ref.at[j // wide, :cut, j % wide], tok_ref.at[j // wide, cut:, j % wide]
+
+    def other(r):
+        return lambda j, seen: (recv[r - 1].at[seen[r], :cut], recv[r - 1].at[seen[r], cut:])
+
+    return {r: own if r == 0 else other(r) for r in range(tiles) if (wanted >> r) & 1}
+
+
+def relay_parts(recv, tok_ref, tiles, wanted, cap):
+    near, first, second, x_same, x_cross, y_same, y_cross, rest = recv
+    cut = tok_ref.shape[1] // 2
+    wide = tok_ref.shape[2]
+    deep = tok_ref.shape[1]
+    at = lambda ref, j: ref.at[j // wide, :, j % wide]
+    table = {
+        0: lambda j, seen: (tok_ref.at[j // wide, :cut, j % wide], tok_ref.at[j // wide, cut:, j % wide]),
+        1: lambda j, seen: (near.at[deep + seen[1], :cut], near.at[deep + seen[1], cut:]),
+        2: lambda j, seen: (at(first, j), x_same.at[seen[2] + seen[6]]),
+        3: lambda j, seen: (rest.at[seen[3]], x_cross.at[seen[3] + seen[7]]),
+        4: lambda j, seen: (y_same.at[seen[4] + seen[6]], at(second, j)),
+        5: lambda j, seen: (y_cross.at[seen[5] + seen[7]], rest.at[cap + seen[5]]),
+        6: lambda j, seen: (y_same.at[seen[4] + seen[6]], x_same.at[seen[2] + seen[6]]),
+        7: lambda j, seen: (y_cross.at[seen[5] + seen[7]], x_cross.at[seen[3] + seen[7]]),
+    }
+    return {r: table[r] for r in range(tiles) if (wanted >> r) & 1}
+
+
+def cross_kernel(plan, tiles, head_width, wanted, recv_count, cap, refs):
+    me_ref, tile_ref, panel_ref, valid_ref, half_ref, tok_ref = refs[:6]
+    recv = refs[6 : 6 + recv_count]
+    q_ref, mix_a, mix_b, gain_ref, wqkv_ref, wproj_ref = refs[6 + recv_count : 12 + recv_count]
     out_ref, got, q_s, own_s, res_s, wkv_s, wp_s, kv_s, mixed_s, seen, ids, w_sem, sems = refs[-13:]
     panels, deep, run, feat = got.shape
     half = panels // 2
+    cut = deep // 2
     length = deep * run
     me = me_ref[0]
+    parts = plan(recv, tok_ref, tiles, wanted, cap)
     for t in range(tiles):
         seen[t] = 0
 
     def fetch(p, count):
-        source = tile_ref[me * panels + p]
-        slot = seen[source]
-        seen[source] = slot + 1
-        r = source ^ me
+        r = tile_ref[me * panels + p] ^ me
         hit = ((wanted >> r) & 1) == 1
 
         @pl.when(hit)
         def _():
             ids[count] = p
             j = panel_ref[me * panels + p]
-
-            @pl.when(r == 0)
-            def _():
-                pltpu.make_async_copy(tok_ref.at[j // half, :, j % half], got.at[count], sems.at[0, count]).start()
-
-            for k in range(1, tiles):
-                if (wanted >> k) & 1:
-
-                    @pl.when(r == k)
-                    def _(k=k):
-                        pltpu.make_async_copy(recv[k - 1].at[slot], got.at[count], sems.at[0, count]).start()
+            for k, pick in parts.items():
+
+                @pl.when(r == k)
+                def _(pick=pick):
+                    top, bottom = pick(j, seen)
+                    pltpu.make_async_copy(top, got.at[count, :cut], sems.at[0, count]).start()
+                    pltpu.make_async_copy(bottom, got.at[count, cut:], sems.at[4, count]).start()
 
             u = p // half
             w = p % half
             pltpu.make_async_copy(q_ref.at[u, :, w], q_s.at[count], sems.at[1, count]).start()
 
-            @pl.when(u == own_halves[0])
+            @pl.when(u == half_ref[0])
             def _():
                 pltpu.make_async_copy(mix_a.at[:, w], own_s.at[count], sems.at[2, count]).start()
 
-            @pl.when(u == own_halves[1])
+            @pl.when(u != half_ref[0])
             def _():
                 pltpu.make_async_copy(mix_b.at[:, w], own_s.at[count], sems.at[2, count]).start()
 
+        seen[r] = seen[r] + 1
         return count + hit.astype(jnp.int32)
 
     load_wkv = pltpu.make_async_copy(wqkv_ref.at[:, feat:], wkv_s, w_sem.at[0])
@@ -269,8 +519,11 @@
 
             @pl.when(first + i < total)
             def _(i=i):
-                for k, place in enumerate((got, q_s, own_s)):
-                    pltpu.make_async_copy(tok_ref.at[0, :, 0], place.at[first + i], sems.at[k, first + i]).wait()
+                n_i = first + i
+                for k, place in ((0, got.at[n_i, :cut]), (4, got.at[n_i, cut:])):
+                    pltpu.make_async_copy(tok_ref.at[0, :cut, 0], place, sems.at[k, n_i]).wait()
+                for k, place in ((1, q_s.at[n_i]), (2, own_s.at[n_i])):
+                    pltpu.make_async_copy(tok_ref.at[0, :, 0], place, sems.at[k, n_i]).wait()
 
         rows = got[pl.ds(first, 2)].reshape(2 * length, feat)
         normed = layer_norm(rows, gain_ref[...])
@@ -323,10 +576,11 @@
     lax.fori_loop(0, total, finish, 0)
 
 
-def cross_and_project(wanted, me, tile_table, panel_table, valid, tok, recv, q, mixes, gain_row, w_qkv, w_proj, earlier):
+def cross_and_project(
+    plan, wanted, tiles, cap, me, tile_table, panel_table, valid, half_keep, tok, recv, q, mixes, gain_row, w_qkv, w_proj, earlier
+):
     halves, deep, wide, run, feat = tok.shape
     panels = halves * wide
-    tiles = len(recv) + 1
     head_width = feat // HEADS
     length = deep * run
     smem = pl.BlockSpec(memory_space=pltpu.SMEM)
@@ -334,8 +588,8 @@
     share = bin(wanted).count("1") / tiles
     tokens = int(panels * length * share)
     many = pltpu.VMEM((panels, deep, run, feat), jnp.bfloat16)
-    operands = [me, tile_table, panel_table, valid, tok, *recv, q, *mixes, gain_row, w_qkv, w_proj]
-    specs = [smem] * 4 + [anym] * (tiles + 3) + [pl.BlockSpec((1, feat), lambda: (0, 0))] + [anym] * 2
+    operands = [me, tile_table, panel_table, valid, half_keep, tok, *recv, q, *mixes, gain_row, w_qkv, w_proj]
+    specs = [smem] * 5 + [anym] * (len(recv) + 4) + [pl.BlockSpec((1, feat), lambda: (0, 0))] + [anym] * 2
     aliases = {}
     if earlier is not None:
         aliases = {len(operands): 0}
@@ -343,7 +597,7 @@
         specs.append(anym)
 
     def kernel(*refs):
-        cross_kernel(tiles, head_width, wanted, (0, 1), refs)
+        cross_kernel(plan, tiles, head_width, wanted, len(recv), cap, refs)
 
     return pl.pallas_call(
         kernel,
@@ -362,7 +616,7 @@
             pltpu.SMEM((tiles,), jnp.int32),
             pltpu.SMEM((panels,), jnp.int32),
             pltpu.SemaphoreType.DMA((2,)),
-            pltpu.SemaphoreType.DMA((4, panels)),
+            pltpu.SemaphoreType.DMA((5, panels)),
         ],
         input_output_aliases=aliases,
         compiler_params=pltpu.CompilerParams(vmem_limit_bytes=VMEM_LIMIT),
@@ -379,42 +633,89 @@
     run = 16
     wide = tok_cols // run
     tok = tokens.reshape(2, tok_rows // 2, wide, run, feat)
-    gain_row = gain.reshape(1, feat)
     tiles = partner_tile.shape[1]
     panels = partner_tile.shape[2]
     cap = 2 * max(1, panels // tiles)
     slab_count = scene_first.shape[0]
-    forward = [(i, i + 1) for i in range(slab_count - 1)]
-    backward = [(i + 1, i) for i in range(slab_count - 1)]
-    before = lax.ppermute(tok[1], ("scene", "tile"), forward)
-    after = lax.ppermute(tok[0], ("scene", "tile"), backward)
-
     me = lax.axis_index("tile").reshape(1).astype(jnp.int32)
     tile_table = partner_tile.reshape(tiles * panels)
     panel_table = partner_panel.reshape(tiles * panels)
-    outgoing = pack(me, tile_table, panel_table, tok, tiles, cap)
-    recv = [
-        lax.ppermute(outgoing[r - 1], "tile", [(i, i ^ r) for i in range(tiles)]) for r in range(1, tiles)
-    ]
-
+    valid = window_valid.reshape(panels)
+    gain_row = gain.reshape(1, feat)
     slab_index = lax.axis_index(("scene", "tile"))
     after_index = jnp.minimum(slab_index + 1, slab_count - 1)
     own_first = jnp.logical_or(scene_first[slab_index] == 1, slab_index == 0)
     next_first = jnp.logical_or(scene_first[after_index] == 1, slab_index + 1 >= slab_count)
-    keep_before = jnp.logical_not(own_first).astype(jnp.int32).reshape(1)
-    keep_after = jnp.logical_not(next_first).astype(jnp.int32).reshape(1)
-
-    q, kv = project_own(tok, gain_row, w_qkv)
-    mix_up = window_mix(0, keep_before, before, q, kv, gain_row, w_qkv)
-    mix_down = window_mix(1, keep_after, after, q, kv, gain_row, w_qkv)
-    valid = window_valid.reshape(panels)
-    out = None
-    late = (1 << tiles) - (1 << (tiles - tiles // 4))
-    for wanted in ((1 << tiles) - 1 - late, late):
-        parts = [block if (wanted >> r) & 1 else tok for r, block in enumerate(recv, 1)]
-        out = cross_and_project(
-            wanted, me, tile_table, panel_table, valid, tok, parts, q, (mix_up, mix_down), gain_row, w_qkv, w_proj, out
+    keep_before = jnp.logical_not(own_first).astype(jnp.int32)
+    keep_after = jnp.logical_not(next_first).astype(jnp.int32)
+
+    def xor(block, bits):
+        return lax.ppermute(block, "tile", [(i, i ^ bits) for i in range(tiles)])
+
+    def cross(plan, wanted, recv, mixes, half_keep, earlier):
+        return cross_and_project(
+            plan,
+            wanted,
+            tiles,
+            cap,
+            me,
+            tile_table,
+            panel_table,
+            valid,
+            half_keep,
+            tok,
+            recv,
+            q,
+            mixes,
+            gain_row,
+            w_qkv,
+            w_proj,
+            earlier,
         )
+
+    if tiles == 8:
+        first, second = split_halves(tok)
+        first = xor(first, 2)
+        second = xor(second, 4)
+        near = xor(pack_near(me, tile_table, panel_table, tok, cap), 1)
+        q, kv = project_own(tok, gain_row, w_qkv)
+        odd = slab_index % 2
+        near_half = jnp.stack([1 - odd, jnp.where(odd == 1, keep_before, keep_after)]).astype(jnp.int32)
+        far_half = jnp.stack([odd, jnp.where(odd == 1, keep_after, keep_before)]).astype(jnp.int32)
+        mix_near = window_mix(near_half, (near, near), (0, 1), q, kv, gain_row, w_qkv)
+        rim_a, rim_b = pack_rim(me, tok, first, second)
+        links_a, links_b = [], []
+        for low in range(1, slab_count - 1, 2):
+            held = (low, low + 1) if low % 4 == 1 else (low ^ 4, (low + 1) ^ 4)
+            links_a += [(low ^ 2, low + 1), ((low + 1) ^ 2, low)]
+            links_b += [(held[0], low + 1), (held[1], low)]
+        rim_a = lax.ppermute(rim_a, ("scene", "tile"), links_a)
+        rim_b = lax.ppermute(rim_b, ("scene", "tile"), links_b)
+        x_same, x_cross, y_same, y_cross, rest = pack_far(me, tile_table, panel_table, tok, first, second, cap)
+        rim_a, rim_b, x_same, y_same, rest = lax.optimization_barrier((rim_a, rim_b, x_same, y_same, rest))
+        x_same, y_same, rest = xor(x_same, 2), xor(y_same, 4), xor(rest, 1)
+        mix_far = window_mix(far_half, (rim_a, rim_b), (0, 0), q, kv, gain_row, w_qkv)
+        x_same, y_same, x_cross, y_cross = lax.optimization_barrier((x_same, y_same, x_cross, y_cross))
+        x_cross, y_cross = xor(x_cross, 3), xor(y_cross, 5)
+        mixes = (mix_near, mix_far)
+        idle = rest
+        early = (near, first, second, x_same, idle, y_same, idle, idle)
+        late = (near, first, second, x_same, x_cross, y_same, y_cross, rest)
+        out = cross(relay_parts, 0b01010111, early, mixes, near_half, None)
+        out = cross(relay_parts, 0b10101000, late, mixes, near_half, out)
+    else:
+        forward = [(i, i + 1) for i in range(slab_count - 1)]
+        backward = [(i + 1, i) for i in range(slab_count - 1)]
+        before = lax.ppermute(tok[1], ("scene", "tile"), forward)
+        after = lax.ppermute(tok[0], ("scene", "tile"), backward)
+        outgoing = pack(me, tile_table, panel_table, tok, tiles, cap)
+        recv = [xor(outgoing[r - 1], r) for r in range(1, tiles)]
+        q, kv = project_own(tok, gain_row, w_qkv)
+        zero = jnp.zeros((), jnp.int32)
+        upper = jnp.stack([zero, keep_before])
+        mix_up = window_mix(upper, (before, before), (0, 1), q, kv, gain_row, w_qkv)
+        mix_down = window_mix(jnp.stack([zero + 1, keep_after]), (after, after), (0, 1), q, kv, gain_row, w_qkv)
+        out = cross(direct_parts, (1 << tiles) - 1, recv, (mix_up, mix_down), upper, None)
     return out.reshape(tokens.shape)
 
 

time: 173 us -> 196 us (1.13)
  the two profiles are of different devices: /device:TPU:16 before, /device:TPU:11 now
where the time goes in v4:
time: 196 us; the launch traced here: 192 us
  Pallas kernels  111 us (57%)
  waiting for transfers between devices  54.1 us (28%)
  starting transfers between devices  15.1 us (8%)
  local copies, waits for them, and re-layouts  8.55 us (4%)
    pallas_call x2, Pallas kernels, cross_and_project(): pl.pallas_call(kernel, out_shape=jax.ShapeDtypeStruct(tok.shape, jnp.bflo...  37.6 us
    ppermute x8, waiting for transfers between devices, xor(): return lax.ppermute(block, 'tile', [(i, i ^ bits) for i in range(tiles)])  37.3 us
    pallas_call x2, Pallas kernels, window_mix(): pl.pallas_call(functools.partial(window_kernel, head_width), out_shape=ja...  37.2 us
    pallas_call x1, Pallas kernels, project_own(): pl.pallas_call(qkv_kernel, grid=(halves * 2,), out_shape=[jax.ShapeDtypeS...  20.2 us
    ppermute x1, waiting for transfers between devices, per_device(): rim_b = lax.ppermute(rim_b, ('scene', 'tile'), links_b)  13.4 us
    ppermute x8, starting transfers between devices, xor(): return lax.ppermute(block, 'tile', [(i, i ^ bits) for i in range(tiles)])  7.41 us
    pallas_call x1, Pallas kernels, pack_far(): pl.pallas_call(functools.partial(far_kernel, cap), out_shape=[jax.ShapeDt...  6.15 us
    unnamed x23, local copies, waits for them, and re-layouts  6.08 us
  transfers between devices with their start and end apart: 10, of which 3 were waited for; matrix products, arithmetic and copies ran while one was open for 3% of the time, Pallas kernels for 48%

profile of v4, /device:TPU:11, one launch (start us, length us, event | category | flops | bytes accessed | tf_op | source)
XLA Modules:
  0.0 192.3 jit_solution(8744695956045537705)
XLA Ops:
  0.0 3.3 %shard_map.83 = (bf16[2,4,8,16,1024]{4,3,2,1,0:T(8,128)(2,1)}, bf16[2,4,8,16,1024]{4,3,2,1,0:T(8,128)(2,1)}) custom-call(bf16[2,8,8,16,1024]{4,3,2,1,0:T(8,128)(2,1)} %bitcast.11), custom_call_target="tpu_custom_call" | custom-call | bytes 16777216 | tf_op jit(solution)/shard_map/pallas_call | solution.py:122
  3.6 1.2 collective-permute-start.2
  7.3 4.2 %shard_map.82 = bf16[12,8,16,1024]{3,2,1,0:T(8,128)(2,1)} custom-call(s32[1]{0:T(128)} %bitcast.me_ref.refs_0_, s32[128]{0:T(128)} %reshape.26.tile_ref.refs_1_, s32[128]{0:T(128)} %reshape.27.panel_ref.refs_2_, bf16[2,8,8,16,1024]{4,3,2,1,0:T(8,128)(2,1)} %bitcast.12), custom_call_target="tpu_custom_call" | custom-call | bytes 6291456 | tf_op jit(solution)/shard_map/pallas_call | solution.py:169
  11.5 1.3 collective-permute-start
  12.8 37.3 %collective-permute-done.1.first_ref.refs_7_ = bf16[2,4,8,16,1024]{4,3,2,1,0:T(8,128)(2,1)} collective-permute-done((bf16[2,4,8,16,1024]{4,3,2,1,0:T(8,128)(2,1)}, bf16[2,4,8,16,1024]{4,3,2,1,0:T(8,128)(2,1)}, u32[]{:S(2)}, u32[]{:S(2)}) %collective-permute-start.1) | collective-permute-done | bytes 2097184 | tf_op jit(solution)/shard_map/ppermute | solution.py:653
  50.2 2.6 %shard_map.84 = (bf16[4,8,16,1024]{3,2,1,0:T(8,128)(2,1)}, bf16[4,8,16,1024]{3,2,1,0:T(8,128)(2,1)}) custom-call(s32[1]{0:T(128)} %bitcast.me_ref.refs_0_, bf16[2,8,8,16,1024]{4,3,2,1,0:T(8,128)(2,1)} %bitcast.13, bf16[2,4,8,16,1024]{4,3,2,1,0:T(8,128)(2,1)} %collective-permute-done.1.first_ref.refs_7_, ...), custom_call_target="tpu_custom_call" | custom-call | bytes 4194304 | tf_op jit(solution)/shard_map/pallas_call | solution.py:217
  52.8 3.7 %collective-permute-start.3 = (bf16[4,8,16,1024]{3,2,1,0:T(8,128)(2,1)}, bf16[4,8,16,1024]{3,2,1,0:T(8,128)(2,1)S(1)}, u32[]{:S(2)}, u32[]{:S(2)}) collective-permute-start(bf16[4,8,16,1024]{3,2,1,0:T(8,128)(2,1)} %get-tuple-element.27), channel_id=1, source_target_pairs={{3,2},{0,1},{1,4},{6,3},{7,6},{4,5},{5,8},{10,7},{11,10},{8,9},{9,... | collective-permute-start | bytes 3145736 | tf_op jit(solution)/shard_map/ppermute | solution.py:692
  56.5 4.0 %collective-permute-start.4 = (bf16[4,8,16,1024]{3,2,1,0:T(8,128)(2,1)}, bf16[4,8,16,1024]{3,2,1,0:T(8,128)(2,1)S(1)}, u32[]{:S(2)}, u32[]{:S(2)}) collective-permute-start(bf16[4,8,16,1024]{3,2,1,0:T(8,128)(2,1)} %get-tuple-element.28), channel_id=1, source_target_pairs={{1,2},{2,1},{7,4},{0,3},{5,6},{6,5},{3,8},{12,7},{9,10},{10,9},{15... | collective-permute-start | bytes 3145736 | tf_op jit(solution)/shard_map/ppermute | solution.py:693
  61.1 6.1 %shard_map.85 = (bf16[8,4,16,1024]{3,2,1,0:T(8,128)(2,1)}, bf16[8,4,16,1024]{3,2,1,0:T(8,128)(2,1)}, bf16[8,4,16,1024]{3,2,1,0:T(8,128)(2,1)}, bf16[8,4,16,1024]{3,2,1,0:T(8,128)(2,1)}, bf16[8,4,16,1024]{3,2,1,0:T(8,128)(2,1)}) custom-call(s32[1]{0:T(128)} %bitcast.me_ref.refs_0_, s32[128]{0:T(128)} %reshape.26.tile_ref.refs_1_, ...), custom_call_target="tpu_custom_call" | custom-call | bytes 14680064 | tf_op jit(solution)/shard_map/pallas_call | solution.py:296
  67.3 3.3 %collective-permute-done.3.top_ref = bf16[4,8,16,1024]{3,2,1,0:T(8,128)(2,1)S(1)} collective-permute-done((bf16[4,8,16,1024]{3,2,1,0:T(8,128)(2,1)}, bf16[4,8,16,1024]{3,2,1,0:T(8,128)(2,1)S(1)}, u32[]{:S(2)}, u32[]{:S(2)}) %collective-permute-start.3) | collective-permute-done | bytes 1048608 | tf_op jit(solution)/shard_map/ppermute | solution.py:692
  70.6 13.4 %collective-permute-done.4.low_ref = bf16[4,8,16,1024]{3,2,1,0:T(8,128)(2,1)S(1)} collective-permute-done((bf16[4,8,16,1024]{3,2,1,0:T(8,128)(2,1)}, bf16[4,8,16,1024]{3,2,1,0:T(8,128)(2,1)S(1)}, u32[]{:S(2)}, u32[]{:S(2)}) %collective-permute-start.4) | collective-permute-done | bytes 1048608 | tf_op jit(solution)/shard_map/ppermute | solution.py:693
  84.0 1.0 copy-done.10
  85.0 1.5 collective-permute-start.5
  86.8 20.2 %shard_map.86 = (bf16[2,8,8,16,1024]{4,3,2,1,0:T(8,128)(2,1)}, bf16[2,8,8,16,2048]{4,3,2,1,0:T(8,128)(2,1)}) custom-call(bf16[2,8,8,16,1024]{4,3,2,1,0:T(8,128)(2,1)} %bitcast.15, bf16[1,1024]{1,0:T(2,128)(2,1)} %reshape.30.gain_ref.refs_17_, bf16[1024,3072]{1,0:T(8,128)(2,1)} %refs_18_.3), custom_call_target="tpu_custom_call" | custom-call | flops 12884901888 | bytes 23068672 | tf_op jit(solution)/shard_map/pallas_call | solution.py:327
  110.0 0.7 collective-permute-start.9
  110.7 18.7 %shard_map.88.refs_16_ = bf16[8,8,16,1024]{3,2,1,0:T(8,128)(2,1)} custom-call(s32[2]{0:T(128)} %pad_add_fusion.1.half_ref, bf16[4,8,16,1024]{3,2,1,0:T(8,128)(2,1)} %copy-done.9, bf16[4,8,16,1024]{3,2,1,0:T(8,128)(2,1)} %copy-done.10, bf16[2,8,8,16,1024]{4,3,2,1,0:T(8,128)(2,1)} %get-tuple-element.41.q_ref.refs_14_, ...), custom_call_target="tpu_custom_call" | custom-call | flops 6442450944 | bytes 16777216 | tf_op jit(solution)/shard_map/pallas_call | solution.py:397
  129.4 1.7 collective-permute-start.7
  131.4 1.6 copy-done
  133.1 18.5 %shard_map.87.refs_15_ = bf16[8,8,16,1024]{3,2,1,0:T(8,128)(2,1)} custom-call(s32[2]{0:T(128)} %pad_add_fusion.half_ref.refs_4_, bf16[12,8,16,1024]{3,2,1,0:T(8,128)(2,1)} %copy-done, bf16[12,8,16,1024]{3,2,1,0:T(8,128)(2,1)} %copy-done, bf16[2,8,8,16,1024]{4,3,2,1,0:T(8,128)(2,1)} %get-tuple-element.41.q_ref.refs_14_, ...), custom_call_target="tpu_custom_call" | custom-call | flops 6442450944 | bytes 16777216 | tf_op jit(solution)/shard_map/pallas_call | solution.py:397
  151.6 1.0 copy-done.1
  152.6 22.2 %shard_map.89.refs_20_ = bf16[2,8,8,16,1024]{4,3,2,1,0:T(8,128)(2,1)} custom-call(s32[1]{0:T(128)} %bitcast.me_ref.refs_0_, s32[128]{0:T(128)} %reshape.26.tile_ref.refs_1_, s32[128]{0:T(128)} %reshape.27.panel_ref.refs_2_, s32[16]{0:T(128)} %bitcast.18, s32[2]{0:T(128)} %pad_add_fusion.half_ref.refs_4_, bf16[2,8,8,16,1024]{4,3,2,1,0:T(8,128)(2,1)} %bitcast.16, ...), custom_call_target="tpu_custom_call" | custom-call | flops 9395240960 | bytes 16777216 | tf_op jit(solution)/shard_map/pallas_call | solution.py:602
  174.8 0.9 copy-done.2
  175.8 1.0 copy-done.3
  176.8 15.4 %shard_map.90 = bf16[2,8,8,16,1024]{4,3,2,1,0:T(8,128)(2,1)} custom-call(s32[1]{0:T(128)} %bitcast.me_ref.refs_0_, s32[128]{0:T(128)} %reshape.26.tile_ref.refs_1_, s32[128]{0:T(128)} %reshape.27.panel_ref.refs_2_, s32[16]{0:T(128)} %bitcast.19, s32[2]{0:T(128)} %pad_add_fusion.half_ref.refs_4_, ...), custom_call_target="tpu_custom_call", output_to_operand_aliasing={{}: (20, {})} | custom-call | flops 5637144576 | bytes 12582912 | tf_op jit(solution)/shard_map/pallas_call | solution.py:602
  (35 shorter events, 5.9 us)
Async XLA Ops:
  0.0 4.9 %copy-start.4 = (s32[1,8,16]{2,1,0:T(8,128)S(1)}, s32[1,8,16]{2,1,0:T(8,128)}, u32[]{:S(2)}) copy-start(s32[1,8,16]{2,1,0:T(8,128)} %param.15) | copy-start | bytes 1540
  0.0 6.0 %copy-start.5 = (s32[1,8,16,1]{2,3,1,0:T(1,128)S(1)}, s32[1,8,16,1]{2,3,1,0:T(1,128)}, u32[]{:S(2)}) copy-start(s32[1,8,16,1]{2,3,1,0:T(1,128)} %param.14) | copy-start | bytes 1540
  3.3 46.9 %collective-permute-start.1 = (bf16[2,4,8,16,1024]{4,3,2,1,0:T(8,128)(2,1)}, bf16[2,4,8,16,1024]{4,3,2,1,0:T(8,128)(2,1)}, u32[]{:S(2)}, u32[]{:S(2)}) collective-permute-start(bf16[2,4,8,16,1024]{4,3,2,1,0:T(8,128)(2,1)} %get-tuple-element.25), channel_id=1, source_target_pairs={{0,2},{1,3},{2,0},{3,1},{4,6},{5,7},{6,4},{7,5},{8,10},{9,11},{10,... | collective-permute-start | bytes 6291464 | tf_op jit(solution)/shard_map/ppermute | solution.py:653
  3.6 46.6 %collective-permute-start.2 = (bf16[2,4,8,16,1024]{4,3,2,1,0:T(8,128)(2,1)}, bf16[2,4,8,16,1024]{4,3,2,1,0:T(8,128)(2,1)}, u32[]{:S(2)}, u32[]{:S(2)}) collective-permute-start(bf16[2,4,8,16,1024]{4,3,2,1,0:T(8,128)(2,1)} %get-tuple-element.26), channel_id=1, source_target_pairs={{0,4},{1,5},{2,6},{3,7},{4,0},{5,1},{6,2},{7,3},{8,12},{9,13},{10,... | collective-permute-start | bytes 6291464 | tf_op jit(solution)/shard_map/ppermute | solution.py:653
  11.5 49.0 %copy-start.6 = (bf16[1024]{0:T(1024)(128)(2,1)S(1)}, bf16[1024]{0:T(1024)(128)(2,1)}, u32[]{:S(2)}) copy-start(bf16[1024]{0:T(1024)(128)(2,1)} %param.9) | copy-start | bytes 6148
  11.5 119.9 %collective-permute-start = (bf16[12,8,16,1024]{3,2,1,0:T(8,128)(2,1)}, bf16[12,8,16,1024]{3,2,1,0:T(8,128)(2,1)S(1)}, u32[]{:S(2)}, u32[]{:S(2)}) collective-permute-start(bf16[12,8,16,1024]{3,2,1,0:T(8,128)(2,1)} %shard_map.82), channel_id=1, source_target_pairs={{0,1},{1,0},{2,3},{3,2},{4,5},{5,4},{6,7},{7,6},{8,9},{9,8},{10,11... | collective-permute-start | bytes 9437192 | tf_op jit(solution)/shard_map/ppermute | solution.py:653
  52.8 17.8 %collective-permute-start.3 = (bf16[4,8,16,1024]{3,2,1,0:T(8,128)(2,1)}, bf16[4,8,16,1024]{3,2,1,0:T(8,128)(2,1)S(1)}, u32[]{:S(2)}, u32[]{:S(2)}) collective-permute-start(bf16[4,8,16,1024]{3,2,1,0:T(8,128)(2,1)} %get-tuple-element.27), channel_id=1, source_target_pairs={{3,2},{0,1},{1,4},{6,3},{7,6},{4,5},{5,8},{10,7},{11,10},{8,9},{9,... | collective-permute-start | bytes 3145736 | tf_op jit(solution)/shard_map/ppermute | solution.py:692
  56.5 27.5 %collective-permute-start.4 = (bf16[4,8,16,1024]{3,2,1,0:T(8,128)(2,1)}, bf16[4,8,16,1024]{3,2,1,0:T(8,128)(2,1)S(1)}, u32[]{:S(2)}, u32[]{:S(2)}) collective-permute-start(bf16[4,8,16,1024]{3,2,1,0:T(8,128)(2,1)} %get-tuple-element.28), channel_id=1, source_target_pairs={{1,2},{2,1},{7,4},{0,3},{5,6},{6,5},{3,8},{12,7},{9,10},{10,9},{15... | collective-permute-start | bytes 3145736 | tf_op jit(solution)/shard_map/ppermute | solution.py:693
  70.6 13.5 %copy-start.9 = (bf16[4,8,16,1024]{3,2,1,0:T(8,128)(2,1)}, bf16[4,8,16,1024]{3,2,1,0:T(8,128)(2,1)S(1)}, u32[]{:S(2)}) copy-start(bf16[4,8,16,1024]{3,2,1,0:T(8,128)(2,1)S(1)} %collective-permute-done.3.top_ref) | copy-start | bytes 3145732
  84.0 1.0 copy-start.10
  85.0 22.0 %copy-start.7 = (s32[32]{0:T(128)S(1)}, s32[32]{0:T(128)}, u32[]{:S(2)}) copy-start(s32[32]{0:T(128)} %param.12) | copy-start | bytes 388
  85.0 44.4 %collective-permute-start.5 = (bf16[8,4,16,1024]{3,2,1,0:T(8,128)(2,1)}, bf16[8,4,16,1024]{3,2,1,0:T(8,128)(2,1)}, u32[]{:S(2)}, u32[]{:S(2)}) collective-permute-start(bf16[8,4,16,1024]{3,2,1,0:T(8,128)(2,1)} %get-tuple-element.32), channel_id=1, source_target_pairs={{0,2},{1,3},{2,0},{3,1},{4,6},{5,7},{6,4},{7,5},{8,10},{9,11},{10,... | collective-permute-start | bytes 3145736 | tf_op jit(solution)/shard_map/ppermute | solution.py:653
  86.5 42.9 %collective-permute-start.6 = (bf16[8,4,16,1024]{3,2,1,0:T(8,128)(2,1)}, bf16[8,4,16,1024]{3,2,1,0:T(8,128)(2,1)}, u32[]{:S(2)}, u32[]{:S(2)}) collective-permute-start(bf16[8,4,16,1024]{3,2,1,0:T(8,128)(2,1)} %get-tuple-element.33), channel_id=1, source_target_pairs={{0,4},{1,5},{2,6},{3,7},{4,0},{5,1},{6,2},{7,3},{8,12},{9,13},{10,... | collective-permute-start | bytes 3145736 | tf_op jit(solution)/shard_map/ppermute | solution.py:653
  110.0 41.6 %collective-permute-start.9 = (bf16[8,4,16,1024]{3,2,1,0:T(8,128)(2,1)}, bf16[8,4,16,1024]{3,2,1,0:T(8,128)(2,1)S(1)}, u32[]{:S(2)}, u32[]{:S(2)}) collective-permute-start(bf16[8,4,16,1024]{3,2,1,0:T(8,128)(2,1)} %get-tuple-element.40), channel_id=1, source_target_pairs={{0,1},{1,0},{2,3},{3,2},{4,5},{5,4},{6,7},{7,6},{8,9},{9,8},{10,11... | collective-permute-start | bytes 3145736 | tf_op jit(solution)/shard_map/ppermute | solution.py:653
  110.7 20.4 %copy-start.8 = (bf16[8,4,16,1024]{3,2,1,0:T(8,128)(2,1)S(1)}, bf16[8,4,16,1024]{3,2,1,0:T(8,128)(2,1)}, u32[]{:S(2)}) copy-start(bf16[8,4,16,1024]{3,2,1,0:T(8,128)(2,1)} %get-tuple-element.39) | copy-start | bytes 3145732
  129.4 45.4 %collective-permute-start.7 = (bf16[8,4,16,1024]{3,2,1,0:T(8,128)(2,1)}, bf16[8,4,16,1024]{3,2,1,0:T(8,128)(2,1)S(1)}, u32[]{:S(2)}, u32[]{:S(2)}) collective-permute-start(bf16[8,4,16,1024]{3,2,1,0:T(8,128)(2,1)} %get-tuple-element.37), channel_id=1, source_target_pairs={{0,3},{1,2},{2,1},{3,0},{4,7},{5,6},{6,5},{7,4},{8,11},{9,10},{10,... | collective-permute-start | bytes 3145736 | tf_op jit(solution)/shard_map/ppermute | solution.py:653
  131.1 43.7 %collective-permute-start.8 = (bf16[8,4,16,1024]{3,2,1,0:T(8,128)(2,1)S(1)}, bf16[8,4,16,1024]{3,2,1,0:T(8,128)(2,1)S(1)}, u32[]{:S(2)}, u32[]{:S(2)}) collective-permute-start(bf16[8,4,16,1024]{3,2,1,0:T(8,128)(2,1)S(1)} %copy-done.8), channel_id=1, source_target_pairs={{0,5},{1,4},{2,7},{3,6},{4,1},{5,0},{6,3},{7,2},{8,13},{9,12},{10,... | collective-permute-start | bytes 3145736 | tf_op jit(solution)/shard_map/ppermute | solution.py:653
  131.4 1.6 copy-start
  151.6 1.0 copy-start.1
  174.8 1.0 copy-start.2
  175.8 1.0 copy-start.3

commit v5 on v4

--- a/solution.py
+++ b/solution.py
@@ -106,27 +106,31 @@
         store.wait()
 
 
-def halves_kernel(tok_ref, first_ref, second_ref, bounce, sems):
-    deep = first_ref.shape[1]
-    pairs = []
-    for u in range(2):
-        pairs.append((tok_ref.at[u, :deep], first_ref.at[u]))
-        pairs.append((tok_ref.at[u, deep:], second_ref.at[u]))
-    copy_through(pairs, bounce, sems)
-
-
-def split_halves(tok):
+def halves_kernel(me_ref, tok_ref, *rest):
+    outs, bounce, sems = rest[:4], rest[4], rest[5]
+    deep = outs[0].shape[0]
+    part = me_ref[0] & 1
+    sources = [
+        tok_ref.at[part, :deep],
+        tok_ref.at[part, deep:],
+        tok_ref.at[1 - part, :deep],
+        tok_ref.at[1 - part, deep:],
+    ]
+    copy_through(list(zip(sources, outs)), bounce, sems)
+
+
+def split_halves(me, tok):
     halves, deep, wide, run, feat = tok.shape
-    part = (halves, deep // 2, wide, run, feat)
+    part = (deep // 2, wide, run, feat)
     anym = pl.BlockSpec(memory_space=pl.ANY)
     return pl.pallas_call(
         halves_kernel,
-        out_shape=[jax.ShapeDtypeStruct(part, tok.dtype)] * 2,
-        in_specs=[anym],
-        out_specs=[anym] * 2,
-        scratch_shapes=[pltpu.VMEM((4,) + part[1:], tok.dtype), pltpu.SemaphoreType.DMA((2, 4))],
-        cost_estimate=pl.CostEstimate(flops=0, bytes_accessed=16 << 20, transcendentals=0),
-    )(tok)
+        out_shape=[jax.ShapeDtypeStruct(part, tok.dtype)] * 4,
+        in_specs=[pl.BlockSpec(memory_space=pltpu.SMEM), anym],
+        out_specs=[anym] * 4,
+        scratch_shapes=[pltpu.VMEM((4,) + part, tok.dtype), pltpu.SemaphoreType.DMA((2, 4))],
+        cost_estimate=pl.CostEstimate(flops=0, bytes_accessed=8 << 20, transcendentals=0),
+    )(me, tok)
 
 
 def near_kernel(cap, me_ref, tile_ref, panel_ref, tok_ref, out_ref, bounce, sems, slots, slot_sems):
@@ -181,59 +185,17 @@
     )(me, tile_table, panel_table, tok)
 
 
-def rim_kernel(me_ref, tok_ref, first_ref, second_ref, out_a, out_b, bounce, sems):
-    deep = out_a.shape[0]
-    me = me_ref[0]
-    part = me & 1
-    held = jnp.logical_or(me % 4 == 1, me % 4 == 2)
-    bite = deep // 2
-    spots = [pl.ds(k * bite, bite) for k in range(2)]
-    for k in range(2):
-        pltpu.make_async_copy(first_ref.at[part, spots[k]], bounce.at[k], sems.at[0, k]).start()
-
-        @pl.when(held)
-        def _(k=k):
-            pltpu.make_async_copy(
-                tok_ref.at[part, pl.ds(deep + k * bite, bite)], bounce.at[2 + k], sems.at[0, 2 + k]
-            ).start()
-
-        @pl.when(jnp.logical_not(held))
-        def _(k=k):
-            pltpu.make_async_copy(second_ref.at[part, spots[k]], bounce.at[2 + k], sems.at[0, 2 + k]).start()
-
-    stores = []
-    for k in range(4):
-        pltpu.make_async_copy(first_ref.at[0, spots[0]], bounce.at[k], sems.at[0, k]).wait()
-        store = pltpu.make_async_copy(bounce.at[k], (out_a if k < 2 else out_b).at[spots[k % 2]], sems.at[1, k])
-        store.start()
-        stores.append(store)
-    for store in stores:
-        store.wait()
-
-
-def pack_rim(me, tok, first, second):
-    halves, deep, wide, run, feat = first.shape
-    anym = pl.BlockSpec(memory_space=pl.ANY)
-    return pl.pallas_call(
-        rim_kernel,
-        out_shape=[jax.ShapeDtypeStruct(first.shape[1:], tok.dtype)] * 2,
-        in_specs=[pl.BlockSpec(memory_space=pltpu.SMEM), anym, anym, anym],
-        out_specs=[anym] * 2,
-        scratch_shapes=[pltpu.VMEM((4, deep // 2, wide, run, feat), tok.dtype), pltpu.SemaphoreType.DMA((2, 4))],
-        cost_estimate=pl.CostEstimate(flops=0, bytes_accessed=4 << 20, transcendentals=0),
-    )(me, tok, first, second)
-
-
-def far_kernel(cap, me_ref, tile_ref, panel_ref, tok_ref, first_ref, second_ref, *rest):
-    outs, slab, got_a, got_b, sem, sems = rest[:5], *rest[5:]
+def far_kernel(cap, me_ref, tile_ref, panel_ref, tok_ref, *rest):
+    sides, outs, slab, got, sem, sems = rest[:4], rest[4:9], *rest[9:]
     halves, deep, wide, run, feat = tok_ref.shape
     panels = halves * wide
     cut = deep // 2
     me = me_ref[0]
-    loads = [
-        pltpu.make_async_copy(src, dst, sem.at[k])
-        for k, (src, dst) in enumerate(((tok_ref, slab), (first_ref, got_a), (second_ref, got_b)))
-    ]
+    part = me & 1
+    loads = [pltpu.make_async_copy(tok_ref, slab, sem.at[4])]
+    for k in range(4):
+        u = part if k < 2 else 1 - part
+        loads.append(pltpu.make_async_copy(sides[k], got.at[k % 2, u], sem.at[k]))
     for load in loads:
         load.start()
     for load in loads:
@@ -241,7 +203,7 @@
     totals = []
     for k, (bits, relay) in enumerate(((2, 4), (3, 4), (4, 2), (5, 2))):
         asker = me ^ bits
-        buffer, rows = (got_b, slice(cut, deep)) if relay == 4 else (got_a, slice(0, cut))
+        buffer, rows = (1, slice(cut, deep)) if relay == 4 else (0, slice(0, cut))
 
         def body(p, count, k=k, asker=asker, relay=relay, buffer=buffer, rows=rows):
             named = tile_ref[asker * panels + p]
@@ -255,7 +217,9 @@
 
             @pl.when(jnp.logical_and(hit, jnp.logical_not(own)))
             def _():
-                pltpu.make_async_copy(buffer.at[j // wide, :, j % wide], outs[k].at[count], sems.at[k, count]).start()
+                pltpu.make_async_copy(
+                    got.at[buffer, j // wide, :, j % wide], outs[k].at[count], sems.at[k, count]
+                ).start()
 
             return count + hit.astype(jnp.int32)
 
@@ -267,13 +231,13 @@
         named = tile_ref[asker * panels + p]
         j = panel_ref[asker * panels + p]
         fresh = []
-        for k, (relay, buffer) in enumerate(((2, got_a), (4, got_b))):
+        for k, relay in enumerate((2, 4)):
             hit = jnp.logical_and(named == me ^ relay, counts[k] < cap)
 
             @pl.when(hit)
-            def _(k=k, buffer=buffer):
+            def _(k=k):
                 spot = k * cap + counts[k]
-                pltpu.make_async_copy(buffer.at[j // wide, :, j % wide], outs[4].at[spot], sems.at[4, spot]).start()
+                pltpu.make_async_copy(got.at[k, j // wide, :, j % wide], outs[4].at[spot], sems.at[4, spot]).start()
 
             fresh.append(counts[k] + hit.astype(jnp.int32))
         return tuple(fresh)
@@ -285,10 +249,10 @@
 
             @pl.when(used)
             def _(k=k, c=c):
-                pltpu.make_async_copy(got_a.at[0, :, 0], outs[k].at[c], sems.at[k, c]).wait()
-
-
-def pack_far(me, tile_table, panel_table, tok, first, second, cap):
+                pltpu.make_async_copy(got.at[0, 0, :, 0], outs[k].at[c], sems.at[k, c]).wait()
+
+
+def pack_far(me, tile_table, panel_table, tok, sides, cap):
     halves, deep, wide, run, feat = tok.shape
     smem = pl.BlockSpec(memory_space=pltpu.SMEM)
     anym = pl.BlockSpec(memory_space=pl.ANY)
@@ -296,18 +260,17 @@
     return pl.pallas_call(
         functools.partial(far_kernel, cap),
         out_shape=[jax.ShapeDtypeStruct(block, tok.dtype)] * 5,
-        in_specs=[smem, smem, smem, anym, anym, anym],
+        in_specs=[smem, smem, smem] + [anym] * 5,
         out_specs=[anym] * 5,
         scratch_shapes=[
             pltpu.VMEM(tok.shape, tok.dtype),
-            pltpu.VMEM(first.shape, tok.dtype),
-            pltpu.VMEM(second.shape, tok.dtype),
-            pltpu.SemaphoreType.DMA((3,)),
+            pltpu.VMEM((2, halves, deep // 2, wide, run, feat), tok.dtype),
+            pltpu.SemaphoreType.DMA((5,)),
             pltpu.SemaphoreType.DMA((5, 2 * cap)),
         ],
         compiler_params=pltpu.CompilerParams(vmem_limit_bytes=VMEM_LIMIT),
         cost_estimate=pl.CostEstimate(flops=0, bytes_accessed=14 << 20, transcendentals=0),
-    )(me, tile_table, panel_table, tok, first, second)
+    )(me, tile_table, panel_table, tok, *sides)
 
 
 def qkv_kernel(tok_ref, gain_ref, w_ref, q_ref, kv_ref):
@@ -344,10 +307,14 @@
     )(tok, gain_row, w_qkv)
 
 
-def window_kernel(head_width, half_ref, top_ref, low_ref, q_ref, kvo_ref, gain_ref, w_ref, mix_ref, kv_s):
+def window_kernel(head_width, half_ref, *refs):
+    edges, (q_ref, kvo_ref, gain_ref, w_ref, mix_ref, kv_s) = refs[:-6], refs[-6:]
     deep, group, run, feat = mix_ref.shape
     length = deep * run
-    rows = jnp.concatenate([top_ref[...], low_ref[...]], axis=0).reshape(deep * group * run, feat)
+    bottom = edges[1][...]
+    if len(edges) == 3:
+        bottom = jnp.where(half_ref[2] == 1, bottom, edges[2][...])
+    rows = jnp.concatenate([edges[0][...], bottom], axis=0).reshape(deep * group * run, feat)
     normed = layer_norm(rows, gain_ref[...])
     kv_s[...] = dot_f32(normed, w_ref[:, feat:]).astype(jnp.bfloat16).reshape(kv_s.shape)
     pair = 2 * head_width
@@ -401,8 +368,7 @@
             num_scalar_prefetch=1,
             grid=(wide // group,),
             in_specs=[
-                side(spots[0]),
-                side(spots[1]),
+                *[side(spot) for spot in spots],
                 own(feat),
                 own(2 * feat),
                 pl.BlockSpec((1, feat), lambda i, hk: (0, 0)),
@@ -417,7 +383,7 @@
             bytes_accessed=tokens * feat * 10 + feat * feat * 6,
             transcendentals=tokens * 256 * HEADS,
         ),
-    )(half_keep, edges[0], edges[1], q, kv_own, gain_row, w_qkv)
+    )(half_keep, *edges, q, kv_own, gain_row, w_qkv)
 
 
 def direct_parts(recv, tok_ref, tiles, wanted, cap):
@@ -434,17 +400,17 @@
 
 
 def relay_parts(recv, tok_ref, tiles, wanted, cap):
-    near, first, second, x_same, x_cross, y_same, y_cross, rest = recv
+    near, whole, x_same, x_cross, y_same, y_cross, rest = recv[0], recv[1:5], *recv[5:]
     cut = tok_ref.shape[1] // 2
     wide = tok_ref.shape[2]
     deep = tok_ref.shape[1]
-    at = lambda ref, j: ref.at[j // wide, :, j % wide]
+    same = lambda k, j: [(True, whole[k].at[:, j % wide]), (False, whole[k + 2].at[:, j % wide])]
     table = {
         0: lambda j, seen: (tok_ref.at[j // wide, :cut, j % wide], tok_ref.at[j // wide, cut:, j % wide]),
         1: lambda j, seen: (near.at[deep + seen[1], :cut], near.at[deep + seen[1], cut:]),
-        2: lambda j, seen: (at(first, j), x_same.at[seen[2] + seen[6]]),
+        2: lambda j, seen: (same(0, j), x_same.at[seen[2] + seen[6]]),
         3: lambda j, seen: (rest.at[seen[3]], x_cross.at[seen[3] + seen[7]]),
-        4: lambda j, seen: (y_same.at[seen[4] + seen[6]], at(second, j)),
+        4: lambda j, seen: (y_same.at[seen[4] + seen[6]], same(1, j)),
         5: lambda j, seen: (y_cross.at[seen[5] + seen[7]], rest.at[cap + seen[5]]),
         6: lambda j, seen: (y_same.at[seen[4] + seen[6]], x_same.at[seen[2] + seen[6]]),
         7: lambda j, seen: (y_cross.at[seen[5] + seen[7]], x_cross.at[seen[3] + seen[7]]),
@@ -478,9 +444,15 @@
 
                 @pl.when(r == k)
                 def _(pick=pick):
-                    top, bottom = pick(j, seen)
-                    pltpu.make_async_copy(top, got.at[count, :cut], sems.at[0, count]).start()
-                    pltpu.make_async_copy(bottom, got.at[count, cut:], sems.at[4, count]).start()
+                    for ref, rows, k in zip(pick(j, seen), (slice(0, cut), slice(cut, deep)), (0, 4)):
+                        if not isinstance(ref, list):
+                            pltpu.make_async_copy(ref, got.at[count, rows], sems.at[k, count]).start()
+                            continue
+                        for mine, choice in ref:
+
+                            @pl.when((j // half == (me & 1)) == mine)
+                            def _(choice=choice, rows=rows, k=k):
+                                pltpu.make_async_copy(choice, got.at[count, rows], sems.at[k, count]).start()
 
             u = p // half
             w = p % half
@@ -674,35 +646,45 @@
         )
 
     if tiles == 8:
-        first, second = split_halves(tok)
-        first = xor(first, 2)
-        second = xor(second, 4)
-        near = xor(pack_near(me, tile_table, panel_table, tok, cap), 1)
+        fence = lax.optimization_barrier
+        odd = slab_index % 2
+        direct = jnp.logical_or(slab_index % 4 == 1, slab_index % 4 == 2).astype(jnp.int32)
+        near_half = jnp.stack([1 - odd, jnp.where(odd == 1, keep_before, keep_after), direct]).astype(jnp.int32)
+        far_half = jnp.stack([odd, jnp.where(odd == 1, keep_after, keep_before), direct]).astype(jnp.int32)
+        links_a, links_b, links_c = [], [], []
+        for low in range(1, slab_count - 1, 2):
+            links_a += [(low ^ 2, low + 1), ((low + 1) ^ 2, low)]
+            if low % 4 == 1:
+                links_b += [(low, low + 1), (low + 1, low)]
+            else:
+                links_c += [(low ^ 4, low + 1), ((low + 1) ^ 4, low)]
+
+        rim_x, rim_y, off_x, off_y = split_halves(me, tok)
+        own_rim = rim_y
+        rim_x, rim_y = xor(rim_x, 2), xor(rim_y, 4)
+        off_x, off_y = xor(off_x, 2), xor(off_y, 4)
         q, kv = project_own(tok, gain_row, w_qkv)
-        odd = slab_index % 2
-        near_half = jnp.stack([1 - odd, jnp.where(odd == 1, keep_before, keep_after)]).astype(jnp.int32)
-        far_half = jnp.stack([odd, jnp.where(odd == 1, keep_after, keep_before)]).astype(jnp.int32)
+        me_next, q = fence((me, q))
+        near = xor(pack_near(me_next, tile_table, panel_table, tok, cap), 1)
+        edge_b = lax.ppermute(own_rim, ("scene", "tile"), links_b)
         mix_near = window_mix(near_half, (near, near), (0, 1), q, kv, gain_row, w_qkv)
-        rim_a, rim_b = pack_rim(me, tok, first, second)
-        links_a, links_b = [], []
-        for low in range(1, slab_count - 1, 2):
-            held = (low, low + 1) if low % 4 == 1 else (low ^ 4, (low + 1) ^ 4)
-            links_a += [(low ^ 2, low + 1), ((low + 1) ^ 2, low)]
-            links_b += [(held[0], low + 1), (held[1], low)]
-        rim_a = lax.ppermute(rim_a, ("scene", "tile"), links_a)
-        rim_b = lax.ppermute(rim_b, ("scene", "tile"), links_b)
-        x_same, x_cross, y_same, y_cross, rest = pack_far(me, tile_table, panel_table, tok, first, second, cap)
-        rim_a, rim_b, x_same, y_same, rest = lax.optimization_barrier((rim_a, rim_b, x_same, y_same, rest))
-        x_same, y_same, rest = xor(x_same, 2), xor(y_same, 4), xor(rest, 1)
-        mix_far = window_mix(far_half, (rim_a, rim_b), (0, 0), q, kv, gain_row, w_qkv)
-        x_same, y_same, x_cross, y_cross = lax.optimization_barrier((x_same, y_same, x_cross, y_cross))
-        x_cross, y_cross = xor(x_cross, 3), xor(y_cross, 5)
+        rim_x, rim_y, mix_near = fence((rim_x, rim_y, mix_near))
+        edge_c = lax.ppermute(rim_y, ("scene", "tile"), links_c)
+        edge_a = lax.ppermute(rim_x, ("scene", "tile"), links_a)
+        off_x, off_y, mix_near = fence((off_x, off_y, mix_near))
+        sides = (rim_x, rim_y, off_x, off_y)
+        x_same, x_cross, y_same, y_cross, rest = pack_far(me, tile_table, panel_table, tok, sides, cap)
+        y_same, rest = xor(y_same, 4), xor(rest, 1)
+        edge_a, edge_b, edge_c, x_same, y_cross = fence((edge_a, edge_b, edge_c, x_same, y_cross))
+        x_same, y_cross = xor(x_same, 2), xor(y_cross, 5)
+        mix_far = window_mix(far_half, (edge_a, edge_b, edge_c), (0, 0, 0), q, kv, gain_row, w_qkv)
+        x_cross, mix_far = fence((x_cross, mix_far))
+        x_cross = xor(x_cross, 3)
         mixes = (mix_near, mix_far)
-        idle = rest
-        early = (near, first, second, x_same, idle, y_same, idle, idle)
-        late = (near, first, second, x_same, x_cross, y_same, y_cross, rest)
-        out = cross(relay_parts, 0b01010111, early, mixes, near_half, None)
-        out = cross(relay_parts, 0b10101000, late, mixes, near_half, out)
+        early = (near, *sides, x_same, rest, y_same, y_cross, rest)
+        late = (near, *sides, x_same, x_cross, y_same, y_cross, rest)
+        out = cross(relay_parts, 0b01110111, early, mixes, near_half, None)
+        out = cross(relay_parts, 0b10001000, late, mixes, near_half, out)
     else:
         forward = [(i, i + 1) for i in range(slab_count - 1)]
         backward = [(i + 1, i) for i in range(slab_count - 1)]

time: 196 us -> 201 us (1.026); the launches traced: 192 us -> 200 us
  waiting for transfers between devices: 54.1 us -> 58.6 us
    ppermute x8 -> x10, waiting for transfers between devices: 37.3 us -> 58.6 us  [xor(): return lax.ppermute(block, 'tile', [(i, i ^ bits) for i in range(tiles)])]
    ppermute x2 -> x3, waiting for transfers between devices: 16.7 us -> 0.01 us  [the longest x1 0.01 us: per_device(): edge_a = lax.ppermute(rim_x, ('scene', 'tile'), links_a)]
    pallas_call x2, Pallas kernels: 37.6 us -> 40.4 us  [cross_and_project(): pl.pallas_call(kernel, out_shape=jax.ShapeDtypeStruct(tok.shape, jnp.bflo...]
    pallas_call x1 -> x0, Pallas kernels: 2.59 us -> none  [pack_rim(): pl.pallas_call(rim_kernel, out_shape=[jax.ShapeDtypeStruct(first.shape[1:...]
    ppermute x8 -> x10, starting transfers between devices: 7.41 us -> 8.41 us  [xor(): return lax.ppermute(block, 'tile', [(i, i ^ bits) for i in range(tiles)])]
    unnamed x23 -> x21, local copies, waits for them, and re-layouts: 6.08 us -> 5.36 us
    ppermute x2 -> x3, starting transfers between devices: 7.73 us -> 7.83 us  [the longest x1 4.27 us: per_device(): edge_c = lax.ppermute(rim_y, ('scene', 'tile'), links_c)]
  transfers between devices with their start and end apart: 10 -> 13, of which waited for: 3 -> 4; matrix products, arithmetic and copies ran while one was open for 3% -> 1% of each run, Pallas kernels for 48% -> 38%
where the time goes in v5:
time: 201 us; the launch traced here: 200 us
  Pallas kernels  111 us (55%)
  waiting for transfers between devices  58.6 us (29%)
  starting transfers between devices  16.2 us (8%)
  local copies, waits for them, and re-layouts  9.23 us (5%)
  other arithmetic  2.61 us (1%)
    ppermute x10, waiting for transfers between devices, xor(): return lax.ppermute(block, 'tile', [(i, i ^ bits) for i in range(tiles)])  58.6 us
    pallas_call x2, Pallas kernels, cross_and_project(): pl.pallas_call(kernel, out_shape=jax.ShapeDtypeStruct(tok.shape, jnp.bflo...  40.4 us
    pallas_call x2, Pallas kernels, window_mix(): pl.pallas_call(functools.partial(window_kernel, head_width), out_shape=ja...  37.5 us
    pallas_call x1, Pallas kernels, project_own(): pl.pallas_call(qkv_kernel, grid=(halves * 2,), out_shape=[jax.ShapeDtypeS...  20.1 us
    ppermute x10, starting transfers between devices, xor(): return lax.ppermute(block, 'tile', [(i, i ^ bits) for i in range(tiles)])  8.41 us
    pallas_call x1, Pallas kernels, pack_far(): pl.pallas_call(functools.partial(far_kernel, cap), out_shape=[jax.ShapeDt...  5.76 us
    unnamed x21, local copies, waits for them, and re-layouts  5.36 us
    pallas_call x1, Pallas kernels, pack_near(): pl.pallas_call(functools.partial(near_kernel, cap), out_shape=jax.ShapeDt...  4.34 us
  transfers between devices with their start and end apart: 13, of which 4 were waited for; matrix products, arithmetic and copies ran while one was open for 1% of the time, Pallas kernels for 38%

profile of v5, /device:TPU:11, one launch (start us, length us, event | category | flops | bytes accessed | tf_op | source)
XLA Modules:
  0.0 199.8 jit_solution(5832620177311327236)
XLA Ops:
  0.0 1.3 reshape.27.panel_ref.refs_2_
  1.9 1.3 reduce.3
  3.8 1.3 reshape.30.gain_ref.refs_4_.refs_5_.refs_19_
  5.1 20.1 %shard_map.82 = (bf16[2,8,8,16,1024]{4,3,2,1,0:T(8,128)(2,1)}, bf16[2,8,8,16,2048]{4,3,2,1,0:T(8,128)(2,1)}) custom-call(bf16[2,8,8,16,1024]{4,3,2,1,0:T(8,128)(2,1)} %bitcast.12, bf16[1,1024]{1,0:T(2,128)(2,1)} %reshape.30.gain_ref.refs_4_.refs_5_.refs_19_, bf16[1024,3072]{1,0:T(8,128)(2,1)} %refs_20_.3), custom_call_target="tpu_custom_call" | custom-call | flops 12884901888 | bytes 23068672 | tf_op jit(solution)/shard_map/pallas_call | solution.py:290
  25.2 4.3 %shard_map.83 = bf16[12,8,16,1024]{3,2,1,0:T(8,128)(2,1)} custom-call(s32[1]{0:T(128)} %bitcast.me_ref.refs_0_, s32[128]{0:T(128)} %reshape.26.tile_ref.refs_1_, s32[128]{0:T(128)} %reshape.27.panel_ref.refs_2_, bf16[2,8,8,16,1024]{4,3,2,1,0:T(8,128)(2,1)} %bitcast.13), custom_call_target="tpu_custom_call" | custom-call | bytes 6291456 | tf_op jit(solution)/shard_map/pallas_call | solution.py:173
  29.6 1.1 collective-permute-start
  30.7 3.4 %shard_map.84 = (bf16[4,8,16,1024]{3,2,1,0:T(8,128)(2,1)}, bf16[4,8,16,1024]{3,2,1,0:T(8,128)(2,1)}, bf16[4,8,16,1024]{3,2,1,0:T(8,128)(2,1)}, bf16[4,8,16,1024]{3,2,1,0:T(8,128)(2,1)}) custom-call(s32[1]{0:T(128)} %bitcast.me_ref.refs_0_, bf16[2,8,8,16,1024]{4,3,2,1,0:T(8,128)(2,1)} %bitcast.14), custom_call_target="tpu_custom_call" | custom-call | bytes 8388608 | tf_op jit(solution)/shard_map/pallas_call | solution.py:126
  34.1 1.2 collective-permute-start.2
  35.3 1.6 collective-permute-start.6
  37.0 2.3 %collective-permute-start.3 = (bf16[4,8,16,1024]{3,2,1,0:T(8,128)(2,1)}, bf16[4,8,16,1024]{3,2,1,0:T(8,128)(2,1)}, u32[]{:S(2)}, u32[]{:S(2)}) collective-permute-start(bf16[4,8,16,1024]{3,2,1,0:T(8,128)(2,1)} %get-tuple-element.39), channel_id=1, source_target_pairs={{0,2},{1,3},{2,0},{3,1},{4,6},{5,7},{6,4},{7,5},{8,10},{9,11},{10,... | collective-permute-start | bytes 3145736 | tf_op jit(solution)/shard_map/ppermute | solution.py:625
  42.0 1.5 copy-done
  43.5 18.6 %shard_map.85.refs_17_ = bf16[8,8,16,1024]{3,2,1,0:T(8,128)(2,1)} custom-call(s32[3]{0:T(128)} %add_add_fusion.half_ref.refs_4_, bf16[12,8,16,1024]{3,2,1,0:T(8,128)(2,1)} %copy-done, bf16[12,8,16,1024]{3,2,1,0:T(8,128)(2,1)} %copy-done, bf16[2,8,8,16,1024]{4,3,2,1,0:T(8,128)(2,1)} %get-tuple-element.35.refs_2_.refs_3_.refs_16_, ...), custom_call_target="tpu_custom_call" | custom-call | flops 6442450944 | bytes 16777216 | tf_op jit(solution)/shard_map/pallas_call | solution.py:364
  62.1 1.9 collective-permute-start.5
  64.0 4.3 %collective-permute-start.7 = (bf16[4,8,16,1024]{3,2,1,0:T(8,128)(2,1)}, bf16[4,8,16,1024]{3,2,1,0:T(8,128)(2,1)S(1)}, u32[]{:S(2)}, u32[]{:S(2)}) collective-permute-start(bf16[4,8,16,1024]{3,2,1,0:T(8,128)(2,1)} %collective-permute-done.2.rest_1_.refs_8_), channel_id=1, source_target_pairs={{7,4},{0,3},{3,8},{12,7},{15,12},{8,11},{11,16},{20,15},{23,20},{1... | collective-permute-start | bytes 3145736 | tf_op jit(solution)/shard_map/ppermute | solution.py:672
  68.3 35.6 %collective-permute-done.3.rest_2_.refs_9_ = bf16[4,8,16,1024]{3,2,1,0:T(8,128)(2,1)} collective-permute-done((bf16[4,8,16,1024]{3,2,1,0:T(8,128)(2,1)}, bf16[4,8,16,1024]{3,2,1,0:T(8,128)(2,1)}, u32[]{:S(2)}, u32[]{:S(2)}) %collective-permute-start.3) | collective-permute-done | bytes 1048608 | tf_op jit(solution)/shard_map/ppermute | solution.py:625
  103.8 1.0 copy-done.1
  104.9 5.8 %shard_map.86 = (bf16[8,4,16,1024]{3,2,1,0:T(8,128)(2,1)}, bf16[8,4,16,1024]{3,2,1,0:T(8,128)(2,1)}, bf16[8,4,16,1024]{3,2,1,0:T(8,128)(2,1)}, bf16[8,4,16,1024]{3,2,1,0:T(8,128)(2,1)}, bf16[8,4,16,1024]{3,2,1,0:T(8,128)(2,1)}) custom-call(s32[1]{0:T(128)} %bitcast.me_ref.refs_0_, s32[128]{0:T(128)} %reshape.26.tile_ref.refs_1_, ...), custom_call_target="tpu_custom_call" | custom-call | bytes 14680064 | tf_op jit(solution)/shard_map/pallas_call | solution.py:260
  110.6 1.5 collective-permute-start.10
  113.5 1.2 collective-permute-start.8
  115.9 18.9 %shard_map.87.refs_18_ = bf16[8,8,16,1024]{3,2,1,0:T(8,128)(2,1)} custom-call(s32[3]{0:T(128)} %add_add_fusion.1.half_ref, bf16[4,8,16,1024]{3,2,1,0:T(8,128)(2,1)} %copy-done.5, bf16[4,8,16,1024]{3,2,1,0:T(8,128)(2,1)} %collective-permute-done.6.refs_1_, bf16[4,8,16,1024]{3,2,1,0:T(8,128)(2,1)} %copy-done.6, ...), custom_call_target="tpu_custom_call" | custom-call | flops 6442450944 | bytes 16777216 | tf_op jit(solution)/shard_map/pallas_call | solution.py:364
  136.1 1.9 collective-permute-done.8.refs_11_
  138.0 20.2 %collective-permute-done.11.refs_14_ = bf16[8,4,16,1024]{3,2,1,0:T(8,128)(2,1)} collective-permute-done((bf16[8,4,16,1024]{3,2,1,0:T(8,128)(2,1)}, bf16[8,4,16,1024]{3,2,1,0:T(8,128)(2,1)}, u32[]{:S(2)}, u32[]{:S(2)}) %collective-permute-start.11) | collective-permute-done | bytes 1048608 | tf_op jit(solution)/shard_map/ppermute | solution.py:625
  158.1 28.7 %shard_map.88.refs_22_ = bf16[2,8,8,16,1024]{4,3,2,1,0:T(8,128)(2,1)} custom-call(s32[1]{0:T(128)} %bitcast.me_ref.refs_0_, s32[128]{0:T(128)} %reshape.26.tile_ref.refs_1_, s32[128]{0:T(128)} %reshape.27.panel_ref.refs_2_, s32[16]{0:T(128)} %bitcast.18, s32[3]{0:T(128)} %add_add_fusion.half_ref.refs_4_, bf16[2,8,8,16,1024]{4,3,2,1,0:T(8,128)(2,1)} %bitcast.16, ...), custom_call_target="tpu_custom_call" | custom-call | flops 11274289152 | bytes 18874368 | tf_op jit(solution)/shard_map/pallas_call | solution.py:574
  187.9 11.7 %shard_map.89 = bf16[2,8,8,16,1024]{4,3,2,1,0:T(8,128)(2,1)} custom-call(s32[1]{0:T(128)} %bitcast.me_ref.refs_0_, s32[128]{0:T(128)} %reshape.26.tile_ref.refs_1_, s32[128]{0:T(128)} %reshape.27.panel_ref.refs_2_, s32[16]{0:T(128)} %bitcast.19, s32[3]{0:T(128)} %add_add_fusion.half_ref.refs_4_, ...), custom_call_target="tpu_custom_call", output_to_operand_aliasing={{}: (22, {})} | custom-call | flops 3758096384 | bytes 10485760 | tf_op jit(solution)/shard_map/pallas_call | solution.py:574
  (38 shorter events, 7.5 us)
Async XLA Ops:
  25.2 14.0 %copy-start.8 = (s32[32]{0:T(128)S(1)}, s32[32]{0:T(128)}, u32[]{:S(2)}) copy-start(s32[32]{0:T(128)} %param.12) | copy-start | bytes 388
  29.6 12.3 %collective-permute-start = (bf16[12,8,16,1024]{3,2,1,0:T(8,128)(2,1)}, bf16[12,8,16,1024]{3,2,1,0:T(8,128)(2,1)S(1)}, u32[]{:S(2)}, u32[]{:S(2)}) collective-permute-start(bf16[12,8,16,1024]{3,2,1,0:T(8,128)(2,1)} %shard_map.83), channel_id=1, source_target_pairs={{0,1},{1,0},{2,3},{3,2},{4,5},{5,4},{6,7},{7,6},{8,9},{9,8},{10,11... | collective-permute-start | bytes 9437192 | tf_op jit(solution)/shard_map/ppermute | solution.py:625
  34.0 28.0 %collective-permute-start.1 = (bf16[4,8,16,1024]{3,2,1,0:T(8,128)(2,1)}, bf16[4,8,16,1024]{3,2,1,0:T(8,128)(2,1)}, u32[]{:S(2)}, u32[]{:S(2)}) collective-permute-start(bf16[4,8,16,1024]{3,2,1,0:T(8,128)(2,1)} %get-tuple-element.33), channel_id=1, source_target_pairs={{0,2},{1,3},{2,0},{3,1},{4,6},{5,7},{6,4},{7,5},{8,10},{9,11},{10,... | collective-permute-start | bytes 3145736 | tf_op jit(solution)/shard_map/ppermute | solution.py:625
  34.1 27.9 %collective-permute-start.2 = (bf16[4,8,16,1024]{3,2,1,0:T(8,128)(2,1)}, bf16[4,8,16,1024]{3,2,1,0:T(8,128)(2,1)}, u32[]{:S(2)}, u32[]{:S(2)}) collective-permute-start(bf16[4,8,16,1024]{3,2,1,0:T(8,128)(2,1)} %get-tuple-element.34), channel_id=1, source_target_pairs={{0,4},{1,5},{2,6},{3,7},{4,0},{5,1},{6,2},{7,3},{8,12},{9,13},{10,... | collective-permute-start | bytes 3145736 | tf_op jit(solution)/shard_map/ppermute | solution.py:625
  35.3 76.8 %collective-permute-start.6 = (bf16[4,8,16,1024]{3,2,1,0:T(8,128)(2,1)}, bf16[4,8,16,1024]{3,2,1,0:T(8,128)(2,1)}, u32[]{:S(2)}, u32[]{:S(2)}) collective-permute-start(bf16[4,8,16,1024]{3,2,1,0:T(8,128)(2,1)} %get-tuple-element.34), channel_id=1, source_target_pairs={{1,2},{2,1},{5,6},{6,5},{9,10},{10,9},{13,14},{14,13},{17,18},{18,... | collective-permute-start | bytes 3145736 | tf_op jit(solution)/shard_map/ppermute | solution.py:669
  37.0 66.9 %collective-permute-start.3 = (bf16[4,8,16,1024]{3,2,1,0:T(8,128)(2,1)}, bf16[4,8,16,1024]{3,2,1,0:T(8,128)(2,1)}, u32[]{:S(2)}, u32[]{:S(2)}) collective-permute-start(bf16[4,8,16,1024]{3,2,1,0:T(8,128)(2,1)} %get-tuple-element.39), channel_id=1, source_target_pairs={{0,2},{1,3},{2,0},{3,1},{4,6},{5,7},{6,4},{7,5},{8,10},{9,11},{10,... | collective-permute-start | bytes 3145736 | tf_op jit(solution)/shard_map/ppermute | solution.py:625
  41.9 1.7 copy-start
  41.9 62.0 %collective-permute-start.4 = (bf16[4,8,16,1024]{3,2,1,0:T(8,128)(2,1)}, bf16[4,8,16,1024]{3,2,1,0:T(8,128)(2,1)S(1)}, u32[]{:S(2)}, u32[]{:S(2)}) collective-permute-start(bf16[4,8,16,1024]{3,2,1,0:T(8,128)(2,1)} %get-tuple-element.40), channel_id=1, source_target_pairs={{0,4},{1,5},{2,6},{3,7},{4,0},{5,1},{6,2},{7,3},{8,12},{9,13},{10,... | collective-permute-start | bytes 3145736 | tf_op jit(solution)/shard_map/ppermute | solution.py:625
  62.1 50.0 %collective-permute-start.5 = (bf16[4,8,16,1024]{3,2,1,0:T(8,128)(2,1)}, bf16[4,8,16,1024]{3,2,1,0:T(8,128)(2,1)S(1)}, u32[]{:S(2)}, u32[]{:S(2)}) collective-permute-start(bf16[4,8,16,1024]{3,2,1,0:T(8,128)(2,1)} %collective-permute-done.1.rest_0_.refs_7_), channel_id=1, source_target_pairs={{3,2},{0,1},{1,4},{6,3},{7,6},{4,5},{5,8},{10,7},{11,10},{8,9},{9,... | collective-permute-start | bytes 3145736 | tf_op jit(solution)/shard_map/ppermute | solution.py:673
  64.0 48.1 %collective-permute-start.7 = (bf16[4,8,16,1024]{3,2,1,0:T(8,128)(2,1)}, bf16[4,8,16,1024]{3,2,1,0:T(8,128)(2,1)S(1)}, u32[]{:S(2)}, u32[]{:S(2)}) collective-permute-start(bf16[4,8,16,1024]{3,2,1,0:T(8,128)(2,1)} %collective-permute-done.2.rest_1_.refs_8_), channel_id=1, source_target_pairs={{7,4},{0,3},{3,8},{12,7},{15,12},{8,11},{11,16},{20,15},{23,20},{1... | collective-permute-start | bytes 3145736 | tf_op jit(solution)/shard_map/ppermute | solution.py:672
  103.8 1.0 copy-start.1
  110.6 25.5 %collective-permute-start.10 = (bf16[8,4,16,1024]{3,2,1,0:T(8,128)(2,1)}, bf16[8,4,16,1024]{3,2,1,0:T(8,128)(2,1)S(1)}, u32[]{:S(2)}, u32[]{:S(2)}) collective-permute-start(bf16[8,4,16,1024]{3,2,1,0:T(8,128)(2,1)} %get-tuple-element.52), channel_id=1, source_target_pairs={{0,4},{1,5},{2,6},{3,7},{4,0},{5,1},{6,2},{7,3},{8,12},{9,13},{10,... | collective-permute-start | bytes 3145736 | tf_op jit(solution)/shard_map/ppermute | solution.py:625
  112.1 24.0 %collective-permute-start.12 = (bf16[8,4,16,1024]{3,2,1,0:T(8,128)(2,1)}, bf16[8,4,16,1024]{3,2,1,0:T(8,128)(2,1)S(1)}, u32[]{:S(2)}, u32[]{:S(2)}) collective-permute-start(bf16[8,4,16,1024]{3,2,1,0:T(8,128)(2,1)} %get-tuple-element.54), channel_id=1, source_target_pairs={{0,1},{1,0},{2,3},{3,2},{4,5},{5,4},{6,7},{7,6},{8,9},{9,8},{10,11... | collective-permute-start | bytes 3145736 | tf_op jit(solution)/shard_map/ppermute | solution.py:625
  112.1 1.0 copy-start.5
  112.1 1.3 copy-start.6
  113.5 24.5 %collective-permute-start.8 = (bf16[8,4,16,1024]{3,2,1,0:T(8,128)(2,1)}, bf16[8,4,16,1024]{3,2,1,0:T(8,128)(2,1)S(1)}, u32[]{:S(2)}, u32[]{:S(2)}) collective-permute-start(bf16[8,4,16,1024]{3,2,1,0:T(8,128)(2,1)} %get-tuple-element.46), channel_id=1, source_target_pairs={{0,2},{1,3},{2,0},{3,1},{4,6},{5,7},{6,4},{7,5},{8,10},{9,11},{10,... | collective-permute-start | bytes 3145736 | tf_op jit(solution)/shard_map/ppermute | solution.py:625
  114.7 43.5 %collective-permute-start.11 = (bf16[8,4,16,1024]{3,2,1,0:T(8,128)(2,1)}, bf16[8,4,16,1024]{3,2,1,0:T(8,128)(2,1)}, u32[]{:S(2)}, u32[]{:S(2)}) collective-permute-start(bf16[8,4,16,1024]{3,2,1,0:T(8,128)(2,1)} %get-tuple-element.53), channel_id=1, source_target_pairs={{0,5},{1,4},{2,7},{3,6},{4,1},{5,0},{6,3},{7,2},{8,13},{9,12},{10,... | collective-permute-start | bytes 3145736 | tf_op jit(solution)/shard_map/ppermute | solution.py:625
  115.9 18.9 %copy-start.9 = (bf16[8,4,16,1024]{3,2,1,0:T(8,128)(2,1)S(1)}, bf16[8,4,16,1024]{3,2,1,0:T(8,128)(2,1)}, u32[]{:S(2)}) copy-start(bf16[8,4,16,1024]{3,2,1,0:T(8,128)(2,1)} %get-tuple-element.51) | copy-start | bytes 3145732
  134.8 52.1 %collective-permute-start.9 = (bf16[8,4,16,1024]{3,2,1,0:T(8,128)(2,1)S(1)}, bf16[8,4,16,1024]{3,2,1,0:T(8,128)(2,1)S(1)}, u32[]{:S(2)}, u32[]{:S(2)}) collective-permute-start(bf16[8,4,16,1024]{3,2,1,0:T(8,128)(2,1)S(1)} %copy-done.9), channel_id=1, source_target_pairs={{0,3},{1,2},{2,1},{3,0},{4,7},{5,6},{6,5},{7,4},{8,11},{9,10},{10,... | collective-permute-start | bytes 3145736 | tf_op jit(solution)/shard_map/ppermute | solution.py:625
  136.1 22.1 %copy-start.2 = (bf16[8,4,16,1024]{3,2,1,0:T(8,128)(2,1)}, bf16[8,4,16,1024]{3,2,1,0:T(8,128)(2,1)S(1)}, u32[]{:S(2)}) copy-start(bf16[8,4,16,1024]{3,2,1,0:T(8,128)(2,1)S(1)} %collective-permute-done.10.refs_13_) | copy-start | bytes 3145732
  136.1 22.1 %copy-start.3 = (bf16[8,4,16,1024]{3,2,1,0:T(8,128)(2,1)}, bf16[8,4,16,1024]{3,2,1,0:T(8,128)(2,1)S(1)}, u32[]{:S(2)}) copy-start(bf16[8,4,16,1024]{3,2,1,0:T(8,128)(2,1)S(1)} %collective-permute-done.12.refs_12_.refs_15_) | copy-start | bytes 3145732
  138.0 20.2 %copy-start.4 = (bf16[8,4,16,1024]{3,2,1,0:T(8,128)(2,1)}, bf16[8,4,16,1024]{3,2,1,0:T(8,128)(2,1)S(1)}, u32[]{:S(2)}) copy-start(bf16[8,4,16,1024]{3,2,1,0:T(8,128)(2,1)S(1)} %collective-permute-done.8.refs_11_) | copy-start | bytes 3145732
  186.9 1.0 copy-start.7

commit v6 on v5

--- a/solution.py
+++ b/solution.py
@@ -41,9 +41,9 @@
     return lax.broadcasted_iota(jnp.int32, (rows, width), 1) < head_width
 
 
-def pack_kernel(tiles, panels, cap, me_ref, tile_ref, panel_ref, tok_ref, *rest):
+def pack_kernel(tiles, panels, cap, tile_ref, panel_ref, tok_ref, *rest):
     outs, slab, sem, sems = rest[: tiles - 1], rest[tiles - 1], rest[tiles], rest[tiles + 1]
-    me = me_ref[0]
+    me = lax.axis_index("tile")
     load = pltpu.make_async_copy(tok_ref, slab, sem)
     load.start()
     load.wait()
@@ -53,11 +53,11 @@
         out = outs[r - 1]
 
         def body(p, count, asker=asker, out=out, r=r):
-            hit = jnp.logical_and(tile_ref[asker * panels + p] == me, count < cap)
+            hit = jnp.logical_and(tile_ref[0, asker, p] == me, count < cap)
 
             @pl.when(hit)
             def _():
-                j = panel_ref[asker * panels + p]
+                j = panel_ref[0, asker, p]
                 pltpu.make_async_copy(
                     slab.at[j // (panels // 2), :, j % (panels // 2)], out.at[count], sems.at[r, count]
                 ).start()
@@ -73,7 +73,7 @@
                 pltpu.make_async_copy(slab.at[0, :, 0], outs[r - 1].at[c], sems.at[r, c]).wait()
 
 
-def pack(me, tile_table, panel_table, tok, tiles, cap):
+def pack(tile_table, panel_table, tok, tiles, cap):
     panels = 2 * tok.shape[2]
     block = (cap, tok.shape[1], tok.shape[3], tok.shape[4])
     smem = pl.BlockSpec(memory_space=pltpu.SMEM)
@@ -81,7 +81,7 @@
     return pl.pallas_call(
         functools.partial(pack_kernel, tiles, panels, cap),
         out_shape=[jax.ShapeDtypeStruct(block, tok.dtype)] * (tiles - 1),
-        in_specs=[smem, smem, smem, anym],
+        in_specs=[smem, smem, anym],
         out_specs=[anym] * (tiles - 1),
         scratch_shapes=[
             pltpu.VMEM(tok.shape, tok.dtype),
@@ -89,7 +89,7 @@
             pltpu.SemaphoreType.DMA((tiles, cap)),
         ],
         cost_estimate=pl.CostEstimate(flops=0, bytes_accessed=16 << 20, transcendentals=0),
-    )(me, tile_table, panel_table, tok)
+    )(tile_table, panel_table, tok)
 
 
 def copy_through(pairs, bounce, sems):
@@ -106,10 +106,10 @@
         store.wait()
 
 
-def halves_kernel(me_ref, tok_ref, *rest):
+def halves_kernel(tok_ref, *rest):
     outs, bounce, sems = rest[:4], rest[4], rest[5]
     deep = outs[0].shape[0]
-    part = me_ref[0] & 1
+    part = lax.axis_index("tile") & 1
     sources = [
         tok_ref.at[part, :deep],
         tok_ref.at[part, deep:],
@@ -119,158 +119,102 @@
     copy_through(list(zip(sources, outs)), bounce, sems)
 
 
-def split_halves(me, tok):
+def split_halves(tok):
     halves, deep, wide, run, feat = tok.shape
     part = (deep // 2, wide, run, feat)
     anym = pl.BlockSpec(memory_space=pl.ANY)
     return pl.pallas_call(
         halves_kernel,
         out_shape=[jax.ShapeDtypeStruct(part, tok.dtype)] * 4,
-        in_specs=[pl.BlockSpec(memory_space=pltpu.SMEM), anym],
+        in_specs=[anym],
         out_specs=[anym] * 4,
         scratch_shapes=[pltpu.VMEM((4,) + part, tok.dtype), pltpu.SemaphoreType.DMA((2, 4))],
         cost_estimate=pl.CostEstimate(flops=0, bytes_accessed=8 << 20, transcendentals=0),
-    )(me, tok)
-
-
-def near_kernel(cap, me_ref, tile_ref, panel_ref, tok_ref, out_ref, bounce, sems, slots, slot_sems):
-    halves, deep, wide, run, feat = tok_ref.shape
-    panels = halves * wide
-    me = me_ref[0]
-    asker = me ^ 1
-    part = 1 - (me & 1)
-
-    def body(p, count):
-        hit = jnp.logical_and(tile_ref[asker * panels + p] == me, count < cap)
-
-        @pl.when(hit)
-        def _():
-            j = panel_ref[asker * panels + p]
-            pltpu.make_async_copy(tok_ref.at[j // wide, :, j % wide], slots.at[count], slot_sems.at[0, count]).start()
-
-        return count + hit.astype(jnp.int32)
-
-    total = lax.fori_loop(0, panels, body, jnp.int32(0))
-    copy_through([(tok_ref.at[part, 2 * k : 2 * k + 2], out_ref.at[2 * k : 2 * k + 2]) for k in range(deep // 2)], bounce, sems)
-    for c in range(cap):
-
-        @pl.when(c < total)
-        def _(c=c):
-            pltpu.make_async_copy(tok_ref.at[0, :, 0], slots.at[c], slot_sems.at[0, c]).wait()
-            pltpu.make_async_copy(slots.at[c], out_ref.at[deep + c], slot_sems.at[1, c]).start()
-
-    for c in range(cap):
-
-        @pl.when(c < total)
-        def _(c=c):
-            pltpu.make_async_copy(slots.at[c], out_ref.at[deep + c], slot_sems.at[1, c]).wait()
-
-
-def pack_near(me, tile_table, panel_table, tok, cap):
-    halves, deep, wide, run, feat = tok.shape
-    smem = pl.BlockSpec(memory_space=pltpu.SMEM)
-    anym = pl.BlockSpec(memory_space=pl.ANY)
-    return pl.pallas_call(
-        functools.partial(near_kernel, cap),
-        out_shape=jax.ShapeDtypeStruct((deep + cap, wide, run, feat), tok.dtype),
-        in_specs=[smem, smem, smem, anym],
-        out_specs=anym,
-        scratch_shapes=[
-            pltpu.VMEM((deep // 2, 2, wide, run, feat), tok.dtype),
-            pltpu.SemaphoreType.DMA((2, deep // 2)),
-            pltpu.VMEM((cap, deep, run, feat), tok.dtype),
-            pltpu.SemaphoreType.DMA((2, cap)),
-        ],
-        cost_estimate=pl.CostEstimate(flops=0, bytes_accessed=6 << 20, transcendentals=0),
-    )(me, tile_table, panel_table, tok)
-
-
-def far_kernel(cap, me_ref, tile_ref, panel_ref, tok_ref, *rest):
-    sides, outs, slab, got, sem, sems = rest[:4], rest[4:9], *rest[9:]
+    )(tok)
+
+
+def far_kernel(cap, tile_ref, panel_ref, tok_ref, *rest):
+    sides, outs, stage, in_sems, out_sems = rest[:4], rest[4:9], *rest[9:]
     halves, deep, wide, run, feat = tok_ref.shape
     panels = halves * wide
     cut = deep // 2
-    me = me_ref[0]
+    me = lax.axis_index("tile")
     part = me & 1
-    loads = [pltpu.make_async_copy(tok_ref, slab, sem.at[4])]
+
+    def bring(cond, ref, k, spot):
+        @pl.when(cond)
+        def _():
+            pltpu.make_async_copy(ref, stage.at[k, spot], in_sems.at[k, spot]).start()
+
+    def bring_side(cond, axis, j, k, spot):
+        aligned = j // wide == part
+        bring(jnp.logical_and(cond, aligned), sides[axis].at[:, j % wide], k, spot)
+        bring(jnp.logical_and(cond, jnp.logical_not(aligned)), sides[2 + axis].at[:, j % wide], k, spot)
+
+    totals = []
+    for k, (bits, relay) in enumerate(((2, 4), (4, 2), (3, 4), (5, 2))):
+        asker = me ^ bits
+        axis, rows = (1, slice(cut, deep)) if relay == 4 else (0, slice(0, cut))
+
+        def body(p, count, k=k, asker=asker, relay=relay, axis=axis, rows=rows):
+            named = tile_ref[0, asker, p]
+            own = jnp.logical_and(named == me, count < 2 * cap)
+            other = jnp.logical_and(named == me ^ relay, count < 2 * cap)
+            j = panel_ref[0, asker, p]
+            bring(own, tok_ref.at[j // wide, rows, j % wide], k, count)
+            bring_side(other, axis, j, k, count)
+            return count + jnp.logical_or(own, other).astype(jnp.int32)
+
+        totals.append(lax.fori_loop(0, panels, body, jnp.int32(0)))
+
+    def near(p, counts):
+        named = tile_ref[0, me ^ 1, p]
+        j = panel_ref[0, me ^ 1, p]
+        hits = [jnp.logical_and(named == me ^ relay, counts[k] < cap) for k, relay in enumerate((2, 4, 0))]
+        for k in range(2):
+            bring_side(hits[k], k, j, 4, k * cap + counts[k])
+        bring(hits[2], tok_ref.at[j // wide, :cut, j % wide], 4, 2 * cap + counts[2])
+        bring(hits[2], tok_ref.at[j // wide, cut:, j % wide], 4, 3 * cap + counts[2])
+        return tuple(count + hit.astype(jnp.int32) for count, hit in zip(counts, hits))
+
+    near_totals = lax.fori_loop(0, panels, near, (jnp.int32(0),) * 3)
+    used = []
     for k in range(4):
-        u = part if k < 2 else 1 - part
-        loads.append(pltpu.make_async_copy(sides[k], got.at[k % 2, u], sem.at[k]))
-    for load in loads:
-        load.start()
-    for load in loads:
-        load.wait()
-    totals = []
-    for k, (bits, relay) in enumerate(((2, 4), (3, 4), (4, 2), (5, 2))):
-        asker = me ^ bits
-        buffer, rows = (1, slice(cut, deep)) if relay == 4 else (0, slice(0, cut))
-
-        def body(p, count, k=k, asker=asker, relay=relay, buffer=buffer, rows=rows):
-            named = tile_ref[asker * panels + p]
-            own = named == me
-            hit = jnp.logical_and(jnp.logical_or(own, named == me ^ relay), count < 2 * cap)
-            j = panel_ref[asker * panels + p]
-
-            @pl.when(jnp.logical_and(hit, own))
-            def _():
-                pltpu.make_async_copy(slab.at[j // wide, rows, j % wide], outs[k].at[count], sems.at[k, count]).start()
-
-            @pl.when(jnp.logical_and(hit, jnp.logical_not(own)))
-            def _():
-                pltpu.make_async_copy(
-                    got.at[buffer, j // wide, :, j % wide], outs[k].at[count], sems.at[k, count]
-                ).start()
-
-            return count + hit.astype(jnp.int32)
-
-        totals.append(lax.fori_loop(0, panels, body, jnp.int32(0)))
-
-    asker = me ^ 1
-
-    def near(p, counts):
-        named = tile_ref[asker * panels + p]
-        j = panel_ref[asker * panels + p]
-        fresh = []
-        for k, relay in enumerate((2, 4)):
-            hit = jnp.logical_and(named == me ^ relay, counts[k] < cap)
-
-            @pl.when(hit)
-            def _(k=k):
-                spot = k * cap + counts[k]
-                pltpu.make_async_copy(got.at[k, j // wide, :, j % wide], outs[4].at[spot], sems.at[4, spot]).start()
-
-            fresh.append(counts[k] + hit.astype(jnp.int32))
-        return tuple(fresh)
-
-    near_totals = lax.fori_loop(0, panels, near, (jnp.int32(0), jnp.int32(0)))
-    for k in range(5):
-        for c in range(2 * cap):
-            used = c < totals[k] if k < 4 else c % cap < near_totals[c // cap]
-
-            @pl.when(used)
-            def _(k=k, c=c):
-                pltpu.make_async_copy(got.at[0, 0, :, 0], outs[k].at[c], sems.at[k, c]).wait()
-
-
-def pack_far(me, tile_table, panel_table, tok, sides, cap):
+        used += [(k, c, c < totals[k]) for c in range(2 * cap)]
+    used += [(4, c, c % cap < near_totals[min(c // cap, 2)]) for c in range(4 * cap)]
+    for k, c, cond in used:
+
+        @pl.when(cond)
+        def _(k=k, c=c):
+            pltpu.make_async_copy(sides[0].at[:, 0], stage.at[k, c], in_sems.at[k, c]).wait()
+            pltpu.make_async_copy(stage.at[k, c], outs[k].at[c], out_sems.at[k, c]).start()
+
+    for k, c, cond in used:
+
+        @pl.when(cond)
+        def _(k=k, c=c):
+            pltpu.make_async_copy(stage.at[k, c], outs[k].at[c], out_sems.at[k, c]).wait()
+
+
+def pack_far(tile_table, panel_table, tok, sides, cap):
     halves, deep, wide, run, feat = tok.shape
     smem = pl.BlockSpec(memory_space=pltpu.SMEM)
     anym = pl.BlockSpec(memory_space=pl.ANY)
     block = (2 * cap, deep // 2, run, feat)
     return pl.pallas_call(
         functools.partial(far_kernel, cap),
-        out_shape=[jax.ShapeDtypeStruct(block, tok.dtype)] * 5,
-        in_specs=[smem, smem, smem] + [anym] * 5,
+        out_shape=[jax.ShapeDtypeStruct(block, tok.dtype)] * 4
+        + [jax.ShapeDtypeStruct((4 * cap,) + block[1:], tok.dtype)],
+        in_specs=[smem, smem] + [anym] * 5,
         out_specs=[anym] * 5,
         scratch_shapes=[
-            pltpu.VMEM(tok.shape, tok.dtype),
-            pltpu.VMEM((2, halves, deep // 2, wide, run, feat), tok.dtype),
-            pltpu.SemaphoreType.DMA((5,)),
-            pltpu.SemaphoreType.DMA((5, 2 * cap)),
+            pltpu.VMEM((5, 4 * cap) + block[1:], tok.dtype),
+            pltpu.SemaphoreType.DMA((5, 4 * cap)),
+            pltpu.SemaphoreType.DMA((5, 4 * cap)),
         ],
         compiler_params=pltpu.CompilerParams(vmem_limit_bytes=VMEM_LIMIT),
-        cost_estimate=pl.CostEstimate(flops=0, bytes_accessed=14 << 20, transcendentals=0),
-    )(me, tile_table, panel_table, tok, *sides)
+        cost_estimate=pl.CostEstimate(flops=0, bytes_accessed=6 << 20, transcendentals=0),
+    )(tile_table, panel_table, tok, *sides)
 
 
 def qkv_kernel(tok_ref, gain_ref, w_ref, q_ref, kv_ref):
@@ -400,14 +344,13 @@
 
 
 def relay_parts(recv, tok_ref, tiles, wanted, cap):
-    near, whole, x_same, x_cross, y_same, y_cross, rest = recv[0], recv[1:5], *recv[5:]
+    whole, x_same, x_cross, y_same, y_cross, rest = recv[:4], *recv[4:]
     cut = tok_ref.shape[1] // 2
     wide = tok_ref.shape[2]
-    deep = tok_ref.shape[1]
     same = lambda k, j: [(True, whole[k].at[:, j % wide]), (False, whole[k + 2].at[:, j % wide])]
     table = {
         0: lambda j, seen: (tok_ref.at[j // wide, :cut, j % wide], tok_ref.at[j // wide, cut:, j % wide]),
-        1: lambda j, seen: (near.at[deep + seen[1], :cut], near.at[deep + seen[1], cut:]),
+        1: lambda j, seen: (rest.at[2 * cap + seen[1]], rest.at[3 * cap + seen[1]]),
         2: lambda j, seen: (same(0, j), x_same.at[seen[2] + seen[6]]),
         3: lambda j, seen: (rest.at[seen[3]], x_cross.at[seen[3] + seen[7]]),
         4: lambda j, seen: (y_same.at[seen[4] + seen[6]], same(1, j)),
@@ -419,27 +362,27 @@
 
 
 def cross_kernel(plan, tiles, head_width, wanted, recv_count, cap, refs):
-    me_ref, tile_ref, panel_ref, valid_ref, half_ref, tok_ref = refs[:6]
-    recv = refs[6 : 6 + recv_count]
-    q_ref, mix_a, mix_b, gain_ref, wqkv_ref, wproj_ref = refs[6 + recv_count : 12 + recv_count]
-    out_ref, got, q_s, own_s, res_s, wkv_s, wp_s, kv_s, mixed_s, seen, ids, w_sem, sems = refs[-13:]
+    tile_ref, panel_ref, valid_ref, half_ref, tok_ref = refs[:5]
+    recv = refs[5 : 5 + recv_count]
+    q_ref, mix_a, mix_b, gain_ref, wqkv_ref, wproj_ref = refs[5 + recv_count : 11 + recv_count]
+    out_ref, got, q_s, own_s, res_s, wkv_s, wp_s, normed_s, kv_s, mixed_s, seen, ids, w_sem, sems = refs[-14:]
     panels, deep, run, feat = got.shape
     half = panels // 2
     cut = deep // 2
     length = deep * run
-    me = me_ref[0]
+    me = lax.axis_index("tile")
     parts = plan(recv, tok_ref, tiles, wanted, cap)
     for t in range(tiles):
         seen[t] = 0
 
     def fetch(p, count):
-        r = tile_ref[me * panels + p] ^ me
+        r = tile_ref[0, me, p] ^ me
         hit = ((wanted >> r) & 1) == 1
 
         @pl.when(hit)
         def _():
             ids[count] = p
-            j = panel_ref[me * panels + p]
+            j = panel_ref[0, me, p]
             for k, pick in parts.items():
 
                 @pl.when(r == k)
@@ -474,8 +417,6 @@
     load_wkv.start()
     total = lax.fori_loop(0, panels, fetch, jnp.int32(0))
     load_wp.start()
-    load_wkv.wait()
-    load_wp.wait()
 
     pair = 2 * head_width
     scale = LOG2E * head_width ** (-0.5)
@@ -498,8 +439,18 @@
                     pltpu.make_async_copy(tok_ref.at[0, :, 0], place, sems.at[k, n_i]).wait()
 
         rows = got[pl.ds(first, 2)].reshape(2 * length, feat)
-        normed = layer_norm(rows, gain_ref[...])
-        kv_s[...] = dot_f32(normed, wkv_s[...]).astype(jnp.bfloat16)
+        normed_s[...] = layer_norm(rows, gain_ref[...])
+
+        @pl.when(n == 0)
+        def _():
+            load_wkv.wait()
+
+        kv_s[...] = dot_f32(normed_s[...], wkv_s[...]).astype(jnp.bfloat16)
+
+        @pl.when(n == 0)
+        def _():
+            load_wp.wait()
+
         gates = [valid_ref[ids[jnp.minimum(first + i, total - 1)]].astype(jnp.float32) for i in range(2)]
 
         def score(t):
@@ -541,6 +492,11 @@
 
     lax.fori_loop(0, (total + 1) // 2, unit, 0)
 
+    @pl.when(total == 0)
+    def _():
+        load_wkv.wait()
+        load_wp.wait()
+
     def finish(n, carry):
         pltpu.make_async_copy(res_s.at[n], out_ref.at[0, :, 0], sems.at[3, n]).wait()
         return carry
@@ -549,7 +505,7 @@
 
 
 def cross_and_project(
-    plan, wanted, tiles, cap, me, tile_table, panel_table, valid, half_keep, tok, recv, q, mixes, gain_row, w_qkv, w_proj, earlier
+    plan, wanted, tiles, cap, tile_table, panel_table, valid, half_keep, tok, recv, q, mixes, gain_row, w_qkv, w_proj, earlier
 ):
     halves, deep, wide, run, feat = tok.shape
     panels = halves * wide
@@ -560,8 +516,8 @@
     share = bin(wanted).count("1") / tiles
     tokens = int(panels * length * share)
     many = pltpu.VMEM((panels, deep, run, feat), jnp.bfloat16)
-    operands = [me, tile_table, panel_table, valid, half_keep, tok, *recv, q, *mixes, gain_row, w_qkv, w_proj]
-    specs = [smem] * 5 + [anym] * (len(recv) + 4) + [pl.BlockSpec((1, feat), lambda: (0, 0))] + [anym] * 2
+    operands = [tile_table, panel_table, valid, half_keep, tok, *recv, q, *mixes, gain_row, w_qkv, w_proj]
+    specs = [smem] * 4 + [anym] * (len(recv) + 4) + [pl.BlockSpec((1, feat), lambda: (0, 0))] + [anym] * 2
     aliases = {}
     if earlier is not None:
         aliases = {len(operands): 0}
@@ -583,6 +539,7 @@
             many,
             pltpu.VMEM((feat, 2 * feat), jnp.bfloat16),
             pltpu.VMEM((feat, feat), jnp.bfloat16),
+            pltpu.VMEM((2 * length, feat), jnp.bfloat16),
             pltpu.VMEM((2 * length, 2 * feat), jnp.bfloat16),
             pltpu.VMEM((2 * length, feat), jnp.bfloat16),
             pltpu.SMEM((tiles,), jnp.int32),
@@ -609,9 +566,8 @@
     panels = partner_tile.shape[2]
     cap = 2 * max(1, panels // tiles)
     slab_count = scene_first.shape[0]
-    me = lax.axis_index("tile").reshape(1).astype(jnp.int32)
-    tile_table = partner_tile.reshape(tiles * panels)
-    panel_table = partner_panel.reshape(tiles * panels)
+    tile_table = partner_tile[:, :, :, 0]
+    panel_table = partner_panel
     valid = window_valid.reshape(panels)
     gain_row = gain.reshape(1, feat)
     slab_index = lax.axis_index(("scene", "tile"))
@@ -630,7 +586,6 @@
             wanted,
             tiles,
             cap,
-            me,
             tile_table,
             panel_table,
             valid,
@@ -659,38 +614,37 @@
             else:
                 links_c += [(low ^ 4, low + 1), ((low + 1) ^ 4, low)]
 
-        rim_x, rim_y, off_x, off_y = split_halves(me, tok)
+        rim_x, rim_y, off_x, off_y = split_halves(tok)
+        rim_x, rim_y, off_x, off_y, gain_next = fence((rim_x, rim_y, off_x, off_y, gain_row))
+        near = (xor(off_x, 1), xor(off_y, 1))
         own_rim = rim_y
         rim_x, rim_y = xor(rim_x, 2), xor(rim_y, 4)
         off_x, off_y = xor(off_x, 2), xor(off_y, 4)
-        q, kv = project_own(tok, gain_row, w_qkv)
-        me_next, q = fence((me, q))
-        near = xor(pack_near(me_next, tile_table, panel_table, tok, cap), 1)
+        q, kv = project_own(tok, gain_next, w_qkv)
         edge_b = lax.ppermute(own_rim, ("scene", "tile"), links_b)
-        mix_near = window_mix(near_half, (near, near), (0, 1), q, kv, gain_row, w_qkv)
+        mix_near = window_mix(near_half, near, (0, 0), q, kv, gain_row, w_qkv)
         rim_x, rim_y, mix_near = fence((rim_x, rim_y, mix_near))
         edge_c = lax.ppermute(rim_y, ("scene", "tile"), links_c)
         edge_a = lax.ppermute(rim_x, ("scene", "tile"), links_a)
-        off_x, off_y, mix_near = fence((off_x, off_y, mix_near))
         sides = (rim_x, rim_y, off_x, off_y)
-        x_same, x_cross, y_same, y_cross, rest = pack_far(me, tile_table, panel_table, tok, sides, cap)
+        x_same, y_same, x_cross, y_cross, rest = pack_far(tile_table, panel_table, tok, sides, cap)
         y_same, rest = xor(y_same, 4), xor(rest, 1)
-        edge_a, edge_b, edge_c, x_same, y_cross = fence((edge_a, edge_b, edge_c, x_same, y_cross))
-        x_same, y_cross = xor(x_same, 2), xor(y_cross, 5)
+        edge_a, edge_b, edge_c, x_same, x_cross, y_cross = fence((edge_a, edge_b, edge_c, x_same, x_cross, y_cross))
+        x_same = xor(x_same, 2)
         mix_far = window_mix(far_half, (edge_a, edge_b, edge_c), (0, 0, 0), q, kv, gain_row, w_qkv)
-        x_cross, mix_far = fence((x_cross, mix_far))
-        x_cross = xor(x_cross, 3)
+        x_cross, y_cross, mix_far = fence((x_cross, y_cross, mix_far))
+        x_cross, y_cross = xor(x_cross, 3), xor(y_cross, 5)
         mixes = (mix_near, mix_far)
-        early = (near, *sides, x_same, rest, y_same, y_cross, rest)
-        late = (near, *sides, x_same, x_cross, y_same, y_cross, rest)
-        out = cross(relay_parts, 0b01110111, early, mixes, near_half, None)
-        out = cross(relay_parts, 0b10001000, late, mixes, near_half, out)
+        early = (*sides, x_same, rest, y_same, rest, rest)
+        late = (*sides, x_same, x_cross, y_same, y_cross, rest)
+        out = cross(relay_parts, 0b01010111, early, mixes, near_half, None)
+        out = cross(relay_parts, 0b10101000, late, mixes, near_half, out)
     else:
         forward = [(i, i + 1) for i in range(slab_count - 1)]
         backward = [(i + 1, i) for i in range(slab_count - 1)]
         before = lax.ppermute(tok[1], ("scene", "tile"), forward)
         after = lax.ppermute(tok[0], ("scene", "tile"), backward)
-        outgoing = pack(me, tile_table, panel_table, tok, tiles, cap)
+        outgoing = pack(tile_table, panel_table, tok, tiles, cap)
         recv = [xor(outgoing[r - 1], r) for r in range(1, tiles)]
         q, kv = project_own(tok, gain_row, w_qkv)
         zero = jnp.zeros((), jnp.int32)

time: 201 us -> 146 us (0.73)
  waiting for transfers between devices: 58.6 us -> 12.7 us
  Pallas kernels: 111 us -> 107 us
  local copies, waits for them, and re-layouts: 9.23 us -> 6.65 us
    ppermute x10 -> x11, waiting for transfers between devices: 58.6 us -> 4.54 us  [xor(): return lax.ppermute(block, 'tile', [(i, i ^ bits) for i in range(tiles)])]
    ppermute x1, waiting for transfers between devices: 0.01 us -> 5.7 us  [per_device(): edge_c = lax.ppermute(rim_y, ('scene', 'tile'), links_c)]
    pallas_call x1 -> x0, Pallas kernels: 4.34 us -> none  [pack_near(): pl.pallas_call(functools.partial(near_kernel, cap), out_shape=jax.ShapeDt...]
    ppermute x1, waiting for transfers between devices: 0.01 us -> 2.42 us  [per_device(): edge_a = lax.ppermute(rim_x, ('scene', 'tile'), links_a)]
    ppermute x10 -> x11, starting transfers between devices: 8.41 us -> 7.14 us  [xor(): return lax.ppermute(block, 'tile', [(i, i ^ bits) for i in range(tiles)])]
    unnamed x21 -> x20, local copies, waits for them, and re-layouts: 5.36 us -> 4.73 us
  transfers between devices with their start and end apart: 13 -> 14, of which waited for: 4 -> 4; matrix products, arithmetic and copies ran while one was open for 1% -> 1% of each run, Pallas kernels for 38% -> 61%
where the time goes in v6:
time: 146 us; the launch traced here: 145 us
  Pallas kernels  107 us (73%)
  starting transfers between devices  15.8 us (11%)
  waiting for transfers between devices  12.7 us (9%)
  local copies, waits for them, and re-layouts  6.65 us (5%)
  between operations  1.56 us (1%)
    pallas_call x2, Pallas kernels, cross_and_project(): pl.pallas_call(kernel, out_shape=jax.ShapeDtypeStruct(tok.shape, jnp.bflo...  39.8 us
    pallas_call x2, Pallas kernels, window_mix(): pl.pallas_call(functools.partial(window_kernel, head_width), out_shape=ja...  37.4 us
    pallas_call x1, Pallas kernels, project_own(): pl.pallas_call(qkv_kernel, grid=(halves * 2,), out_shape=[jax.ShapeDtypeS...  20.1 us
    ppermute x11, starting transfers between devices, xor(): return lax.ppermute(block, 'tile', [(i, i ^ bits) for i in range(tiles)])  7.14 us
    pallas_call x1, Pallas kernels, pack_far(): pl.pallas_call(functools.partial(far_kernel, cap), out_shape=[jax.ShapeDt...  5.88 us
    ppermute x1, waiting for transfers between devices, per_device(): edge_c = lax.ppermute(rim_y, ('scene', 'tile'), links_c)  5.7 us
    unnamed x20, local copies, waits for them, and re-layouts  4.73 us
    ppermute x11, waiting for transfers between devices, xor(): return lax.ppermute(block, 'tile', [(i, i ^ bits) for i in range(tiles)])  4.54 us
  transfers between devices with their start and end apart: 14, of which 4 were waited for; matrix products, arithmetic and copies ran while one was open for 1% of the time, Pallas kernels for 61%

profile of v6, /device:TPU:11, one launch (start us, length us, event | category | flops | bytes accessed | tf_op | source)
XLA Modules:
  0.0 144.5 jit_solution(8570806804863326192)
XLA Ops:
  0.0 1.3 reshape.18.gain_ref.refs_4_.refs_5_.refs_17_
  1.3 3.3 %shard_map.82 = (bf16[4,8,16,1024]{3,2,1,0:T(8,128)(2,1)}, bf16[4,8,16,1024]{3,2,1,0:T(8,128)(2,1)}, bf16[4,8,16,1024]{3,2,1,0:T(8,128)(2,1)}, bf16[4,8,16,1024]{3,2,1,0:T(8,128)(2,1)}) custom-call(bf16[2,8,8,16,1024]{4,3,2,1,0:T(8,128)(2,1)} %bitcast.11), custom_call_target="tpu_custom_call" | custom-call | bytes 8388608 | tf_op jit(solution)/shard_map/pallas_call | solution.py:126
  4.6 0.7 collective-permute-start.2
  5.6 1.2 collective-permute-start.5
  7.5 1.2 collective-permute-start
  9.1 20.1 %shard_map.83 = (bf16[2,8,8,16,1024]{4,3,2,1,0:T(8,128)(2,1)}, bf16[2,8,8,16,2048]{4,3,2,1,0:T(8,128)(2,1)}) custom-call(bf16[2,8,8,16,1024]{4,3,2,1,0:T(8,128)(2,1)} %bitcast.12, bf16[1,1024]{1,0:T(2,128)(2,1)} %reshape.18.gain_ref.refs_4_.refs_5_.refs_17_, bf16[1024,3072]{1,0:T(8,128)(2,1)} %refs_18_.3), custom_call_target="tpu_custom_call" | custom-call | flops 12884901888 | bytes 23068672 | tf_op jit(solution)/shard_map/pallas_call | solution.py:234
  31.1 0.7 add_add_fusion.half_ref.refs_3_
  31.8 1.6 %collective-permute-start.7 = (bf16[4,8,16,1024]{3,2,1,0:T(8,128)(2,1)}, bf16[4,8,16,1024]{3,2,1,0:T(8,128)(2,1)}, u32[]{:S(2)}, u32[]{:S(2)}) collective-permute-start(bf16[4,8,16,1024]{3,2,1,0:T(8,128)(2,1)} %get-tuple-element.38), channel_id=1, source_target_pairs={{1,2},{2,1},{5,6},{6,5},{9,10},{10,9},{13,14},{14,13},{17,18},{18,... | collective-permute-start | bytes 3145736 | tf_op jit(solution)/shard_map/ppermute | solution.py:624
  33.4 18.5 %shard_map.84.refs_15_ = bf16[8,8,16,1024]{3,2,1,0:T(8,128)(2,1)} custom-call(s32[3]{0:T(128)} %add_add_fusion.half_ref.refs_3_, bf16[4,8,16,1024]{3,2,1,0:T(8,128)(2,1)} %copy-done.7, bf16[4,8,16,1024]{3,2,1,0:T(8,128)(2,1)} %collective-permute-done.3.refs_1_, bf16[2,8,8,16,1024]{4,3,2,1,0:T(8,128)(2,1)} %get-tuple-element.42.refs_2_.refs_3_.refs_14_, ...), custom_call_target="tpu_custom_call" | custom-call | flops 6442450944 | bytes 16777216 | tf_op jit(solution)/shard_map/pallas_call | solution.py:308
  51.9 0.9 collective-permute-done.rest_0_.refs_5_
  52.9 3.2 %collective-permute-start.6 = (bf16[4,8,16,1024]{3,2,1,0:T(8,128)(2,1)}, bf16[4,8,16,1024]{3,2,1,0:T(8,128)(2,1)}, u32[]{:S(2)}, u32[]{:S(2)}) collective-permute-start(bf16[4,8,16,1024]{3,2,1,0:T(8,128)(2,1)} %collective-permute-done.rest_0_.refs_5_), channel_id=1, source_target_pairs={{3,2},{0,1},{1,4},{6,3},{7,6},{4,5},{5,8},{10,7},{11,10},{8,9},{9,... | collective-permute-start | bytes 3145736 | tf_op jit(solution)/shard_map/ppermute | solution.py:628
  56.1 3.8 %collective-permute-start.8 = (bf16[4,8,16,1024]{3,2,1,0:T(8,128)(2,1)}, bf16[4,8,16,1024]{3,2,1,0:T(8,128)(2,1)}, u32[]{:S(2)}, u32[]{:S(2)}) collective-permute-start(bf16[4,8,16,1024]{3,2,1,0:T(8,128)(2,1)} %collective-permute-done.1.rest_1_.refs_6_), channel_id=1, source_target_pairs={{7,4},{0,3},{3,8},{12,7},{15,12},{8,11},{11,16},{20,15},{23,20},{1... | collective-permute-start | bytes 3145736 | tf_op jit(solution)/shard_map/ppermute | solution.py:627
  60.0 0.9 copy-done.1
  61.2 5.9 %shard_map.85 = (bf16[8,4,16,1024]{3,2,1,0:T(8,128)(2,1)}, bf16[8,4,16,1024]{3,2,1,0:T(8,128)(2,1)}, bf16[8,4,16,1024]{3,2,1,0:T(8,128)(2,1)}, bf16[8,4,16,1024]{3,2,1,0:T(8,128)(2,1)}, bf16[16,4,16,1024]{3,2,1,0:T(8,128)(2,1)}) custom-call(s32[1,8,16]{2,1,0:T(8,128)} %bitcast.16, s32[1,8,16]{2,1,0:T(8,128)} %refs_1_.3, ...), custom_call_target="tpu_custom_call" | custom-call | bytes 6291456 | tf_op jit(solution)/shard_map/pallas_call | solution.py:204
  67.6 2.4 %collective-permute-done.6.refs_0_ = bf16[4,8,16,1024]{3,2,1,0:T(8,128)(2,1)} collective-permute-done((bf16[4,8,16,1024]{3,2,1,0:T(8,128)(2,1)}, bf16[4,8,16,1024]{3,2,1,0:T(8,128)(2,1)}, u32[]{:S(2)}, u32[]{:S(2)}) %collective-permute-start.6) | collective-permute-done | bytes 1048608 | tf_op jit(solution)/shard_map/ppermute | solution.py:628
  70.0 5.7 %collective-permute-done.8.refs_2_ = bf16[4,8,16,1024]{3,2,1,0:T(8,128)(2,1)} collective-permute-done((bf16[4,8,16,1024]{3,2,1,0:T(8,128)(2,1)}, bf16[4,8,16,1024]{3,2,1,0:T(8,128)(2,1)}, u32[]{:S(2)}, u32[]{:S(2)}) %collective-permute-start.8) | collective-permute-done | bytes 1048608 | tf_op jit(solution)/shard_map/ppermute | solution.py:627
  76.6 18.9 %shard_map.86.refs_16_ = bf16[8,8,16,1024]{3,2,1,0:T(8,128)(2,1)} custom-call(s32[3]{0:T(128)} %add_add_fusion.1.half_ref, bf16[4,8,16,1024]{3,2,1,0:T(8,128)(2,1)} %collective-permute-done.6.refs_0_, bf16[4,8,16,1024]{3,2,1,0:T(8,128)(2,1)} %collective-permute-done.7.refs_1_, bf16[4,8,16,1024]{3,2,1,0:T(8,128)(2,1)} %collective-permute-done.8.refs_2_, ...), custom_call_target="tpu_custom_call" | custom-call | flops 6442450944 | bytes 16777216 | tf_op jit(solution)/shard_map/pallas_call | solution.py:308
  95.5 2.0 %collective-permute-start.12 = (bf16[8,4,16,1024]{3,2,1,0:T(8,128)(2,1)S(1)}, bf16[8,4,16,1024]{3,2,1,0:T(8,128)(2,1)S(1)}, u32[]{:S(2)}, u32[]{:S(2)}) collective-permute-start(bf16[8,4,16,1024]{3,2,1,0:T(8,128)(2,1)S(1)} %copy-done.8), channel_id=1, source_target_pairs={{0,5},{1,4},{2,7},{3,6},{4,1},{5,0},{6,3},{7,2},{8,13},{9,12},{10,... | collective-permute-start | bytes 3145736 | tf_op jit(solution)/shard_map/ppermute | solution.py:581
  97.5 3.6 %collective-permute-done.9.refs_9_ = bf16[8,4,16,1024]{3,2,1,0:T(8,128)(2,1)} collective-permute-done((bf16[8,4,16,1024]{3,2,1,0:T(8,128)(2,1)}, bf16[8,4,16,1024]{3,2,1,0:T(8,128)(2,1)}, u32[]{:S(2)}, u32[]{:S(2)}) %collective-permute-start.9) | collective-permute-done | bytes 1048608 | tf_op jit(solution)/shard_map/ppermute | solution.py:581
  101.1 1.4 copy-done
  102.5 25.4 %shard_map.87.refs_20_ = bf16[2,8,8,16,1024]{4,3,2,1,0:T(8,128)(2,1)} custom-call(s32[1,8,16]{2,1,0:T(8,128)} %bitcast.17, s32[1,8,16]{2,1,0:T(8,128)} %refs_1_.3, s32[16]{0:T(128)} %bitcast.19, s32[3]{0:T(128)} %add_add_fusion.half_ref.refs_3_, bf16[2,8,8,16,1024]{4,3,2,1,0:T(8,128)(2,1)} %bitcast.14, ...), custom_call_target="tpu_custom_call" | custom-call | flops 9395240960 | bytes 16777216 | tf_op jit(solution)/shard_map/pallas_call | solution.py:530
  127.9 1.0 copy-done.4
  128.9 1.0 copy-done.5
  129.9 14.5 %shard_map.88 = bf16[2,8,8,16,1024]{4,3,2,1,0:T(8,128)(2,1)} custom-call(s32[1,8,16]{2,1,0:T(8,128)} %bitcast.18, s32[1,8,16]{2,1,0:T(8,128)} %refs_1_.3, s32[16]{0:T(128)} %bitcast.20, s32[3]{0:T(128)} %add_add_fusion.half_ref.refs_3_, bf16[2,8,8,16,1024]{4,3,2,1,0:T(8,128)(2,1)} %bitcast.15, ...), custom_call_target="tpu_custom_call", output_to_operand_aliasing={{}: (20, {})} | custom-call | flops 5637144576 | bytes 12582912 | tf_op jit(solution)/shard_map/pallas_call | solution.py:530
  (35 shorter events, 3.7 us)
Async XLA Ops:
  4.6 24.6 %copy-start.6 = (s32[32]{0:T(128)S(1)}, s32[32]{0:T(128)}, u32[]{:S(2)}) copy-start(s32[32]{0:T(128)} %param.12) | copy-start | bytes 388
  4.6 4.1 %collective-permute-start.2 = (bf16[4,8,16,1024]{3,2,1,0:T(8,128)(2,1)}, bf16[4,8,16,1024]{3,2,1,0:T(8,128)(2,1)S(1)}, u32[]{:S(2)}, u32[]{:S(2)}) collective-permute-start(bf16[4,8,16,1024]{3,2,1,0:T(8,128)(2,1)} %get-tuple-element.39), channel_id=1, source_target_pairs={{0,1},{1,0},{2,3},{3,2},{4,5},{5,4},{6,7},{7,6},{8,9},{9,8},{10,11... | collective-permute-start | bytes 3145736 | tf_op jit(solution)/shard_map/ppermute | solution.py:581
  5.4 54.6 %collective-permute-start.4 = (bf16[4,8,16,1024]{3,2,1,0:T(8,128)(2,1)}, bf16[4,8,16,1024]{3,2,1,0:T(8,128)(2,1)S(1)}, u32[]{:S(2)}, u32[]{:S(2)}) collective-permute-start(bf16[4,8,16,1024]{3,2,1,0:T(8,128)(2,1)} %get-tuple-element.39), channel_id=1, source_target_pairs={{0,2},{1,3},{2,0},{3,1},{4,6},{5,7},{6,4},{7,5},{8,10},{9,11},{10,... | collective-permute-start | bytes 3145736 | tf_op jit(solution)/shard_map/ppermute | solution.py:581
  5.6 54.3 %collective-permute-start.5 = (bf16[4,8,16,1024]{3,2,1,0:T(8,128)(2,1)}, bf16[4,8,16,1024]{3,2,1,0:T(8,128)(2,1)S(1)}, u32[]{:S(2)}, u32[]{:S(2)}) collective-permute-start(bf16[4,8,16,1024]{3,2,1,0:T(8,128)(2,1)} %get-tuple-element.40), channel_id=1, source_target_pairs={{0,4},{1,5},{2,6},{3,7},{4,0},{5,1},{6,2},{7,3},{8,12},{9,13},{10,... | collective-permute-start | bytes 3145736 | tf_op jit(solution)/shard_map/ppermute | solution.py:581
  6.9 24.9 %collective-permute-start.3 = (bf16[4,8,16,1024]{3,2,1,0:T(8,128)(2,1)}, bf16[4,8,16,1024]{3,2,1,0:T(8,128)(2,1)}, u32[]{:S(2)}, u32[]{:S(2)}) collective-permute-start(bf16[4,8,16,1024]{3,2,1,0:T(8,128)(2,1)} %get-tuple-element.40), channel_id=1, source_target_pairs={{0,1},{1,0},{2,3},{3,2},{4,5},{5,4},{6,7},{7,6},{8,9},{9,8},{10,11... | collective-permute-start | bytes 3145736 | tf_op jit(solution)/shard_map/ppermute | solution.py:581
  7.5 45.4 %collective-permute-start = (bf16[4,8,16,1024]{3,2,1,0:T(8,128)(2,1)}, bf16[4,8,16,1024]{3,2,1,0:T(8,128)(2,1)}, u32[]{:S(2)}, u32[]{:S(2)}) collective-permute-start(bf16[4,8,16,1024]{3,2,1,0:T(8,128)(2,1)} %get-tuple-element.37), channel_id=1, source_target_pairs={{0,2},{1,3},{2,0},{3,1},{4,6},{5,7},{6,4},{7,5},{8,10},{9,11},{10,... | collective-permute-start | bytes 3145736 | tf_op jit(solution)/shard_map/ppermute | solution.py:581
  8.7 20.5 %copy-start.7 = (bf16[4,8,16,1024]{3,2,1,0:T(8,128)(2,1)}, bf16[4,8,16,1024]{3,2,1,0:T(8,128)(2,1)S(1)}, u32[]{:S(2)}) copy-start(bf16[4,8,16,1024]{3,2,1,0:T(8,128)(2,1)S(1)} %collective-permute-done.2.refs_0_) | copy-start | bytes 3145732
  8.7 44.2 %collective-permute-start.1 = (bf16[4,8,16,1024]{3,2,1,0:T(8,128)(2,1)}, bf16[4,8,16,1024]{3,2,1,0:T(8,128)(2,1)}, u32[]{:S(2)}, u32[]{:S(2)}) collective-permute-start(bf16[4,8,16,1024]{3,2,1,0:T(8,128)(2,1)} %get-tuple-element.38), channel_id=1, source_target_pairs={{0,4},{1,5},{2,6},{3,7},{4,0},{5,1},{6,2},{7,3},{8,12},{9,13},{10,... | collective-permute-start | bytes 3145736 | tf_op jit(solution)/shard_map/ppermute | solution.py:581
  31.8 35.8 %collective-permute-start.7 = (bf16[4,8,16,1024]{3,2,1,0:T(8,128)(2,1)}, bf16[4,8,16,1024]{3,2,1,0:T(8,128)(2,1)}, u32[]{:S(2)}, u32[]{:S(2)}) collective-permute-start(bf16[4,8,16,1024]{3,2,1,0:T(8,128)(2,1)} %get-tuple-element.38), channel_id=1, source_target_pairs={{1,2},{2,1},{5,6},{6,5},{9,10},{10,9},{13,14},{14,13},{17,18},{18,... | collective-permute-start | bytes 3145736 | tf_op jit(solution)/shard_map/ppermute | solution.py:624
  52.9 17.1 %collective-permute-start.6 = (bf16[4,8,16,1024]{3,2,1,0:T(8,128)(2,1)}, bf16[4,8,16,1024]{3,2,1,0:T(8,128)(2,1)}, u32[]{:S(2)}, u32[]{:S(2)}) collective-permute-start(bf16[4,8,16,1024]{3,2,1,0:T(8,128)(2,1)} %collective-permute-done.rest_0_.refs_5_), channel_id=1, source_target_pairs={{3,2},{0,1},{1,4},{6,3},{7,6},{4,5},{5,8},{10,7},{11,10},{8,9},{9,... | collective-permute-start | bytes 3145736 | tf_op jit(solution)/shard_map/ppermute | solution.py:628
  56.1 19.6 %collective-permute-start.8 = (bf16[4,8,16,1024]{3,2,1,0:T(8,128)(2,1)}, bf16[4,8,16,1024]{3,2,1,0:T(8,128)(2,1)}, u32[]{:S(2)}, u32[]{:S(2)}) collective-permute-start(bf16[4,8,16,1024]{3,2,1,0:T(8,128)(2,1)} %collective-permute-done.1.rest_1_.refs_6_), channel_id=1, source_target_pairs={{7,4},{0,3},{3,8},{12,7},{15,12},{8,11},{11,16},{20,15},{23,20},{1... | collective-permute-start | bytes 3145736 | tf_op jit(solution)/shard_map/ppermute | solution.py:627
  59.9 1.0 copy-start.1
  60.0 1.3 copy-start.2
  67.1 34.0 %collective-permute-start.13 = (bf16[16,4,16,1024]{3,2,1,0:T(8,128)(2,1)}, bf16[16,4,16,1024]{3,2,1,0:T(8,128)(2,1)S(1)}, u32[]{:S(2)}, u32[]{:S(2)}) collective-permute-start(bf16[16,4,16,1024]{3,2,1,0:T(8,128)(2,1)} %get-tuple-element.58), channel_id=1, source_target_pairs={{0,1},{1,0},{2,3},{3,2},{4,5},{5,4},{6,7},{7,6},{8,9},{9,8},{10,11... | collective-permute-start | bytes 6291464 | tf_op jit(solution)/shard_map/ppermute | solution.py:581
  67.2 30.3 %collective-permute-start.11 = (bf16[8,4,16,1024]{3,2,1,0:T(8,128)(2,1)}, bf16[8,4,16,1024]{3,2,1,0:T(8,128)(2,1)S(1)}, u32[]{:S(2)}, u32[]{:S(2)}) collective-permute-start(bf16[8,4,16,1024]{3,2,1,0:T(8,128)(2,1)} %get-tuple-element.56), channel_id=1, source_target_pairs={{0,4},{1,5},{2,6},{3,7},{4,0},{5,1},{6,2},{7,3},{8,12},{9,13},{10,... | collective-permute-start | bytes 3145736 | tf_op jit(solution)/shard_map/ppermute | solution.py:581
  75.7 25.4 %collective-permute-start.9 = (bf16[8,4,16,1024]{3,2,1,0:T(8,128)(2,1)}, bf16[8,4,16,1024]{3,2,1,0:T(8,128)(2,1)}, u32[]{:S(2)}, u32[]{:S(2)}) collective-permute-start(bf16[8,4,16,1024]{3,2,1,0:T(8,128)(2,1)} %get-tuple-element.49), channel_id=1, source_target_pairs={{0,2},{1,3},{2,0},{3,1},{4,6},{5,7},{6,4},{7,5},{8,10},{9,11},{10,... | collective-permute-start | bytes 3145736 | tf_op jit(solution)/shard_map/ppermute | solution.py:581
  76.6 18.9 %copy-start.9 = (bf16[8,4,16,1024]{3,2,1,0:T(8,128)(2,1)S(1)}, bf16[8,4,16,1024]{3,2,1,0:T(8,128)(2,1)}, u32[]{:S(2)}) copy-start(bf16[8,4,16,1024]{3,2,1,0:T(8,128)(2,1)} %get-tuple-element.55) | copy-start | bytes 3145732
  76.6 18.9 %copy-start.8 = (bf16[8,4,16,1024]{3,2,1,0:T(8,128)(2,1)S(1)}, bf16[8,4,16,1024]{3,2,1,0:T(8,128)(2,1)}, u32[]{:S(2)}) copy-start(bf16[8,4,16,1024]{3,2,1,0:T(8,128)(2,1)} %get-tuple-element.57) | copy-start | bytes 3145732
  95.5 32.4 %collective-permute-start.10 = (bf16[8,4,16,1024]{3,2,1,0:T(8,128)(2,1)S(1)}, bf16[8,4,16,1024]{3,2,1,0:T(8,128)(2,1)S(1)}, u32[]{:S(2)}, u32[]{:S(2)}) collective-permute-start(bf16[8,4,16,1024]{3,2,1,0:T(8,128)(2,1)S(1)} %copy-done.9), channel_id=1, source_target_pairs={{0,3},{1,2},{2,1},{3,0},{4,7},{5,6},{6,5},{7,4},{8,11},{9,10},{10,... | collective-permute-start | bytes 3145736 | tf_op jit(solution)/shard_map/ppermute | solution.py:581
  95.5 32.4 %collective-permute-start.12 = (bf16[8,4,16,1024]{3,2,1,0:T(8,128)(2,1)S(1)}, bf16[8,4,16,1024]{3,2,1,0:T(8,128)(2,1)S(1)}, u32[]{:S(2)}, u32[]{:S(2)}) collective-permute-start(bf16[8,4,16,1024]{3,2,1,0:T(8,128)(2,1)S(1)} %copy-done.8), channel_id=1, source_target_pairs={{0,5},{1,4},{2,7},{3,6},{4,1},{5,0},{6,3},{7,2},{8,13},{9,12},{10,... | collective-permute-start | bytes 3145736 | tf_op jit(solution)/shard_map/ppermute | solution.py:581
  97.5 3.6 %copy-start.3 = (bf16[8,4,16,1024]{3,2,1,0:T(8,128)(2,1)}, bf16[8,4,16,1024]{3,2,1,0:T(8,128)(2,1)S(1)}, u32[]{:S(2)}) copy-start(bf16[8,4,16,1024]{3,2,1,0:T(8,128)(2,1)S(1)} %collective-permute-done.11.refs_11_) | copy-start | bytes 3145732
  101.1 1.4 copy-start
  127.9 1.1 copy-start.4
  128.9 1.0 copy-start.5

commit v7 on v6

--- a/solution.py
+++ b/solution.py
@@ -10,7 +10,7 @@
 HEADS = 16
 NORM_EPS = 1e-05
 LOG2E = 1.4426950408889634
-VMEM_LIMIT = 56 * 1024 * 1024
+VMEM_LIMIT = 63 * 1024 * 1024
 GROUP = 4
 
 
@@ -240,7 +240,7 @@
         ],
         in_specs=[
             spec(feat),
-            pl.BlockSpec((1, feat), lambda i: (0, 0)),
+            pl.BlockSpec((feat,), lambda i: (0,)),
             pl.BlockSpec((feat, 3 * feat), lambda i: (0, 0), pipeline_mode=pl.Buffered(1)),
         ],
         out_specs=[spec(feat), spec(2 * feat)],
@@ -315,7 +315,7 @@
                 *[side(spot) for spot in spots],
                 own(feat),
                 own(2 * feat),
-                pl.BlockSpec((1, feat), lambda i, hk: (0, 0)),
+                pl.BlockSpec((feat,), lambda i, hk: (0,)),
                 pl.BlockSpec((feat, 3 * feat), lambda i, hk: (0, 0), pipeline_mode=pl.Buffered(1)),
             ],
             out_specs=flat,
@@ -517,7 +517,7 @@
     tokens = int(panels * length * share)
     many = pltpu.VMEM((panels, deep, run, feat), jnp.bfloat16)
     operands = [tile_table, panel_table, valid, half_keep, tok, *recv, q, *mixes, gain_row, w_qkv, w_proj]
-    specs = [smem] * 4 + [anym] * (len(recv) + 4) + [pl.BlockSpec((1, feat), lambda: (0, 0))] + [anym] * 2
+    specs = [smem] * 4 + [anym] * (len(recv) + 4) + [pl.BlockSpec((feat,), lambda: (0,))] + [anym] * 2
     aliases = {}
     if earlier is not None:
         aliases = {len(operands): 0}
@@ -569,7 +569,7 @@
     tile_table = partner_tile[:, :, :, 0]
     panel_table = partner_panel
     valid = window_valid.reshape(panels)
-    gain_row = gain.reshape(1, feat)
+    gain_row = gain
     slab_index = lax.axis_index(("scene", "tile"))
     after_index = jnp.minimum(slab_index + 1, slab_count - 1)
     own_first = jnp.logical_or(scene_first[slab_index] == 1, slab_index == 0)
@@ -606,6 +606,7 @@
         direct = jnp.logical_or(slab_index % 4 == 1, slab_index % 4 == 2).astype(jnp.int32)
         near_half = jnp.stack([1 - odd, jnp.where(odd == 1, keep_before, keep_after), direct]).astype(jnp.int32)
         far_half = jnp.stack([odd, jnp.where(odd == 1, keep_after, keep_before), direct]).astype(jnp.int32)
+        near_half, far_half = fence((near_half, far_half))
         links_a, links_b, links_c = [], [], []
         for low in range(1, slab_count - 1, 2):
             links_a += [(low ^ 2, low + 1), ((low + 1) ^ 2, low)]

time: 146 us -> 142 us (0.973)
  local copies, waits for them, and re-layouts: 6.65 us -> 0.62 us
  waiting for transfers between devices: 12.7 us -> 14.9 us
    unnamed x20 -> x2, local copies, waits for them, and re-layouts: 4.73 us -> 0.01 us
    ppermute x1, waiting for transfers between devices: 2.42 us -> 4.75 us  [per_device(): edge_a = lax.ppermute(rim_x, ('scene', 'tile'), links_a)]
  transfers between devices with their start and end apart: 14 -> 14, of which waited for: 4 -> 4; matrix products, arithmetic and copies ran while one was open for 1% -> 1% of each run, Pallas kernels for 61% -> 63%
where the time goes in v7:
time: 142 us; the launch traced here: 140 us
  Pallas kernels  107 us (75%)
  starting transfers between devices  15.7 us (11%)
  waiting for transfers between devices  14.9 us (10%)
  between operations  1.52 us (1%)
    pallas_call x2, Pallas kernels, cross_and_project(): pl.pallas_call(kernel, out_shape=jax.ShapeDtypeStruct(tok.shape, jnp.bflo...  39.8 us
    pallas_call x2, Pallas kernels, window_mix(): pl.pallas_call(functools.partial(window_kernel, head_width), out_shape=ja...  37.3 us
    pallas_call x1, Pallas kernels, project_own(): pl.pallas_call(qkv_kernel, grid=(halves * 2,), out_shape=[jax.ShapeDtypeS...  20.2 us
    ppermute x11, starting transfers between devices, xor(): return lax.ppermute(block, 'tile', [(i, i ^ bits) for i in range(tiles)])  6.95 us
    pallas_call x1, Pallas kernels, pack_far(): pl.pallas_call(functools.partial(far_kernel, cap), out_shape=[jax.ShapeDt...  6.07 us
    ppermute x11, waiting for transfers between devices, xor(): return lax.ppermute(block, 'tile', [(i, i ^ bits) for i in range(tiles)])  5.36 us
    ppermute x1, waiting for transfers between devices, per_device(): edge_c = lax.ppermute(rim_y, ('scene', 'tile'), links_c)  4.78 us
    ppermute x1, waiting for transfers between devices, per_device(): edge_a = lax.ppermute(rim_x, ('scene', 'tile'), links_a)  4.75 us
  transfers between devices with their start and end apart: 14, of which 4 were waited for; matrix products, arithmetic and copies ran while one was open for 1% of the time, Pallas kernels for 63%

profile of v7, /device:TPU:11, one launch (start us, length us, event | category | flops | bytes accessed | tf_op | source)
XLA Modules:
  0.0 140.0 jit_solution(9961724537754274776)
XLA Ops:
  0.0 3.3 %shard_map.82 = (bf16[4,8,16,1024]{3,2,1,0:T(8,128)(2,1)}, bf16[4,8,16,1024]{3,2,1,0:T(8,128)(2,1)}, bf16[4,8,16,1024]{3,2,1,0:T(8,128)(2,1)}, bf16[4,8,16,1024]{3,2,1,0:T(8,128)(2,1)}) custom-call(bf16[2,8,8,16,1024]{4,3,2,1,0:T(8,128)(2,1)} %bitcast.11), custom_call_target="tpu_custom_call" | custom-call | bytes 8388608 | tf_op jit(solution)/shard_map/pallas_call | solution.py:126
  3.3 0.7 collective-permute-start.2
  4.1 0.3 collective-permute-start.4
  4.3 1.2 collective-permute-start.5
  5.6 0.6 collective-permute-start.3
  6.2 1.2 collective-permute-start
  7.4 0.5 collective-permute-start.1
  7.9 20.2 %shard_map.83 = (bf16[2,8,8,16,1024]{4,3,2,1,0:T(8,128)(2,1)}, bf16[2,8,8,16,2048]{4,3,2,1,0:T(8,128)(2,1)}) custom-call(bf16[2,8,8,16,1024]{4,3,2,1,0:T(8,128)(2,1)} %bitcast.12, bf16[1024]{0:T(1024)(128)(2,1)} %refs_17_.3, bf16[1024,3072]{1,0:T(8,128)(2,1)} %refs_18_.3), custom_call_target="tpu_custom_call" | custom-call | flops 12884901888 | bytes 23068672 | tf_op jit(solution)/shard_map/pallas_call | solution.py:234
  28.1 0.6 fusion
  30.0 0.7 add_add_fusion
  30.7 1.7 %collective-permute-start.7 = (bf16[4,8,16,1024]{3,2,1,0:T(8,128)(2,1)}, bf16[4,8,16,1024]{3,2,1,0:T(8,128)(2,1)}, u32[]{:S(2)}, u32[]{:S(2)}) collective-permute-start(bf16[4,8,16,1024]{3,2,1,0:T(8,128)(2,1)} %get-tuple-element.41), channel_id=1, source_target_pairs={{1,2},{2,1},{5,6},{6,5},{9,10},{10,9},{13,14},{14,13},{17,18},{18,... | collective-permute-start | bytes 3145736 | tf_op jit(solution)/shard_map/ppermute | solution.py:625
  32.4 18.5 %shard_map.84.refs_15_ = bf16[8,8,16,1024]{3,2,1,0:T(8,128)(2,1)} custom-call(s32[3]{0:T(128)} %get-tuple-element.35.half_ref.refs_3_, bf16[4,8,16,1024]{3,2,1,0:T(8,128)(2,1)} %collective-permute-done.2.refs_0_, bf16[4,8,16,1024]{3,2,1,0:T(8,128)(2,1)} %collective-permute-done.3.refs_1_, ...), custom_call_target="tpu_custom_call" | custom-call | flops 6442450944 | bytes 16777216 | tf_op jit(solution)/shard_map/pallas_call | solution.py:308
  50.9 0.7 collective-permute-done.rest_0_.refs_5_
  51.6 3.2 %collective-permute-start.6 = (bf16[4,8,16,1024]{3,2,1,0:T(8,128)(2,1)}, bf16[4,8,16,1024]{3,2,1,0:T(8,128)(2,1)}, u32[]{:S(2)}, u32[]{:S(2)}) collective-permute-start(bf16[4,8,16,1024]{3,2,1,0:T(8,128)(2,1)} %collective-permute-done.rest_0_.refs_5_), channel_id=1, source_target_pairs={{3,2},{0,1},{1,4},{6,3},{7,6},{4,5},{5,8},{10,7},{11,10},{8,9},{9,... | collective-permute-start | bytes 3145736 | tf_op jit(solution)/shard_map/ppermute | solution.py:629
  54.8 3.8 %collective-permute-start.8 = (bf16[4,8,16,1024]{3,2,1,0:T(8,128)(2,1)}, bf16[4,8,16,1024]{3,2,1,0:T(8,128)(2,1)}, u32[]{:S(2)}, u32[]{:S(2)}) collective-permute-start(bf16[4,8,16,1024]{3,2,1,0:T(8,128)(2,1)} %collective-permute-done.1.rest_1_.refs_6_), channel_id=1, source_target_pairs={{7,4},{0,3},{3,8},{12,7},{15,12},{8,11},{11,16},{20,15},{23,20},{1... | collective-permute-start | bytes 3145736 | tf_op jit(solution)/shard_map/ppermute | solution.py:628
  58.7 6.1 %shard_map.85 = (bf16[8,4,16,1024]{3,2,1,0:T(8,128)(2,1)}, bf16[8,4,16,1024]{3,2,1,0:T(8,128)(2,1)}, bf16[8,4,16,1024]{3,2,1,0:T(8,128)(2,1)}, bf16[8,4,16,1024]{3,2,1,0:T(8,128)(2,1)}, bf16[16,4,16,1024]{3,2,1,0:T(8,128)(2,1)}) custom-call(s32[1,8,16]{2,1,0:T(8,128)} %bitcast.16, s32[1,8,16]{2,1,0:T(8,128)} %refs_1_.3, ...), custom_call_target="tpu_custom_call" | custom-call | bytes 6291456 | tf_op jit(solution)/shard_map/pallas_call | solution.py:204
  65.0 4.7 %collective-permute-done.6.refs_0_ = bf16[4,8,16,1024]{3,2,1,0:T(8,128)(2,1)} collective-permute-done((bf16[4,8,16,1024]{3,2,1,0:T(8,128)(2,1)}, bf16[4,8,16,1024]{3,2,1,0:T(8,128)(2,1)}, u32[]{:S(2)}, u32[]{:S(2)}) %collective-permute-start.6) | collective-permute-done | bytes 1048608 | tf_op jit(solution)/shard_map/ppermute | solution.py:629
  69.7 4.8 %collective-permute-done.8.refs_2_ = bf16[4,8,16,1024]{3,2,1,0:T(8,128)(2,1)} collective-permute-done((bf16[4,8,16,1024]{3,2,1,0:T(8,128)(2,1)}, bf16[4,8,16,1024]{3,2,1,0:T(8,128)(2,1)}, u32[]{:S(2)}, u32[]{:S(2)}) %collective-permute-start.8) | collective-permute-done | bytes 1048608 | tf_op jit(solution)/shard_map/ppermute | solution.py:628
  74.5 0.3 collective-permute-start.9
  74.8 18.7 %shard_map.86.refs_16_ = bf16[8,8,16,1024]{3,2,1,0:T(8,128)(2,1)} custom-call(s32[3]{0:T(128)} %get-tuple-element.55.half_ref, bf16[4,8,16,1024]{3,2,1,0:T(8,128)(2,1)} %collective-permute-done.6.refs_0_, bf16[4,8,16,1024]{3,2,1,0:T(8,128)(2,1)} %collective-permute-done.7.refs_1_, bf16[4,8,16,1024]{3,2,1,0:T(8,128)(2,1)} %collective-permute-done.8.refs_2_, ...), custom_call_target="tpu_custom_call" | custom-call | flops 6442450944 | bytes 16777216 | tf_op jit(solution)/shard_map/pallas_call | solution.py:308
  93.5 1.8 %collective-permute-start.12 = (bf16[8,4,16,1024]{3,2,1,0:T(8,128)(2,1)}, bf16[8,4,16,1024]{3,2,1,0:T(8,128)(2,1)}, u32[]{:S(2)}, u32[]{:S(2)}) collective-permute-start(bf16[8,4,16,1024]{3,2,1,0:T(8,128)(2,1)} %get-tuple-element.61), channel_id=1, source_target_pairs={{0,5},{1,4},{2,7},{3,6},{4,1},{5,0},{6,3},{7,2},{8,13},{9,12},{10,... | collective-permute-start | bytes 3145736 | tf_op jit(solution)/shard_map/ppermute | solution.py:581
  95.4 4.7 %collective-permute-done.9.refs_9_ = bf16[8,4,16,1024]{3,2,1,0:T(8,128)(2,1)} collective-permute-done((bf16[8,4,16,1024]{3,2,1,0:T(8,128)(2,1)}, bf16[8,4,16,1024]{3,2,1,0:T(8,128)(2,1)}, u32[]{:S(2)}, u32[]{:S(2)}) %collective-permute-start.9) | collective-permute-done | bytes 1048608 | tf_op jit(solution)/shard_map/ppermute | solution.py:581
  100.0 25.4 %shard_map.87.refs_20_ = bf16[2,8,8,16,1024]{4,3,2,1,0:T(8,128)(2,1)} custom-call(s32[1,8,16]{2,1,0:T(8,128)} %bitcast.17, s32[1,8,16]{2,1,0:T(8,128)} %refs_1_.3, s32[16]{0:T(128)} %bitcast.19, s32[3]{0:T(128)} %get-tuple-element.35.half_ref.refs_3_, bf16[2,8,8,16,1024]{4,3,2,1,0:T(8,128)(2,1)} %bitcast.14, ...), custom_call_target="tpu_custom_call" | custom-call | flops 9395240960 | bytes 16777216 | tf_op jit(solution)/shard_map/pallas_call | solution.py:530
  125.4 14.5 %shard_map.88 = bf16[2,8,8,16,1024]{4,3,2,1,0:T(8,128)(2,1)} custom-call(s32[1,8,16]{2,1,0:T(8,128)} %bitcast.18, s32[1,8,16]{2,1,0:T(8,128)} %refs_1_.3, s32[16]{0:T(128)} %bitcast.20, s32[3]{0:T(128)} %get-tuple-element.35.half_ref.refs_3_, bf16[2,8,8,16,1024]{4,3,2,1,0:T(8,128)(2,1)} %bitcast.15, ...), custom_call_target="tpu_custom_call", output_to_operand_aliasing={{}: (20, {})} | custom-call | flops 5637144576 | bytes 12582912 | tf_op jit(solution)/shard_map/pallas_call | solution.py:530
  (15 shorter events, 0.3 us)
Async XLA Ops:
  3.3 24.8 %copy-start = (s32[32]{0:T(128)S(1)}, s32[32]{0:T(128)}, u32[]{:S(2)}) copy-start(s32[32]{0:T(128)} %param.12) | copy-start | bytes 388
  3.3 4.1 %collective-permute-start.2 = (bf16[4,8,16,1024]{3,2,1,0:T(8,128)(2,1)}, bf16[4,8,16,1024]{3,2,1,0:T(8,128)(2,1)}, u32[]{:S(2)}, u32[]{:S(2)}) collective-permute-start(bf16[4,8,16,1024]{3,2,1,0:T(8,128)(2,1)} %get-tuple-element.42), channel_id=1, source_target_pairs={{0,1},{1,0},{2,3},{3,2},{4,5},{5,4},{6,7},{7,6},{8,9},{9,8},{10,11... | collective-permute-start | bytes 3145736 | tf_op jit(solution)/shard_map/ppermute | solution.py:581
  4.1 54.6 %collective-permute-start.4 = (bf16[4,8,16,1024]{3,2,1,0:T(8,128)(2,1)}, bf16[4,8,16,1024]{3,2,1,0:T(8,128)(2,1)}, u32[]{:S(2)}, u32[]{:S(2)}) collective-permute-start(bf16[4,8,16,1024]{3,2,1,0:T(8,128)(2,1)} %get-tuple-element.42), channel_id=1, source_target_pairs={{0,2},{1,3},{2,0},{3,1},{4,6},{5,7},{6,4},{7,5},{8,10},{9,11},{10,... | collective-permute-start | bytes 3145736 | tf_op jit(solution)/shard_map/ppermute | solution.py:581
  4.3 54.3 %collective-permute-start.5 = (bf16[4,8,16,1024]{3,2,1,0:T(8,128)(2,1)}, bf16[4,8,16,1024]{3,2,1,0:T(8,128)(2,1)}, u32[]{:S(2)}, u32[]{:S(2)}) collective-permute-start(bf16[4,8,16,1024]{3,2,1,0:T(8,128)(2,1)} %get-tuple-element.43), channel_id=1, source_target_pairs={{0,4},{1,5},{2,6},{3,7},{4,0},{5,1},{6,2},{7,3},{8,12},{9,13},{10,... | collective-permute-start | bytes 3145736 | tf_op jit(solution)/shard_map/ppermute | solution.py:581
  5.6 25.1 %collective-permute-start.3 = (bf16[4,8,16,1024]{3,2,1,0:T(8,128)(2,1)}, bf16[4,8,16,1024]{3,2,1,0:T(8,128)(2,1)}, u32[]{:S(2)}, u32[]{:S(2)}) collective-permute-start(bf16[4,8,16,1024]{3,2,1,0:T(8,128)(2,1)} %get-tuple-element.43), channel_id=1, source_target_pairs={{0,1},{1,0},{2,3},{3,2},{4,5},{5,4},{6,7},{7,6},{8,9},{9,8},{10,11... | collective-permute-start | bytes 3145736 | tf_op jit(solution)/shard_map/ppermute | solution.py:581
  6.2 45.4 %collective-permute-start = (bf16[4,8,16,1024]{3,2,1,0:T(8,128)(2,1)}, bf16[4,8,16,1024]{3,2,1,0:T(8,128)(2,1)}, u32[]{:S(2)}, u32[]{:S(2)}) collective-permute-start(bf16[4,8,16,1024]{3,2,1,0:T(8,128)(2,1)} %get-tuple-element.40), channel_id=1, source_target_pairs={{0,2},{1,3},{2,0},{3,1},{4,6},{5,7},{6,4},{7,5},{8,10},{9,11},{10,... | collective-permute-start | bytes 3145736 | tf_op jit(solution)/shard_map/ppermute | solution.py:581
  7.4 44.2 %collective-permute-start.1 = (bf16[4,8,16,1024]{3,2,1,0:T(8,128)(2,1)}, bf16[4,8,16,1024]{3,2,1,0:T(8,128)(2,1)}, u32[]{:S(2)}, u32[]{:S(2)}) collective-permute-start(bf16[4,8,16,1024]{3,2,1,0:T(8,128)(2,1)} %get-tuple-element.41), channel_id=1, source_target_pairs={{0,4},{1,5},{2,6},{3,7},{4,0},{5,1},{6,2},{7,3},{8,12},{9,13},{10,... | collective-permute-start | bytes 3145736 | tf_op jit(solution)/shard_map/ppermute | solution.py:581
  30.7 34.3 %collective-permute-start.7 = (bf16[4,8,16,1024]{3,2,1,0:T(8,128)(2,1)}, bf16[4,8,16,1024]{3,2,1,0:T(8,128)(2,1)}, u32[]{:S(2)}, u32[]{:S(2)}) collective-permute-start(bf16[4,8,16,1024]{3,2,1,0:T(8,128)(2,1)} %get-tuple-element.41), channel_id=1, source_target_pairs={{1,2},{2,1},{5,6},{6,5},{9,10},{10,9},{13,14},{14,13},{17,18},{18,... | collective-permute-start | bytes 3145736 | tf_op jit(solution)/shard_map/ppermute | solution.py:625
  51.6 18.1 %collective-permute-start.6 = (bf16[4,8,16,1024]{3,2,1,0:T(8,128)(2,1)}, bf16[4,8,16,1024]{3,2,1,0:T(8,128)(2,1)}, u32[]{:S(2)}, u32[]{:S(2)}) collective-permute-start(bf16[4,8,16,1024]{3,2,1,0:T(8,128)(2,1)} %collective-permute-done.rest_0_.refs_5_), channel_id=1, source_target_pairs={{3,2},{0,1},{1,4},{6,3},{7,6},{4,5},{5,8},{10,7},{11,10},{8,9},{9,... | collective-permute-start | bytes 3145736 | tf_op jit(solution)/shard_map/ppermute | solution.py:629
  54.8 19.7 %collective-permute-start.8 = (bf16[4,8,16,1024]{3,2,1,0:T(8,128)(2,1)}, bf16[4,8,16,1024]{3,2,1,0:T(8,128)(2,1)}, u32[]{:S(2)}, u32[]{:S(2)}) collective-permute-start(bf16[4,8,16,1024]{3,2,1,0:T(8,128)(2,1)} %collective-permute-done.1.rest_1_.refs_6_), channel_id=1, source_target_pairs={{7,4},{0,3},{3,8},{12,7},{15,12},{8,11},{11,16},{20,15},{23,20},{1... | collective-permute-start | bytes 3145736 | tf_op jit(solution)/shard_map/ppermute | solution.py:628
  64.7 35.3 %collective-permute-start.13 = (bf16[16,4,16,1024]{3,2,1,0:T(8,128)(2,1)}, bf16[16,4,16,1024]{3,2,1,0:T(8,128)(2,1)}, u32[]{:S(2)}, u32[]{:S(2)}) collective-permute-start(bf16[16,4,16,1024]{3,2,1,0:T(8,128)(2,1)} %get-tuple-element.62), channel_id=1, source_target_pairs={{0,1},{1,0},{2,3},{3,2},{4,5},{5,4},{6,7},{7,6},{8,9},{9,8},{10,11... | collective-permute-start | bytes 6291464 | tf_op jit(solution)/shard_map/ppermute | solution.py:581
  64.8 30.5 %collective-permute-start.11 = (bf16[8,4,16,1024]{3,2,1,0:T(8,128)(2,1)}, bf16[8,4,16,1024]{3,2,1,0:T(8,128)(2,1)}, u32[]{:S(2)}, u32[]{:S(2)}) collective-permute-start(bf16[8,4,16,1024]{3,2,1,0:T(8,128)(2,1)} %get-tuple-element.60), channel_id=1, source_target_pairs={{0,4},{1,5},{2,6},{3,7},{4,0},{5,1},{6,2},{7,3},{8,12},{9,13},{10,... | collective-permute-start | bytes 3145736 | tf_op jit(solution)/shard_map/ppermute | solution.py:581
  74.5 25.5 %collective-permute-start.9 = (bf16[8,4,16,1024]{3,2,1,0:T(8,128)(2,1)}, bf16[8,4,16,1024]{3,2,1,0:T(8,128)(2,1)}, u32[]{:S(2)}, u32[]{:S(2)}) collective-permute-start(bf16[8,4,16,1024]{3,2,1,0:T(8,128)(2,1)} %get-tuple-element.52), channel_id=1, source_target_pairs={{0,2},{1,3},{2,0},{3,1},{4,6},{5,7},{6,4},{7,5},{8,10},{9,11},{10,... | collective-permute-start | bytes 3145736 | tf_op jit(solution)/shard_map/ppermute | solution.py:581
  93.5 31.9 %collective-permute-start.10 = (bf16[8,4,16,1024]{3,2,1,0:T(8,128)(2,1)}, bf16[8,4,16,1024]{3,2,1,0:T(8,128)(2,1)}, u32[]{:S(2)}, u32[]{:S(2)}) collective-permute-start(bf16[8,4,16,1024]{3,2,1,0:T(8,128)(2,1)} %get-tuple-element.59), channel_id=1, source_target_pairs={{0,3},{1,2},{2,1},{3,0},{4,7},{5,6},{6,5},{7,4},{8,11},{9,10},{10,... | collective-permute-start | bytes 3145736 | tf_op jit(solution)/shard_map/ppermute | solution.py:581
  93.5 31.9 %collective-permute-start.12 = (bf16[8,4,16,1024]{3,2,1,0:T(8,128)(2,1)}, bf16[8,4,16,1024]{3,2,1,0:T(8,128)(2,1)}, u32[]{:S(2)}, u32[]{:S(2)}) collective-permute-start(bf16[8,4,16,1024]{3,2,1,0:T(8,128)(2,1)} %get-tuple-element.61), channel_id=1, source_target_pairs={{0,5},{1,4},{2,7},{3,6},{4,1},{5,0},{6,3},{7,2},{8,13},{9,12},{10,... | collective-permute-start | bytes 3145736 | tf_op jit(solution)/shard_map/ppermute | solution.py:581

commit v8 on v7

--- a/solution.py
+++ b/solution.py
@@ -106,29 +106,27 @@
         store.wait()
 
 
-def halves_kernel(tok_ref, *rest):
-    outs, bounce, sems = rest[:4], rest[4], rest[5]
-    deep = outs[0].shape[0]
+def halves_kernel(start, tok_ref, rim_ref, off_ref, bounce, sems):
+    deep = rim_ref.shape[0]
     part = lax.axis_index("tile") & 1
-    sources = [
-        tok_ref.at[part, :deep],
-        tok_ref.at[part, deep:],
-        tok_ref.at[1 - part, :deep],
-        tok_ref.at[1 - part, deep:],
-    ]
-    copy_through(list(zip(sources, outs)), bounce, sems)
-
-
-def split_halves(tok):
+    bite = deep // 2
+    pairs = []
+    for u, out in ((1 - part, off_ref), (part, rim_ref)):
+        for k in range(0, deep, bite):
+            pairs.append((tok_ref.at[u, start + k : start + k + bite], out.at[k : k + bite]))
+    copy_through(pairs, bounce, sems)
+
+
+def split_half(start, tok):
     halves, deep, wide, run, feat = tok.shape
     part = (deep // 2, wide, run, feat)
     anym = pl.BlockSpec(memory_space=pl.ANY)
     return pl.pallas_call(
-        halves_kernel,
-        out_shape=[jax.ShapeDtypeStruct(part, tok.dtype)] * 4,
+        functools.partial(halves_kernel, start),
+        out_shape=[jax.ShapeDtypeStruct(part, tok.dtype)] * 2,
         in_specs=[anym],
-        out_specs=[anym] * 4,
-        scratch_shapes=[pltpu.VMEM((4,) + part, tok.dtype), pltpu.SemaphoreType.DMA((2, 4))],
+        out_specs=[anym] * 2,
+        scratch_shapes=[pltpu.VMEM((4, part[0] // 2) + part[1:], tok.dtype), pltpu.SemaphoreType.DMA((2, 4))],
         cost_estimate=pl.CostEstimate(flops=0, bytes_accessed=8 << 20, transcendentals=0),
     )(tok)
 
@@ -252,7 +250,7 @@
 
 
 def window_kernel(head_width, half_ref, *refs):
-    edges, (q_ref, kvo_ref, gain_ref, w_ref, mix_ref, kv_s) = refs[:-6], refs[-6:]
+    edges, (q_ref, kvo_ref, gain_ref, wk_ref, wv_ref, mix_ref, kv_s) = refs[:-7], refs[-7:]
     deep, group, run, feat = mix_ref.shape
     length = deep * run
     bottom = edges[1][...]
@@ -260,7 +258,9 @@
         bottom = jnp.where(half_ref[2] == 1, bottom, edges[2][...])
     rows = jnp.concatenate([edges[0][...], bottom], axis=0).reshape(deep * group * run, feat)
     normed = layer_norm(rows, gain_ref[...])
-    kv_s[...] = dot_f32(normed, w_ref[:, feat:]).astype(jnp.bfloat16).reshape(kv_s.shape)
+    half_shape = kv_s.shape[:-1] + (feat,)
+    kv_s[..., :feat] = dot_f32(normed, wk_ref[...]).astype(jnp.bfloat16).reshape(half_shape)
+    kv_s[..., feat:] = dot_f32(normed, wv_ref[...]).astype(jnp.bfloat16).reshape(half_shape)
     pair = 2 * head_width
     scale = LOG2E * head_width ** (-0.5)
     bias = jnp.where(
@@ -316,7 +316,10 @@
                 own(feat),
                 own(2 * feat),
                 pl.BlockSpec((feat,), lambda i, hk: (0,)),
-                pl.BlockSpec((feat, 3 * feat), lambda i, hk: (0, 0), pipeline_mode=pl.Buffered(1)),
+                *[
+                    pl.BlockSpec((feat, feat), lambda i, hk, k=k: (0, k), pipeline_mode=pl.Buffered(1))
+                    for k in (1, 2)
+                ],
             ],
             out_specs=flat,
             scratch_shapes=[pltpu.VMEM((deep, group, run, 2 * feat), jnp.bfloat16)],
@@ -327,7 +330,7 @@
             bytes_accessed=tokens * feat * 10 + feat * feat * 6,
             transcendentals=tokens * 256 * HEADS,
         ),
-    )(half_keep, *edges, q, kv_own, gain_row, w_qkv)
+    )(half_keep, *edges, q, kv_own, gain_row, w_qkv, w_qkv)
 
 
 def direct_parts(recv, tok_ref, tiles, wanted, cap):
@@ -615,8 +618,10 @@
             else:
                 links_c += [(low ^ 4, low + 1), ((low + 1) ^ 4, low)]
 
-        rim_x, rim_y, off_x, off_y = split_halves(tok)
-        rim_x, rim_y, off_x, off_y, gain_next = fence((rim_x, rim_y, off_x, off_y, gain_row))
+        rim_x, off_x = split_half(0, tok)
+        tok_next, off_x = fence((tok, off_x))
+        rim_y, off_y = split_half(tok.shape[1] // 2, tok_next)
+        rim_y, off_y, gain_next = fence((rim_y, off_y, gain_row))
         near = (xor(off_x, 1), xor(off_y, 1))
         own_rim = rim_y
         rim_x, rim_y = xor(rim_x, 2), xor(rim_y, 4)

time: 142 us -> 141 us (level)
  Pallas kernels: 107 us -> 104 us
  waiting for transfers between devices: 14.9 us -> 16.7 us
    ppermute x11, waiting for transfers between devices: 5.36 us -> 9.66 us  [xor(): return lax.ppermute(block, 'tile', [(i, i ^ bits) for i in range(tiles)])]
    pallas_call x2, Pallas kernels: 39.8 us -> 36.7 us  [cross_and_project(): pl.pallas_call(kernel, out_shape=jax.ShapeDtypeStruct(tok.shape, jnp.bflo...]
    ppermute x1, waiting for transfers between devices: 4.78 us -> 2.42 us  [per_device(): edge_c = lax.ppermute(rim_y, ('scene', 'tile'), links_c)]
    pallas_call x1 -> x2, Pallas kernels: 3.31 us -> 4.88 us  [split_half(): pl.pallas_call(functools.partial(halves_kernel, start), out_shape=[jax.Sh...]
  transfers between devices with their start and end apart: 14 -> 14, of which waited for: 4 -> 5; matrix products, arithmetic and copies ran while one was open for 1% -> 1% of each run, Pallas kernels for 63% -> 59%
where the time goes in v8:
time: 141 us; the launch traced here: 140 us
  Pallas kernels  104 us (74%)
  waiting for transfers between devices  16.7 us (12%)
  starting transfers between devices  16.5 us (12%)
  between operations  1.56 us (1%)
    pallas_call x2, Pallas kernels, cross_and_project(): pl.pallas_call(kernel, out_shape=jax.ShapeDtypeStruct(tok.shape, jnp.bflo...  36.7 us
    pallas_call x2, Pallas kernels, window_mix(): pl.pallas_call(functools.partial(window_kernel, head_width), out_shape=ja...  36.1 us
    pallas_call x1, Pallas kernels, project_own(): pl.pallas_call(qkv_kernel, grid=(halves * 2,), out_shape=[jax.ShapeDtypeS...  20.2 us
    ppermute x11, waiting for transfers between devices, xor(): return lax.ppermute(block, 'tile', [(i, i ^ bits) for i in range(tiles)])  9.66 us
    ppermute x11, starting transfers between devices, xor(): return lax.ppermute(block, 'tile', [(i, i ^ bits) for i in range(tiles)])  7.7 us
    pallas_call x1, Pallas kernels, pack_far(): pl.pallas_call(functools.partial(far_kernel, cap), out_shape=[jax.ShapeDt...  5.84 us
    pallas_call x2, Pallas kernels, split_half(): pl.pallas_call(functools.partial(halves_kernel, start), out_shape=[jax.Sh...  4.88 us
    ppermute x1, waiting for transfers between devices, per_device(): edge_a = lax.ppermute(rim_x, ('scene', 'tile'), links_a)  4.66 us
  transfers between devices with their start and end apart: 14, of which 5 were waited for; matrix products, arithmetic and copies ran while one was open for 1% of the time, Pallas kernels for 59%

profile of v8, /device:TPU:11, one launch (start us, length us, event | category | flops | bytes accessed | tf_op | source)
XLA Modules:
  0.0 139.9 jit_solution(17355818368411070404)
XLA Ops:
  0.0 2.4 %shard_map.82 = (bf16[4,8,16,1024]{3,2,1,0:T(8,128)(2,1)}, bf16[4,8,16,1024]{3,2,1,0:T(8,128)(2,1)}) custom-call(bf16[2,8,8,16,1024]{4,3,2,1,0:T(8,128)(2,1)} %bitcast.11), custom_call_target="tpu_custom_call" | custom-call | bytes 8388608 | tf_op jit(solution)/shard_map/pallas_call | solution.py:124
  2.4 0.7 collective-permute-start.2
  3.4 2.5 %shard_map.83 = (bf16[4,8,16,1024]{3,2,1,0:T(8,128)(2,1)}, bf16[4,8,16,1024]{3,2,1,0:T(8,128)(2,1)}) custom-call(bf16[2,8,8,16,1024]{4,3,2,1,0:T(8,128)(2,1)} %bitcast.12), custom_call_target="tpu_custom_call" | custom-call | bytes 8388608 | tf_op jit(solution)/shard_map/pallas_call | solution.py:124
  5.9 1.3 collective-permute-start.5
  7.2 0.6 collective-permute-start.3
  7.8 1.2 collective-permute-start
  9.3 20.2 %shard_map.84 = (bf16[2,8,8,16,1024]{4,3,2,1,0:T(8,128)(2,1)}, bf16[2,8,8,16,2048]{4,3,2,1,0:T(8,128)(2,1)}) custom-call(bf16[2,8,8,16,1024]{4,3,2,1,0:T(8,128)(2,1)} %bitcast.13, bf16[1024]{0:T(1024)(128)(2,1)} %refs_17_.3, bf16[1024,3072]{1,0:T(8,128)(2,1)} %refs_18_.3), custom_call_target="tpu_custom_call" | custom-call | flops 12884901888 | bytes 23068672 | tf_op jit(solution)/shard_map/pallas_call | solution.py:232
  29.5 0.6 fusion
  31.4 0.7 add_add_fusion
  32.1 1.7 %collective-permute-start.7 = (bf16[4,8,16,1024]{3,2,1,0:T(8,128)(2,1)}, bf16[4,8,16,1024]{3,2,1,0:T(8,128)(2,1)}, u32[]{:S(2)}, u32[]{:S(2)}) collective-permute-start(bf16[4,8,16,1024]{3,2,1,0:T(8,128)(2,1)} %get-tuple-element.41), channel_id=1, source_target_pairs={{1,2},{2,1},{5,6},{6,5},{9,10},{10,9},{13,14},{14,13},{17,18},{18,... | collective-permute-start | bytes 3145736 | tf_op jit(solution)/shard_map/ppermute | solution.py:630
  33.8 18.0 %shard_map.85.refs_15_ = bf16[8,8,16,1024]{3,2,1,0:T(8,128)(2,1)} custom-call(s32[3]{0:T(128)} %get-tuple-element.35.half_ref.refs_3_, bf16[4,8,16,1024]{3,2,1,0:T(8,128)(2,1)} %collective-permute-done.2.refs_0_, bf16[4,8,16,1024]{3,2,1,0:T(8,128)(2,1)} %collective-permute-done.3.refs_1_, ...), custom_call_target="tpu_custom_call" | custom-call | flops 6442450944 | bytes 16777216 | tf_op jit(solution)/shard_map/pallas_call | solution.py:308
  51.8 1.4 collective-permute-done.1.rest_1_.refs_6_
  53.2 3.1 %collective-permute-start.6 = (bf16[4,8,16,1024]{3,2,1,0:T(8,128)(2,1)}, bf16[4,8,16,1024]{3,2,1,0:T(8,128)(2,1)}, u32[]{:S(2)}, u32[]{:S(2)}) collective-permute-start(bf16[4,8,16,1024]{3,2,1,0:T(8,128)(2,1)} %collective-permute-done.rest_0_.refs_5_), channel_id=1, source_target_pairs={{3,2},{0,1},{1,4},{6,3},{7,6},{4,5},{5,8},{10,7},{11,10},{8,9},{9,... | collective-permute-start | bytes 3145736 | tf_op jit(solution)/shard_map/ppermute | solution.py:634
  56.2 4.0 %collective-permute-start.8 = (bf16[4,8,16,1024]{3,2,1,0:T(8,128)(2,1)}, bf16[4,8,16,1024]{3,2,1,0:T(8,128)(2,1)}, u32[]{:S(2)}, u32[]{:S(2)}) collective-permute-start(bf16[4,8,16,1024]{3,2,1,0:T(8,128)(2,1)} %collective-permute-done.1.rest_1_.refs_6_), channel_id=1, source_target_pairs={{7,4},{0,3},{3,8},{12,7},{15,12},{8,11},{11,16},{20,15},{23,20},{1... | collective-permute-start | bytes 3145736 | tf_op jit(solution)/shard_map/ppermute | solution.py:633
  60.3 5.8 %shard_map.86 = (bf16[8,4,16,1024]{3,2,1,0:T(8,128)(2,1)}, bf16[8,4,16,1024]{3,2,1,0:T(8,128)(2,1)}, bf16[8,4,16,1024]{3,2,1,0:T(8,128)(2,1)}, bf16[8,4,16,1024]{3,2,1,0:T(8,128)(2,1)}, bf16[16,4,16,1024]{3,2,1,0:T(8,128)(2,1)}) custom-call(s32[1,8,16]{2,1,0:T(8,128)} %bitcast.17, s32[1,8,16]{2,1,0:T(8,128)} %refs_1_.3, ...), custom_call_target="tpu_custom_call" | custom-call | bytes 6291456 | tf_op jit(solution)/shard_map/pallas_call | solution.py:202
  66.5 4.7 %collective-permute-done.6.refs_0_ = bf16[4,8,16,1024]{3,2,1,0:T(8,128)(2,1)} collective-permute-done((bf16[4,8,16,1024]{3,2,1,0:T(8,128)(2,1)}, bf16[4,8,16,1024]{3,2,1,0:T(8,128)(2,1)}, u32[]{:S(2)}, u32[]{:S(2)}) %collective-permute-start.6) | collective-permute-done | bytes 1048608 | tf_op jit(solution)/shard_map/ppermute | solution.py:634
  71.2 2.4 %collective-permute-done.8.refs_2_ = bf16[4,8,16,1024]{3,2,1,0:T(8,128)(2,1)} collective-permute-done((bf16[4,8,16,1024]{3,2,1,0:T(8,128)(2,1)}, bf16[4,8,16,1024]{3,2,1,0:T(8,128)(2,1)}, u32[]{:S(2)}, u32[]{:S(2)}) %collective-permute-start.8) | collective-permute-done | bytes 1048608 | tf_op jit(solution)/shard_map/ppermute | solution.py:633
  73.6 18.2 %shard_map.87.refs_16_ = bf16[8,8,16,1024]{3,2,1,0:T(8,128)(2,1)} custom-call(s32[3]{0:T(128)} %get-tuple-element.55.half_ref, bf16[4,8,16,1024]{3,2,1,0:T(8,128)(2,1)} %collective-permute-done.6.refs_0_, bf16[4,8,16,1024]{3,2,1,0:T(8,128)(2,1)} %collective-permute-done.7.refs_1_, bf16[4,8,16,1024]{3,2,1,0:T(8,128)(2,1)} %collective-permute-done.8.refs_2_, ...), custom_call_target="tpu_custom_call" | custom-call | flops 6442450944 | bytes 16777216 | tf_op jit(solution)/shard_map/pallas_call | solution.py:308
  91.8 1.1 collective-permute-start.10
  92.8 1.9 %collective-permute-start.12 = (bf16[8,4,16,1024]{3,2,1,0:T(8,128)(2,1)}, bf16[8,4,16,1024]{3,2,1,0:T(8,128)(2,1)}, u32[]{:S(2)}, u32[]{:S(2)}) collective-permute-start(bf16[8,4,16,1024]{3,2,1,0:T(8,128)(2,1)} %get-tuple-element.61), channel_id=1, source_target_pairs={{0,5},{1,4},{2,7},{3,6},{4,1},{5,0},{6,3},{7,2},{8,13},{9,12},{10,... | collective-permute-start | bytes 3145736 | tf_op jit(solution)/shard_map/ppermute | solution.py:584
  94.7 4.4 %collective-permute-done.9.refs_9_ = bf16[8,4,16,1024]{3,2,1,0:T(8,128)(2,1)} collective-permute-done((bf16[8,4,16,1024]{3,2,1,0:T(8,128)(2,1)}, bf16[8,4,16,1024]{3,2,1,0:T(8,128)(2,1)}, u32[]{:S(2)}, u32[]{:S(2)}) %collective-permute-start.9) | collective-permute-done | bytes 1048608 | tf_op jit(solution)/shard_map/ppermute | solution.py:584
  99.1 18.4 %shard_map.88.refs_20_ = bf16[2,8,8,16,1024]{4,3,2,1,0:T(8,128)(2,1)} custom-call(s32[1,8,16]{2,1,0:T(8,128)} %bitcast.18, s32[1,8,16]{2,1,0:T(8,128)} %refs_1_.3, s32[16]{0:T(128)} %bitcast.20, s32[3]{0:T(128)} %get-tuple-element.35.half_ref.refs_3_, bf16[2,8,8,16,1024]{4,3,2,1,0:T(8,128)(2,1)} %bitcast.15, ...), custom_call_target="tpu_custom_call" | custom-call | flops 9395240960 | bytes 16777216 | tf_op jit(solution)/shard_map/pallas_call | solution.py:533
  117.5 3.9 %collective-permute-done.10.refs_10_ = bf16[8,4,16,1024]{3,2,1,0:T(8,128)(2,1)} collective-permute-done((bf16[8,4,16,1024]{3,2,1,0:T(8,128)(2,1)}, bf16[8,4,16,1024]{3,2,1,0:T(8,128)(2,1)}, u32[]{:S(2)}, u32[]{:S(2)}) %collective-permute-start.10) | collective-permute-done | bytes 1048608 | tf_op jit(solution)/shard_map/ppermute | solution.py:584
  121.4 18.4 %shard_map.89 = bf16[2,8,8,16,1024]{4,3,2,1,0:T(8,128)(2,1)} custom-call(s32[1,8,16]{2,1,0:T(8,128)} %bitcast.19, s32[1,8,16]{2,1,0:T(8,128)} %refs_1_.3, s32[16]{0:T(128)} %bitcast.21, s32[3]{0:T(128)} %get-tuple-element.35.half_ref.refs_3_, bf16[2,8,8,16,1024]{4,3,2,1,0:T(8,128)(2,1)} %bitcast.16, ...), custom_call_target="tpu_custom_call", output_to_operand_aliasing={{}: (20, {})} | custom-call | flops 5637144576 | bytes 12582912 | tf_op jit(solution)/shard_map/pallas_call | solution.py:533
  (16 shorter events, 0.9 us)
Async XLA Ops:
  2.4 6.6 %collective-permute-start.2 = (bf16[4,8,16,1024]{3,2,1,0:T(8,128)(2,1)}, bf16[4,8,16,1024]{3,2,1,0:T(8,128)(2,1)}, u32[]{:S(2)}, u32[]{:S(2)}) collective-permute-start(bf16[4,8,16,1024]{3,2,1,0:T(8,128)(2,1)} %get-tuple-element.42), channel_id=1, source_target_pairs={{0,1},{1,0},{2,3},{3,2},{4,5},{5,4},{6,7},{7,6},{8,9},{9,8},{10,11... | collective-permute-start | bytes 3145736 | tf_op jit(solution)/shard_map/ppermute | solution.py:584
  3.2 57.1 %collective-permute-start.4 = (bf16[4,8,16,1024]{3,2,1,0:T(8,128)(2,1)}, bf16[4,8,16,1024]{3,2,1,0:T(8,128)(2,1)}, u32[]{:S(2)}, u32[]{:S(2)}) collective-permute-start(bf16[4,8,16,1024]{3,2,1,0:T(8,128)(2,1)} %get-tuple-element.42), channel_id=1, source_target_pairs={{0,2},{1,3},{2,0},{3,1},{4,6},{5,7},{6,4},{7,5},{8,10},{9,11},{10,... | collective-permute-start | bytes 3145736 | tf_op jit(solution)/shard_map/ppermute | solution.py:584
  5.9 54.4 %collective-permute-start.5 = (bf16[4,8,16,1024]{3,2,1,0:T(8,128)(2,1)}, bf16[4,8,16,1024]{3,2,1,0:T(8,128)(2,1)}, u32[]{:S(2)}, u32[]{:S(2)}) collective-permute-start(bf16[4,8,16,1024]{3,2,1,0:T(8,128)(2,1)} %get-tuple-element.43), channel_id=1, source_target_pairs={{0,4},{1,5},{2,6},{3,7},{4,0},{5,1},{6,2},{7,3},{8,12},{9,13},{10,... | collective-permute-start | bytes 3145736 | tf_op jit(solution)/shard_map/ppermute | solution.py:584
  7.2 24.9 %collective-permute-start.3 = (bf16[4,8,16,1024]{3,2,1,0:T(8,128)(2,1)}, bf16[4,8,16,1024]{3,2,1,0:T(8,128)(2,1)}, u32[]{:S(2)}, u32[]{:S(2)}) collective-permute-start(bf16[4,8,16,1024]{3,2,1,0:T(8,128)(2,1)} %get-tuple-element.43), channel_id=1, source_target_pairs={{0,1},{1,0},{2,3},{3,2},{4,5},{5,4},{6,7},{7,6},{8,9},{9,8},{10,11... | collective-permute-start | bytes 3145736 | tf_op jit(solution)/shard_map/ppermute | solution.py:584
  7.8 21.6 %copy-start = (s32[32]{0:T(128)S(1)}, s32[32]{0:T(128)}, u32[]{:S(2)}) copy-start(s32[32]{0:T(128)} %param.12) | copy-start | bytes 388
  7.8 43.9 %collective-permute-start = (bf16[4,8,16,1024]{3,2,1,0:T(8,128)(2,1)}, bf16[4,8,16,1024]{3,2,1,0:T(8,128)(2,1)}, u32[]{:S(2)}, u32[]{:S(2)}) collective-permute-start(bf16[4,8,16,1024]{3,2,1,0:T(8,128)(2,1)} %get-tuple-element.36), channel_id=1, source_target_pairs={{0,2},{1,3},{2,0},{3,1},{4,6},{5,7},{6,4},{7,5},{8,10},{9,11},{10,... | collective-permute-start | bytes 3145736 | tf_op jit(solution)/shard_map/ppermute | solution.py:584
  9.1 44.1 %collective-permute-start.1 = (bf16[4,8,16,1024]{3,2,1,0:T(8,128)(2,1)}, bf16[4,8,16,1024]{3,2,1,0:T(8,128)(2,1)}, u32[]{:S(2)}, u32[]{:S(2)}) collective-permute-start(bf16[4,8,16,1024]{3,2,1,0:T(8,128)(2,1)} %get-tuple-element.41), channel_id=1, source_target_pairs={{0,4},{1,5},{2,6},{3,7},{4,0},{5,1},{6,2},{7,3},{8,12},{9,13},{10,... | collective-permute-start | bytes 3145736 | tf_op jit(solution)/shard_map/ppermute | solution.py:584
  32.1 34.5 %collective-permute-start.7 = (bf16[4,8,16,1024]{3,2,1,0:T(8,128)(2,1)}, bf16[4,8,16,1024]{3,2,1,0:T(8,128)(2,1)}, u32[]{:S(2)}, u32[]{:S(2)}) collective-permute-start(bf16[4,8,16,1024]{3,2,1,0:T(8,128)(2,1)} %get-tuple-element.41), channel_id=1, source_target_pairs={{1,2},{2,1},{5,6},{6,5},{9,10},{10,9},{13,14},{14,13},{17,18},{18,... | collective-permute-start | bytes 3145736 | tf_op jit(solution)/shard_map/ppermute | solution.py:630
  53.2 18.0 %collective-permute-start.6 = (bf16[4,8,16,1024]{3,2,1,0:T(8,128)(2,1)}, bf16[4,8,16,1024]{3,2,1,0:T(8,128)(2,1)}, u32[]{:S(2)}, u32[]{:S(2)}) collective-permute-start(bf16[4,8,16,1024]{3,2,1,0:T(8,128)(2,1)} %collective-permute-done.rest_0_.refs_5_), channel_id=1, source_target_pairs={{3,2},{0,1},{1,4},{6,3},{7,6},{4,5},{5,8},{10,7},{11,10},{8,9},{9,... | collective-permute-start | bytes 3145736 | tf_op jit(solution)/shard_map/ppermute | solution.py:634
  56.2 17.4 %collective-permute-start.8 = (bf16[4,8,16,1024]{3,2,1,0:T(8,128)(2,1)}, bf16[4,8,16,1024]{3,2,1,0:T(8,128)(2,1)}, u32[]{:S(2)}, u32[]{:S(2)}) collective-permute-start(bf16[4,8,16,1024]{3,2,1,0:T(8,128)(2,1)} %collective-permute-done.1.rest_1_.refs_6_), channel_id=1, source_target_pairs={{7,4},{0,3},{3,8},{12,7},{15,12},{8,11},{11,16},{20,15},{23,20},{1... | collective-permute-start | bytes 3145736 | tf_op jit(solution)/shard_map/ppermute | solution.py:633
  66.1 33.0 %collective-permute-start.13 = (bf16[16,4,16,1024]{3,2,1,0:T(8,128)(2,1)}, bf16[16,4,16,1024]{3,2,1,0:T(8,128)(2,1)}, u32[]{:S(2)}, u32[]{:S(2)}) collective-permute-start(bf16[16,4,16,1024]{3,2,1,0:T(8,128)(2,1)} %get-tuple-element.62), channel_id=1, source_target_pairs={{0,1},{1,0},{2,3},{3,2},{4,5},{5,4},{6,7},{7,6},{8,9},{9,8},{10,11... | collective-permute-start | bytes 6291464 | tf_op jit(solution)/shard_map/ppermute | solution.py:584
  66.2 28.5 %collective-permute-start.11 = (bf16[8,4,16,1024]{3,2,1,0:T(8,128)(2,1)}, bf16[8,4,16,1024]{3,2,1,0:T(8,128)(2,1)}, u32[]{:S(2)}, u32[]{:S(2)}) collective-permute-start(bf16[8,4,16,1024]{3,2,1,0:T(8,128)(2,1)} %get-tuple-element.60), channel_id=1, source_target_pairs={{0,4},{1,5},{2,6},{3,7},{4,0},{5,1},{6,2},{7,3},{8,12},{9,13},{10,... | collective-permute-start | bytes 3145736 | tf_op jit(solution)/shard_map/ppermute | solution.py:584
  73.6 25.5 %collective-permute-start.9 = (bf16[8,4,16,1024]{3,2,1,0:T(8,128)(2,1)}, bf16[8,4,16,1024]{3,2,1,0:T(8,128)(2,1)}, u32[]{:S(2)}, u32[]{:S(2)}) collective-permute-start(bf16[8,4,16,1024]{3,2,1,0:T(8,128)(2,1)} %get-tuple-element.52), channel_id=1, source_target_pairs={{0,2},{1,3},{2,0},{3,1},{4,6},{5,7},{6,4},{7,5},{8,10},{9,11},{10,... | collective-permute-start | bytes 3145736 | tf_op jit(solution)/shard_map/ppermute | solution.py:584
  91.8 29.6 %collective-permute-start.10 = (bf16[8,4,16,1024]{3,2,1,0:T(8,128)(2,1)}, bf16[8,4,16,1024]{3,2,1,0:T(8,128)(2,1)}, u32[]{:S(2)}, u32[]{:S(2)}) collective-permute-start(bf16[8,4,16,1024]{3,2,1,0:T(8,128)(2,1)} %get-tuple-element.59), channel_id=1, source_target_pairs={{0,3},{1,2},{2,1},{3,0},{4,7},{5,6},{6,5},{7,4},{8,11},{9,10},{10,... | collective-permute-start | bytes 3145736 | tf_op jit(solution)/shard_map/ppermute | solution.py:584
  92.8 28.5 %collective-permute-start.12 = (bf16[8,4,16,1024]{3,2,1,0:T(8,128)(2,1)}, bf16[8,4,16,1024]{3,2,1,0:T(8,128)(2,1)}, u32[]{:S(2)}, u32[]{:S(2)}) collective-permute-start(bf16[8,4,16,1024]{3,2,1,0:T(8,128)(2,1)} %get-tuple-element.61), channel_id=1, source_target_pairs={{0,5},{1,4},{2,7},{3,6},{4,1},{5,0},{6,3},{7,2},{8,13},{9,12},{10,... | collective-permute-start | bytes 3145736 | tf_op jit(solution)/shard_map/ppermute | solution.py:584

commit v9 on v8

--- a/solution.py
+++ b/solution.py
@@ -106,28 +106,34 @@
         store.wait()
 
 
-def halves_kernel(start, tok_ref, rim_ref, off_ref, bounce, sems):
-    deep = rim_ref.shape[0]
+def halves_kernel(picks, tok_ref, *rest):
+    outs, bounce, sems = rest[: len(picks)], rest[-2], rest[-1]
+    deep = outs[0].shape[0]
     part = lax.axis_index("tile") & 1
     bite = deep // 2
     pairs = []
-    for u, out in ((1 - part, off_ref), (part, rim_ref)):
+    for (rim, start), out in zip(picks, outs):
+        u = part if rim else 1 - part
         for k in range(0, deep, bite):
             pairs.append((tok_ref.at[u, start + k : start + k + bite], out.at[k : k + bite]))
     copy_through(pairs, bounce, sems)
 
 
-def split_half(start, tok):
+def split_halves(picks, tok):
     halves, deep, wide, run, feat = tok.shape
     part = (deep // 2, wide, run, feat)
+    count = len(picks)
     anym = pl.BlockSpec(memory_space=pl.ANY)
     return pl.pallas_call(
-        functools.partial(halves_kernel, start),
-        out_shape=[jax.ShapeDtypeStruct(part, tok.dtype)] * 2,
+        functools.partial(halves_kernel, picks),
+        out_shape=[jax.ShapeDtypeStruct(part, tok.dtype)] * count,
         in_specs=[anym],
-        out_specs=[anym] * 2,
-        scratch_shapes=[pltpu.VMEM((4, part[0] // 2) + part[1:], tok.dtype), pltpu.SemaphoreType.DMA((2, 4))],
-        cost_estimate=pl.CostEstimate(flops=0, bytes_accessed=8 << 20, transcendentals=0),
+        out_specs=[anym] * count,
+        scratch_shapes=[
+            pltpu.VMEM((2 * count, part[0] // 2) + part[1:], tok.dtype),
+            pltpu.SemaphoreType.DMA((2, 2 * count)),
+        ],
+        cost_estimate=pl.CostEstimate(flops=0, bytes_accessed=count << 21, transcendentals=0),
     )(tok)
 
 
@@ -368,7 +374,7 @@
     tile_ref, panel_ref, valid_ref, half_ref, tok_ref = refs[:5]
     recv = refs[5 : 5 + recv_count]
     q_ref, mix_a, mix_b, gain_ref, wqkv_ref, wproj_ref = refs[5 + recv_count : 11 + recv_count]
-    out_ref, got, q_s, own_s, res_s, wkv_s, wp_s, normed_s, kv_s, mixed_s, seen, ids, w_sem, sems = refs[-14:]
+    out_ref, got, q_s, own_s, res_s, wkv_s, wp_s, normed_s, kv_s, mixed_s, seen, ids, slots, w_sem, sems = refs[-15:]
     panels, deep, run, feat = got.shape
     half = panels // 2
     cut = deep // 2
@@ -378,47 +384,61 @@
     for t in range(tiles):
         seen[t] = 0
 
-    def fetch(p, count):
+    def record(p, count):
         r = tile_ref[0, me, p] ^ me
         hit = ((wanted >> r) & 1) == 1
 
         @pl.when(hit)
         def _():
             ids[count] = p
-            j = panel_ref[0, me, p]
-            for k, pick in parts.items():
-
-                @pl.when(r == k)
-                def _(pick=pick):
-                    for ref, rows, k in zip(pick(j, seen), (slice(0, cut), slice(cut, deep)), (0, 4)):
-                        if not isinstance(ref, list):
-                            pltpu.make_async_copy(ref, got.at[count, rows], sems.at[k, count]).start()
-                            continue
-                        for mine, choice in ref:
-
-                            @pl.when((j // half == (me & 1)) == mine)
-                            def _(choice=choice, rows=rows, k=k):
-                                pltpu.make_async_copy(choice, got.at[count, rows], sems.at[k, count]).start()
-
-            u = p // half
-            w = p % half
-            pltpu.make_async_copy(q_ref.at[u, :, w], q_s.at[count], sems.at[1, count]).start()
-
-            @pl.when(u == half_ref[0])
-            def _():
-                pltpu.make_async_copy(mix_a.at[:, w], own_s.at[count], sems.at[2, count]).start()
-
-            @pl.when(u != half_ref[0])
-            def _():
-                pltpu.make_async_copy(mix_b.at[:, w], own_s.at[count], sems.at[2, count]).start()
+            for t in range(tiles):
+                slots[count, t] = seen[t]
 
         seen[r] = seen[r] + 1
         return count + hit.astype(jnp.int32)
+
+    def fetch(n):
+        p = ids[n]
+        j = panel_ref[0, me, p]
+        r = tile_ref[0, me, p] ^ me
+        for k, pick in parts.items():
+
+            @pl.when(r == k)
+            def _(pick=pick):
+                for ref, rows, k in zip(pick(j, slots.at[n]), (slice(0, cut), slice(cut, deep)), (0, 4)):
+                    if not isinstance(ref, list):
+                        pltpu.make_async_copy(ref, got.at[n, rows], sems.at[k, n]).start()
+                        continue
+                    for mine, choice in ref:
+
+                        @pl.when((j // half == (me & 1)) == mine)
+                        def _(choice=choice, rows=rows, k=k):
+                            pltpu.make_async_copy(choice, got.at[n, rows], sems.at[k, n]).start()
+
+        u = p // half
+        w = p % half
+        pltpu.make_async_copy(q_ref.at[u, :, w], q_s.at[n], sems.at[1, n]).start()
+
+        @pl.when(u == half_ref[0])
+        def _():
+            pltpu.make_async_copy(mix_a.at[:, w], own_s.at[n], sems.at[2, n]).start()
+
+        @pl.when(u != half_ref[0])
+        def _():
+            pltpu.make_async_copy(mix_b.at[:, w], own_s.at[n], sems.at[2, n]).start()
+
+    def fetch_unit(n):
+        def one(i, carry):
+            fetch(i)
+            return carry
+
+        lax.fori_loop(2 * n, jnp.minimum(2 * n + 2, total), one, 0)
 
     load_wkv = pltpu.make_async_copy(wqkv_ref.at[:, feat:], wkv_s, w_sem.at[0])
     load_wp = pltpu.make_async_copy(wproj_ref, wp_s, w_sem.at[1])
     load_wkv.start()
-    total = lax.fori_loop(0, panels, fetch, jnp.int32(0))
+    total = lax.fori_loop(0, panels, record, jnp.int32(0))
+    fetch_unit(0)
     load_wp.start()
 
     pair = 2 * head_width
@@ -448,6 +468,7 @@
         def _():
             load_wkv.wait()
 
+        fetch_unit(n + 1)
         kv_s[...] = dot_f32(normed_s[...], wkv_s[...]).astype(jnp.bfloat16)
 
         @pl.when(n == 0)
@@ -547,6 +568,7 @@
             pltpu.VMEM((2 * length, feat), jnp.bfloat16),
             pltpu.SMEM((tiles,), jnp.int32),
             pltpu.SMEM((panels,), jnp.int32),
+            pltpu.SMEM((panels, tiles), jnp.int32),
             pltpu.SemaphoreType.DMA((2,)),
             pltpu.SemaphoreType.DMA((5, panels)),
         ],
@@ -618,10 +640,11 @@
             else:
                 links_c += [(low ^ 4, low + 1), ((low + 1) ^ 4, low)]
 
-        rim_x, off_x = split_half(0, tok)
+        cut = tok.shape[1] // 2
+        (off_x,) = split_halves(((False, 0),), tok)
         tok_next, off_x = fence((tok, off_x))
-        rim_y, off_y = split_half(tok.shape[1] // 2, tok_next)
-        rim_y, off_y, gain_next = fence((rim_y, off_y, gain_row))
+        off_y, rim_x, rim_y = split_halves(((False, cut), (True, 0), (True, cut)), tok_next)
+        rim_x, rim_y, off_y, gain_next = fence((rim_x, rim_y, off_y, gain_row))
         near = (xor(off_x, 1), xor(off_y, 1))
         own_rim = rim_y
         rim_x, rim_y = xor(rim_x, 2), xor(rim_y, 4)

time: 141 us -> 140 us (level)
  waiting for transfers between devices: 16.7 us -> 11.7 us
  Pallas kernels: 104 us -> 107 us
    ppermute x11, waiting for transfers between devices: 9.66 us -> 5.26 us  [xor(): return lax.ppermute(block, 'tile', [(i, i ^ bits) for i in range(tiles)])]
    pallas_call x2, Pallas kernels: 36.7 us -> 39.3 us  [cross_and_project(): pl.pallas_call(kernel, out_shape=jax.ShapeDtypeStruct(tok.shape, jnp.bflo...]
  transfers between devices with their start and end apart: 14 -> 14, of which waited for: 5 -> 4; matrix products, arithmetic and copies ran while one was open for 1% -> 1% of each run, Pallas kernels for 59% -> 65%
where the time goes in v9:
time: 140 us; the launch traced here: 138 us
  Pallas kernels  107 us (76%)
  starting transfers between devices  16.9 us (12%)
  waiting for transfers between devices  11.7 us (8%)
  between operations  1.53 us (1%)
    pallas_call x2, Pallas kernels, cross_and_project(): pl.pallas_call(kernel, out_shape=jax.ShapeDtypeStruct(tok.shape, jnp.bflo...  39.3 us
    pallas_call x2, Pallas kernels, window_mix(): pl.pallas_call(functools.partial(window_kernel, head_width), out_shape=ja...  36.2 us
    pallas_call x1, Pallas kernels, project_own(): pl.pallas_call(qkv_kernel, grid=(halves * 2,), out_shape=[jax.ShapeDtypeS...  20.2 us
    ppermute x11, starting transfers between devices, xor(): return lax.ppermute(block, 'tile', [(i, i ^ bits) for i in range(tiles)])  8.07 us
    pallas_call x1, Pallas kernels, pack_far(): pl.pallas_call(functools.partial(far_kernel, cap), out_shape=[jax.ShapeDt...  6.08 us
    ppermute x11, waiting for transfers between devices, xor(): return lax.ppermute(block, 'tile', [(i, i ^ bits) for i in range(tiles)])  5.26 us
    pallas_call x2, Pallas kernels, split_halves(): pl.pallas_call(functools.partial(halves_kernel, picks), out_shape=[jax.Sh...  4.86 us
    ppermute x1, waiting for transfers between devices, per_device(): edge_a = lax.ppermute(rim_x, ('scene', 'tile'), links_a)  4.15 us
  transfers between devices with their start and end apart: 14, of which 4 were waited for; matrix products, arithmetic and copies ran while one was open for 1% of the time, Pallas kernels for 65%

profile of v9, /device:TPU:11, one launch (start us, length us, event | category | flops | bytes accessed | tf_op | source)
XLA Modules:
  0.0 138.0 jit_solution(15536041764388853578)
XLA Ops:
  0.0 2.1 %shard_map.82 = bf16[4,8,16,1024]{3,2,1,0:T(8,128)(2,1)} custom-call(bf16[2,8,8,16,1024]{4,3,2,1,0:T(8,128)(2,1)} %bitcast.11), custom_call_target="tpu_custom_call" | custom-call | bytes 2097152 | tf_op jit(solution)/shard_map/pallas_call | solution.py:127
  2.1 0.7 collective-permute-start.2
  3.1 2.8 %shard_map.83 = (bf16[4,8,16,1024]{3,2,1,0:T(8,128)(2,1)}, bf16[4,8,16,1024]{3,2,1,0:T(8,128)(2,1)}, bf16[4,8,16,1024]{3,2,1,0:T(8,128)(2,1)}) custom-call(bf16[2,8,8,16,1024]{4,3,2,1,0:T(8,128)(2,1)} %bitcast.12), custom_call_target="tpu_custom_call" | custom-call | bytes 6291456 | tf_op jit(solution)/shard_map/pallas_call | solution.py:127
  5.9 1.3 collective-permute-start.5
  7.2 0.6 collective-permute-start.3
  7.8 1.2 collective-permute-start
  9.3 20.2 %shard_map.84 = (bf16[2,8,8,16,1024]{4,3,2,1,0:T(8,128)(2,1)}, bf16[2,8,8,16,2048]{4,3,2,1,0:T(8,128)(2,1)}) custom-call(bf16[2,8,8,16,1024]{4,3,2,1,0:T(8,128)(2,1)} %bitcast.13, bf16[1024]{0:T(1024)(128)(2,1)} %refs_17_.3, bf16[1024,3072]{1,0:T(8,128)(2,1)} %refs_18_.3), custom_call_target="tpu_custom_call" | custom-call | flops 12884901888 | bytes 23068672 | tf_op jit(solution)/shard_map/pallas_call | solution.py:238
  29.5 0.6 fusion
  31.3 0.7 add_add_fusion
  32.0 1.7 %collective-permute-start.7 = (bf16[4,8,16,1024]{3,2,1,0:T(8,128)(2,1)}, bf16[4,8,16,1024]{3,2,1,0:T(8,128)(2,1)}, u32[]{:S(2)}, u32[]{:S(2)}) collective-permute-start(bf16[4,8,16,1024]{3,2,1,0:T(8,128)(2,1)} %get-tuple-element.41), channel_id=1, source_target_pairs={{1,2},{2,1},{5,6},{6,5},{9,10},{10,9},{13,14},{14,13},{17,18},{18,... | collective-permute-start | bytes 3145736 | tf_op jit(solution)/shard_map/ppermute | solution.py:653
  33.7 18.0 %shard_map.85.refs_15_ = bf16[8,8,16,1024]{3,2,1,0:T(8,128)(2,1)} custom-call(s32[3]{0:T(128)} %get-tuple-element.35.half_ref.refs_3_, bf16[4,8,16,1024]{3,2,1,0:T(8,128)(2,1)} %collective-permute-done.2.refs_0_, bf16[4,8,16,1024]{3,2,1,0:T(8,128)(2,1)} %collective-permute-done.3.refs_1_, ...), custom_call_target="tpu_custom_call" | custom-call | flops 6442450944 | bytes 16777216 | tf_op jit(solution)/shard_map/pallas_call | solution.py:314
  51.7 1.4 %collective-permute-done.1.rest_1_.refs_6_ = bf16[4,8,16,1024]{3,2,1,0:T(8,128)(2,1)} collective-permute-done((bf16[4,8,16,1024]{3,2,1,0:T(8,128)(2,1)}, bf16[4,8,16,1024]{3,2,1,0:T(8,128)(2,1)}, u32[]{:S(2)}, u32[]{:S(2)}) %collective-permute-start.1) | collective-permute-done | bytes 1048608 | tf_op jit(solution)/shard_map/ppermute | solution.py:606
  53.1 3.1 %collective-permute-start.6 = (bf16[4,8,16,1024]{3,2,1,0:T(8,128)(2,1)}, bf16[4,8,16,1024]{3,2,1,0:T(8,128)(2,1)}, u32[]{:S(2)}, u32[]{:S(2)}) collective-permute-start(bf16[4,8,16,1024]{3,2,1,0:T(8,128)(2,1)} %collective-permute-done.rest_0_.refs_5_), channel_id=1, source_target_pairs={{3,2},{0,1},{1,4},{6,3},{7,6},{4,5},{5,8},{10,7},{11,10},{8,9},{9,... | collective-permute-start | bytes 3145736 | tf_op jit(solution)/shard_map/ppermute | solution.py:657
  56.2 4.0 %collective-permute-start.8 = (bf16[4,8,16,1024]{3,2,1,0:T(8,128)(2,1)}, bf16[4,8,16,1024]{3,2,1,0:T(8,128)(2,1)}, u32[]{:S(2)}, u32[]{:S(2)}) collective-permute-start(bf16[4,8,16,1024]{3,2,1,0:T(8,128)(2,1)} %collective-permute-done.1.rest_1_.refs_6_), channel_id=1, source_target_pairs={{7,4},{0,3},{3,8},{12,7},{15,12},{8,11},{11,16},{20,15},{23,20},{1... | collective-permute-start | bytes 3145736 | tf_op jit(solution)/shard_map/ppermute | solution.py:656
  60.3 6.1 %shard_map.86 = (bf16[8,4,16,1024]{3,2,1,0:T(8,128)(2,1)}, bf16[8,4,16,1024]{3,2,1,0:T(8,128)(2,1)}, bf16[8,4,16,1024]{3,2,1,0:T(8,128)(2,1)}, bf16[8,4,16,1024]{3,2,1,0:T(8,128)(2,1)}, bf16[16,4,16,1024]{3,2,1,0:T(8,128)(2,1)}) custom-call(s32[1,8,16]{2,1,0:T(8,128)} %bitcast.17, s32[1,8,16]{2,1,0:T(8,128)} %refs_1_.3, ...), custom_call_target="tpu_custom_call" | custom-call | bytes 6291456 | tf_op jit(solution)/shard_map/pallas_call | solution.py:208
  66.5 0.3 collective-permute-start.11
  66.8 4.1 %collective-permute-done.6.refs_0_ = bf16[4,8,16,1024]{3,2,1,0:T(8,128)(2,1)} collective-permute-done((bf16[4,8,16,1024]{3,2,1,0:T(8,128)(2,1)}, bf16[4,8,16,1024]{3,2,1,0:T(8,128)(2,1)}, u32[]{:S(2)}, u32[]{:S(2)}) %collective-permute-start.6) | collective-permute-done | bytes 1048608 | tf_op jit(solution)/shard_map/ppermute | solution.py:657
  70.9 2.3 %collective-permute-done.8.refs_2_ = bf16[4,8,16,1024]{3,2,1,0:T(8,128)(2,1)} collective-permute-done((bf16[4,8,16,1024]{3,2,1,0:T(8,128)(2,1)}, bf16[4,8,16,1024]{3,2,1,0:T(8,128)(2,1)}, u32[]{:S(2)}, u32[]{:S(2)}) %collective-permute-start.8) | collective-permute-done | bytes 1048608 | tf_op jit(solution)/shard_map/ppermute | solution.py:656
  73.3 18.1 %shard_map.87.refs_16_ = bf16[8,8,16,1024]{3,2,1,0:T(8,128)(2,1)} custom-call(s32[3]{0:T(128)} %get-tuple-element.55.half_ref, bf16[4,8,16,1024]{3,2,1,0:T(8,128)(2,1)} %collective-permute-done.6.refs_0_, bf16[4,8,16,1024]{3,2,1,0:T(8,128)(2,1)} %collective-permute-done.7.refs_1_, bf16[4,8,16,1024]{3,2,1,0:T(8,128)(2,1)} %collective-permute-done.8.refs_2_, ...), custom_call_target="tpu_custom_call" | custom-call | flops 6442450944 | bytes 16777216 | tf_op jit(solution)/shard_map/pallas_call | solution.py:314
  91.4 1.4 %collective-permute-start.10 = (bf16[8,4,16,1024]{3,2,1,0:T(8,128)(2,1)}, bf16[8,4,16,1024]{3,2,1,0:T(8,128)(2,1)}, u32[]{:S(2)}, u32[]{:S(2)}) collective-permute-start(bf16[8,4,16,1024]{3,2,1,0:T(8,128)(2,1)} %get-tuple-element.59), channel_id=1, source_target_pairs={{0,3},{1,2},{2,1},{3,0},{4,7},{5,6},{6,5},{7,4},{8,11},{9,10},{10,... | collective-permute-start | bytes 3145736 | tf_op jit(solution)/shard_map/ppermute | solution.py:606
  92.8 1.9 %collective-permute-start.12 = (bf16[8,4,16,1024]{3,2,1,0:T(8,128)(2,1)}, bf16[8,4,16,1024]{3,2,1,0:T(8,128)(2,1)}, u32[]{:S(2)}, u32[]{:S(2)}) collective-permute-start(bf16[8,4,16,1024]{3,2,1,0:T(8,128)(2,1)} %get-tuple-element.61), channel_id=1, source_target_pairs={{0,5},{1,4},{2,7},{3,6},{4,1},{5,0},{6,3},{7,2},{8,13},{9,12},{10,... | collective-permute-start | bytes 3145736 | tf_op jit(solution)/shard_map/ppermute | solution.py:606
  94.7 3.8 %collective-permute-done.9.refs_9_ = bf16[8,4,16,1024]{3,2,1,0:T(8,128)(2,1)} collective-permute-done((bf16[8,4,16,1024]{3,2,1,0:T(8,128)(2,1)}, bf16[8,4,16,1024]{3,2,1,0:T(8,128)(2,1)}, u32[]{:S(2)}, u32[]{:S(2)}) %collective-permute-start.9) | collective-permute-done | bytes 1048608 | tf_op jit(solution)/shard_map/ppermute | solution.py:606
  98.5 24.7 %shard_map.88.refs_20_ = bf16[2,8,8,16,1024]{4,3,2,1,0:T(8,128)(2,1)} custom-call(s32[1,8,16]{2,1,0:T(8,128)} %bitcast.18, s32[1,8,16]{2,1,0:T(8,128)} %refs_1_.3, s32[16]{0:T(128)} %bitcast.20, s32[3]{0:T(128)} %get-tuple-element.35.half_ref.refs_3_, bf16[2,8,8,16,1024]{4,3,2,1,0:T(8,128)(2,1)} %bitcast.15, ...), custom_call_target="tpu_custom_call" | custom-call | flops 9395240960 | bytes 16777216 | tf_op jit(solution)/shard_map/pallas_call | solution.py:554
  123.2 14.6 %shard_map.89 = bf16[2,8,8,16,1024]{4,3,2,1,0:T(8,128)(2,1)} custom-call(s32[1,8,16]{2,1,0:T(8,128)} %bitcast.19, s32[1,8,16]{2,1,0:T(8,128)} %refs_1_.3, s32[16]{0:T(128)} %bitcast.21, s32[3]{0:T(128)} %get-tuple-element.35.half_ref.refs_3_, bf16[2,8,8,16,1024]{4,3,2,1,0:T(8,128)(2,1)} %bitcast.16, ...), custom_call_target="tpu_custom_call", output_to_operand_aliasing={{}: (20, {})} | custom-call | flops 5637144576 | bytes 12582912 | tf_op jit(solution)/shard_map/pallas_call | solution.py:554
  (16 shorter events, 0.6 us)
Async XLA Ops:
  2.1 7.0 %collective-permute-start.2 = (bf16[4,8,16,1024]{3,2,1,0:T(8,128)(2,1)}, bf16[4,8,16,1024]{3,2,1,0:T(8,128)(2,1)}, u32[]{:S(2)}, u32[]{:S(2)}) collective-permute-start(bf16[4,8,16,1024]{3,2,1,0:T(8,128)(2,1)} %shard_map.82), channel_id=1, source_target_pairs={{0,1},{1,0},{2,3},{3,2},{4,5},{5,4},{6,7},{7,6},{8,9},{9,8},{10,11... | collective-permute-start | bytes 3145736 | tf_op jit(solution)/shard_map/ppermute | solution.py:606
  2.8 57.5 %collective-permute-start.4 = (bf16[4,8,16,1024]{3,2,1,0:T(8,128)(2,1)}, bf16[4,8,16,1024]{3,2,1,0:T(8,128)(2,1)}, u32[]{:S(2)}, u32[]{:S(2)}) collective-permute-start(bf16[4,8,16,1024]{3,2,1,0:T(8,128)(2,1)} %shard_map.82), channel_id=1, source_target_pairs={{0,2},{1,3},{2,0},{3,1},{4,6},{5,7},{6,4},{7,5},{8,10},{9,11},{10,... | collective-permute-start | bytes 3145736 | tf_op jit(solution)/shard_map/ppermute | solution.py:606
  5.9 23.6 %copy-start = (s32[32]{0:T(128)S(1)}, s32[32]{0:T(128)}, u32[]{:S(2)}) copy-start(s32[32]{0:T(128)} %param.12) | copy-start | bytes 388
  5.9 54.4 %collective-permute-start.5 = (bf16[4,8,16,1024]{3,2,1,0:T(8,128)(2,1)}, bf16[4,8,16,1024]{3,2,1,0:T(8,128)(2,1)}, u32[]{:S(2)}, u32[]{:S(2)}) collective-permute-start(bf16[4,8,16,1024]{3,2,1,0:T(8,128)(2,1)} %get-tuple-element.43), channel_id=1, source_target_pairs={{0,4},{1,5},{2,6},{3,7},{4,0},{5,1},{6,2},{7,3},{8,12},{9,13},{10,... | collective-permute-start | bytes 3145736 | tf_op jit(solution)/shard_map/ppermute | solution.py:606
  7.2 24.8 %collective-permute-start.3 = (bf16[4,8,16,1024]{3,2,1,0:T(8,128)(2,1)}, bf16[4,8,16,1024]{3,2,1,0:T(8,128)(2,1)}, u32[]{:S(2)}, u32[]{:S(2)}) collective-permute-start(bf16[4,8,16,1024]{3,2,1,0:T(8,128)(2,1)} %get-tuple-element.43), channel_id=1, source_target_pairs={{0,1},{1,0},{2,3},{3,2},{4,5},{5,4},{6,7},{7,6},{8,9},{9,8},{10,11... | collective-permute-start | bytes 3145736 | tf_op jit(solution)/shard_map/ppermute | solution.py:606
  7.8 43.9 %collective-permute-start = (bf16[4,8,16,1024]{3,2,1,0:T(8,128)(2,1)}, bf16[4,8,16,1024]{3,2,1,0:T(8,128)(2,1)}, u32[]{:S(2)}, u32[]{:S(2)}) collective-permute-start(bf16[4,8,16,1024]{3,2,1,0:T(8,128)(2,1)} %get-tuple-element.40), channel_id=1, source_target_pairs={{0,2},{1,3},{2,0},{3,1},{4,6},{5,7},{6,4},{7,5},{8,10},{9,11},{10,... | collective-permute-start | bytes 3145736 | tf_op jit(solution)/shard_map/ppermute | solution.py:606
  9.0 44.1 %collective-permute-start.1 = (bf16[4,8,16,1024]{3,2,1,0:T(8,128)(2,1)}, bf16[4,8,16,1024]{3,2,1,0:T(8,128)(2,1)}, u32[]{:S(2)}, u32[]{:S(2)}) collective-permute-start(bf16[4,8,16,1024]{3,2,1,0:T(8,128)(2,1)} %get-tuple-element.41), channel_id=1, source_target_pairs={{0,4},{1,5},{2,6},{3,7},{4,0},{5,1},{6,2},{7,3},{8,12},{9,13},{10,... | collective-permute-start | bytes 3145736 | tf_op jit(solution)/shard_map/ppermute | solution.py:606
  32.0 34.8 %collective-permute-start.7 = (bf16[4,8,16,1024]{3,2,1,0:T(8,128)(2,1)}, bf16[4,8,16,1024]{3,2,1,0:T(8,128)(2,1)}, u32[]{:S(2)}, u32[]{:S(2)}) collective-permute-start(bf16[4,8,16,1024]{3,2,1,0:T(8,128)(2,1)} %get-tuple-element.41), channel_id=1, source_target_pairs={{1,2},{2,1},{5,6},{6,5},{9,10},{10,9},{13,14},{14,13},{17,18},{18,... | collective-permute-start | bytes 3145736 | tf_op jit(solution)/shard_map/ppermute | solution.py:653
  53.1 17.8 %collective-permute-start.6 = (bf16[4,8,16,1024]{3,2,1,0:T(8,128)(2,1)}, bf16[4,8,16,1024]{3,2,1,0:T(8,128)(2,1)}, u32[]{:S(2)}, u32[]{:S(2)}) collective-permute-start(bf16[4,8,16,1024]{3,2,1,0:T(8,128)(2,1)} %collective-permute-done.rest_0_.refs_5_), channel_id=1, source_target_pairs={{3,2},{0,1},{1,4},{6,3},{7,6},{4,5},{5,8},{10,7},{11,10},{8,9},{9,... | collective-permute-start | bytes 3145736 | tf_op jit(solution)/shard_map/ppermute | solution.py:657
  56.2 17.0 %collective-permute-start.8 = (bf16[4,8,16,1024]{3,2,1,0:T(8,128)(2,1)}, bf16[4,8,16,1024]{3,2,1,0:T(8,128)(2,1)}, u32[]{:S(2)}, u32[]{:S(2)}) collective-permute-start(bf16[4,8,16,1024]{3,2,1,0:T(8,128)(2,1)} %collective-permute-done.1.rest_1_.refs_6_), channel_id=1, source_target_pairs={{7,4},{0,3},{3,8},{12,7},{15,12},{8,11},{11,16},{20,15},{23,20},{1... | collective-permute-start | bytes 3145736 | tf_op jit(solution)/shard_map/ppermute | solution.py:656
  66.4 32.1 %collective-permute-start.13 = (bf16[16,4,16,1024]{3,2,1,0:T(8,128)(2,1)}, bf16[16,4,16,1024]{3,2,1,0:T(8,128)(2,1)}, u32[]{:S(2)}, u32[]{:S(2)}) collective-permute-start(bf16[16,4,16,1024]{3,2,1,0:T(8,128)(2,1)} %get-tuple-element.62), channel_id=1, source_target_pairs={{0,1},{1,0},{2,3},{3,2},{4,5},{5,4},{6,7},{7,6},{8,9},{9,8},{10,11... | collective-permute-start | bytes 6291464 | tf_op jit(solution)/shard_map/ppermute | solution.py:606
  66.5 28.2 %collective-permute-start.11 = (bf16[8,4,16,1024]{3,2,1,0:T(8,128)(2,1)}, bf16[8,4,16,1024]{3,2,1,0:T(8,128)(2,1)}, u32[]{:S(2)}, u32[]{:S(2)}) collective-permute-start(bf16[8,4,16,1024]{3,2,1,0:T(8,128)(2,1)} %get-tuple-element.60), channel_id=1, source_target_pairs={{0,4},{1,5},{2,6},{3,7},{4,0},{5,1},{6,2},{7,3},{8,12},{9,13},{10,... | collective-permute-start | bytes 3145736 | tf_op jit(solution)/shard_map/ppermute | solution.py:606
  73.3 25.2 %collective-permute-start.9 = (bf16[8,4,16,1024]{3,2,1,0:T(8,128)(2,1)}, bf16[8,4,16,1024]{3,2,1,0:T(8,128)(2,1)}, u32[]{:S(2)}, u32[]{:S(2)}) collective-permute-start(bf16[8,4,16,1024]{3,2,1,0:T(8,128)(2,1)} %get-tuple-element.52), channel_id=1, source_target_pairs={{0,2},{1,3},{2,0},{3,1},{4,6},{5,7},{6,4},{7,5},{8,10},{9,11},{10,... | collective-permute-start | bytes 3145736 | tf_op jit(solution)/shard_map/ppermute | solution.py:606
  91.4 31.8 %collective-permute-start.10 = (bf16[8,4,16,1024]{3,2,1,0:T(8,128)(2,1)}, bf16[8,4,16,1024]{3,2,1,0:T(8,128)(2,1)}, u32[]{:S(2)}, u32[]{:S(2)}) collective-permute-start(bf16[8,4,16,1024]{3,2,1,0:T(8,128)(2,1)} %get-tuple-element.59), channel_id=1, source_target_pairs={{0,3},{1,2},{2,1},{3,0},{4,7},{5,6},{6,5},{7,4},{8,11},{9,10},{10,... | collective-permute-start | bytes 3145736 | tf_op jit(solution)/shard_map/ppermute | solution.py:606
  92.8 30.4 %collective-permute-start.12 = (bf16[8,4,16,1024]{3,2,1,0:T(8,128)(2,1)}, bf16[8,4,16,1024]{3,2,1,0:T(8,128)(2,1)}, u32[]{:S(2)}, u32[]{:S(2)}) collective-permute-start(bf16[8,4,16,1024]{3,2,1,0:T(8,128)(2,1)} %get-tuple-element.61), channel_id=1, source_target_pairs={{0,5},{1,4},{2,7},{3,6},{4,1},{5,0},{6,3},{7,2},{8,13},{9,12},{10,... | collective-permute-start | bytes 3145736 | tf_op jit(solution)/shard_map/ppermute | solution.py:606

commit v10 on v9

--- a/solution.py
+++ b/solution.py
@@ -658,7 +658,7 @@
         sides = (rim_x, rim_y, off_x, off_y)
         x_same, y_same, x_cross, y_cross, rest = pack_far(tile_table, panel_table, tok, sides, cap)
         y_same, rest = xor(y_same, 4), xor(rest, 1)
-        edge_a, edge_b, edge_c, x_same, x_cross, y_cross = fence((edge_a, edge_b, edge_c, x_same, x_cross, y_cross))
+        edge_a, edge_c, x_same, x_cross, y_cross = fence((edge_a, edge_c, x_same, x_cross, y_cross))
         x_same = xor(x_same, 2)
         mix_far = window_mix(far_half, (edge_a, edge_b, edge_c), (0, 0, 0), q, kv, gain_row, w_qkv)
         x_cross, y_cross, mix_far = fence((x_cross, y_cross, mix_far))

time: 140 us -> 157 us (1.12)
  starting transfers between devices: 16.9 us -> 33.5 us
  Pallas kernels: 107 us -> 103 us
  waiting for transfers between devices: 11.7 us -> 14.2 us
    ppermute x11, starting transfers between devices: 8.07 us -> 24.8 us  [xor(): return lax.ppermute(block, 'tile', [(i, i ^ bits) for i in range(tiles)])]
    pallas_call x2, Pallas kernels: 39.3 us -> 36.2 us  [cross_and_project(): pl.pallas_call(kernel, out_shape=jax.ShapeDtypeStruct(tok.shape, jnp.bflo...]
    ppermute x11, waiting for transfers between devices: 5.26 us -> 8.19 us  [xor(): return lax.ppermute(block, 'tile', [(i, i ^ bits) for i in range(tiles)])]
    ppermute x1, waiting for transfers between devices: 4.15 us -> 2.01 us  [per_device(): edge_a = lax.ppermute(rim_x, ('scene', 'tile'), links_a)]
    ppermute x1, waiting for transfers between devices: 2.31 us -> 3.99 us  [per_device(): edge_c = lax.ppermute(rim_y, ('scene', 'tile'), links_c)]
  transfers between devices with their start and end apart: 14 -> 14, of which waited for: 4 -> 6; matrix products, arithmetic and copies ran while one was open for 1% -> 1% of each run, Pallas kernels for 65% -> 54%
where the time goes in v10:
time: 157 us; the launch traced here: 154 us
  Pallas kernels  103 us (66%)
  starting transfers between devices  33.5 us (21%)
  waiting for transfers between devices  14.2 us (9%)
    pallas_call x2, Pallas kernels, cross_and_project(): pl.pallas_call(kernel, out_shape=jax.ShapeDtypeStruct(tok.shape, jnp.bflo...  36.2 us
    pallas_call x2, Pallas kernels, window_mix(): pl.pallas_call(functools.partial(window_kernel, head_width), out_shape=ja...  36.1 us
    ppermute x11, starting transfers between devices, xor(): return lax.ppermute(block, 'tile', [(i, i ^ bits) for i in range(tiles)])  24.8 us
    pallas_call x1, Pallas kernels, project_own(): pl.pallas_call(qkv_kernel, grid=(halves * 2,), out_shape=[jax.ShapeDtypeS...  20.2 us
    ppermute x11, waiting for transfers between devices, xor(): return lax.ppermute(block, 'tile', [(i, i ^ bits) for i in range(tiles)])  8.19 us
    pallas_call x1, Pallas kernels, pack_far(): pl.pallas_call(functools.partial(far_kernel, cap), out_shape=[jax.ShapeDt...  6.05 us
    pallas_call x2, Pallas kernels, split_halves(): pl.pallas_call(functools.partial(halves_kernel, picks), out_shape=[jax.Sh...  4.86 us
    ppermute x1, starting transfers between devices, per_device(): edge_c = lax.ppermute(rim_y, ('scene', 'tile'), links_c)  4.03 us
  transfers between devices with their start and end apart: 14, of which 6 were waited for; matrix products, arithmetic and copies ran while one was open for 1% of the time, Pallas kernels for 54%

profile of v10, /device:TPU:11, one launch (start us, length us, event | category | flops | bytes accessed | tf_op | source)
XLA Modules:
  0.0 154.0 jit_solution(15887446250646339348)
XLA Ops:
  0.0 2.1 %shard_map.82 = bf16[4,8,16,1024]{3,2,1,0:T(8,128)(2,1)} custom-call(bf16[2,8,8,16,1024]{4,3,2,1,0:T(8,128)(2,1)} %bitcast.11), custom_call_target="tpu_custom_call" | custom-call | bytes 2097152 | tf_op jit(solution)/shard_map/pallas_call | solution.py:127
  2.1 0.7 collective-permute-start.2
  3.1 2.8 %shard_map.83 = (bf16[4,8,16,1024]{3,2,1,0:T(8,128)(2,1)}, bf16[4,8,16,1024]{3,2,1,0:T(8,128)(2,1)}, bf16[4,8,16,1024]{3,2,1,0:T(8,128)(2,1)}) custom-call(bf16[2,8,8,16,1024]{4,3,2,1,0:T(8,128)(2,1)} %bitcast.12), custom_call_target="tpu_custom_call" | custom-call | bytes 6291456 | tf_op jit(solution)/shard_map/pallas_call | solution.py:127
  5.9 1.3 collective-permute-start.5
  7.2 0.6 collective-permute-start.3
  7.8 1.2 collective-permute-start
  9.3 20.2 %shard_map.84 = (bf16[2,8,8,16,1024]{4,3,2,1,0:T(8,128)(2,1)}, bf16[2,8,8,16,2048]{4,3,2,1,0:T(8,128)(2,1)}) custom-call(bf16[2,8,8,16,1024]{4,3,2,1,0:T(8,128)(2,1)} %bitcast.13, bf16[1024]{0:T(1024)(128)(2,1)} %refs_17_.3, bf16[1024,3072]{1,0:T(8,128)(2,1)} %refs_18_.3), custom_call_target="tpu_custom_call" | custom-call | flops 12884901888 | bytes 23068672 | tf_op jit(solution)/shard_map/pallas_call | solution.py:238
  29.5 0.6 fusion
  31.3 0.7 add_add_fusion
  32.0 18.0 %shard_map.85.refs_15_ = bf16[8,8,16,1024]{3,2,1,0:T(8,128)(2,1)} custom-call(s32[3]{0:T(128)} %get-tuple-element.34.half_ref.refs_3_, bf16[4,8,16,1024]{3,2,1,0:T(8,128)(2,1)} %collective-permute-done.2.refs_0_, bf16[4,8,16,1024]{3,2,1,0:T(8,128)(2,1)} %collective-permute-done.3.refs_1_, ...), custom_call_target="tpu_custom_call" | custom-call | flops 6442450944 | bytes 16777216 | tf_op jit(solution)/shard_map/pallas_call | solution.py:314
  50.3 2.8 %collective-permute-done.1.rest_1_.refs_6_ = bf16[4,8,16,1024]{3,2,1,0:T(8,128)(2,1)} collective-permute-done((bf16[4,8,16,1024]{3,2,1,0:T(8,128)(2,1)}, bf16[4,8,16,1024]{3,2,1,0:T(8,128)(2,1)}, u32[]{:S(2)}, u32[]{:S(2)}) %collective-permute-start.1) | collective-permute-done | bytes 1048608 | tf_op jit(solution)/shard_map/ppermute | solution.py:606
  53.1 3.1 %collective-permute-start.6 = (bf16[4,8,16,1024]{3,2,1,0:T(8,128)(2,1)}, bf16[4,8,16,1024]{3,2,1,0:T(8,128)(2,1)}, u32[]{:S(2)}, u32[]{:S(2)}) collective-permute-start(bf16[4,8,16,1024]{3,2,1,0:T(8,128)(2,1)} %collective-permute-done.rest_0_.refs_5_), channel_id=1, source_target_pairs={{3,2},{0,1},{1,4},{6,3},{7,6},{4,5},{5,8},{10,7},{11,10},{8,9},{9,... | collective-permute-start | bytes 3145736 | tf_op jit(solution)/shard_map/ppermute | solution.py:657
  56.2 4.0 %collective-permute-start.7 = (bf16[4,8,16,1024]{3,2,1,0:T(8,128)(2,1)}, bf16[4,8,16,1024]{3,2,1,0:T(8,128)(2,1)}, u32[]{:S(2)}, u32[]{:S(2)}) collective-permute-start(bf16[4,8,16,1024]{3,2,1,0:T(8,128)(2,1)} %collective-permute-done.1.rest_1_.refs_6_), channel_id=1, source_target_pairs={{7,4},{0,3},{3,8},{12,7},{15,12},{8,11},{11,16},{20,15},{23,20},{1... | collective-permute-start | bytes 3145736 | tf_op jit(solution)/shard_map/ppermute | solution.py:656
  60.3 6.1 %shard_map.86 = (bf16[8,4,16,1024]{3,2,1,0:T(8,128)(2,1)}, bf16[8,4,16,1024]{3,2,1,0:T(8,128)(2,1)}, bf16[8,4,16,1024]{3,2,1,0:T(8,128)(2,1)}, bf16[8,4,16,1024]{3,2,1,0:T(8,128)(2,1)}, bf16[16,4,16,1024]{3,2,1,0:T(8,128)(2,1)}) custom-call(s32[1,8,16]{2,1,0:T(8,128)} %bitcast.17, s32[1,8,16]{2,1,0:T(8,128)} %refs_1_.3, ...), custom_call_target="tpu_custom_call" | custom-call | bytes 6291456 | tf_op jit(solution)/shard_map/pallas_call | solution.py:208
  66.4 1.6 %collective-permute-start.9 = (bf16[4,8,16,1024]{3,2,1,0:T(8,128)(2,1)}, bf16[4,8,16,1024]{3,2,1,0:T(8,128)(2,1)}, u32[]{:S(2)}, u32[]{:S(2)}) collective-permute-start(bf16[4,8,16,1024]{3,2,1,0:T(8,128)(2,1)} %get-tuple-element.40), channel_id=1, source_target_pairs={{1,2},{2,1},{5,6},{6,5},{9,10},{10,9},{13,14},{14,13},{17,18},{18,... | collective-permute-start | bytes 3145736 | tf_op jit(solution)/shard_map/ppermute | solution.py:653
  68.1 2.0 %collective-permute-done.6.refs_0_ = bf16[4,8,16,1024]{3,2,1,0:T(8,128)(2,1)} collective-permute-done((bf16[4,8,16,1024]{3,2,1,0:T(8,128)(2,1)}, bf16[4,8,16,1024]{3,2,1,0:T(8,128)(2,1)}, u32[]{:S(2)}, u32[]{:S(2)}) %collective-permute-start.6) | collective-permute-done | bytes 1048608 | tf_op jit(solution)/shard_map/ppermute | solution.py:657
  70.1 4.0 %collective-permute-done.7.refs_2_ = bf16[4,8,16,1024]{3,2,1,0:T(8,128)(2,1)} collective-permute-done((bf16[4,8,16,1024]{3,2,1,0:T(8,128)(2,1)}, bf16[4,8,16,1024]{3,2,1,0:T(8,128)(2,1)}, u32[]{:S(2)}, u32[]{:S(2)}) %collective-permute-start.7) | collective-permute-done | bytes 1048608 | tf_op jit(solution)/shard_map/ppermute | solution.py:656
  74.1 18.1 %shard_map.87.refs_16_ = bf16[8,8,16,1024]{3,2,1,0:T(8,128)(2,1)} custom-call(s32[3]{0:T(128)} %get-tuple-element.54.half_ref, bf16[4,8,16,1024]{3,2,1,0:T(8,128)(2,1)} %collective-permute-done.6.refs_0_, bf16[4,8,16,1024]{3,2,1,0:T(8,128)(2,1)} %collective-permute-done.9.refs_1_, bf16[4,8,16,1024]{3,2,1,0:T(8,128)(2,1)} %collective-permute-done.7.refs_2_, ...), custom_call_target="tpu_custom_call" | custom-call | flops 6442450944 | bytes 16777216 | tf_op jit(solution)/shard_map/pallas_call | solution.py:314
  92.3 0.6 collective-permute-start.10
  92.9 19.6 %collective-permute-start.12 = (bf16[8,4,16,1024]{3,2,1,0:T(8,128)(2,1)}, bf16[8,4,16,1024]{3,2,1,0:T(8,128)(2,1)}, u32[]{:S(2)}, u32[]{:S(2)}) collective-permute-start(bf16[8,4,16,1024]{3,2,1,0:T(8,128)(2,1)} %get-tuple-element.59), channel_id=1, source_target_pairs={{0,5},{1,4},{2,7},{3,6},{4,1},{5,0},{6,3},{7,2},{8,13},{9,12},{10,... | collective-permute-start | bytes 3145736 | tf_op jit(solution)/shard_map/ppermute | solution.py:606
  112.5 1.3 collective-permute-done.8.refs_9_
  113.9 18.2 %shard_map.88.refs_20_ = bf16[2,8,8,16,1024]{4,3,2,1,0:T(8,128)(2,1)} custom-call(s32[1,8,16]{2,1,0:T(8,128)} %bitcast.18, s32[1,8,16]{2,1,0:T(8,128)} %refs_1_.3, s32[16]{0:T(128)} %bitcast.20, s32[3]{0:T(128)} %get-tuple-element.34.half_ref.refs_3_, bf16[2,8,8,16,1024]{4,3,2,1,0:T(8,128)(2,1)} %bitcast.15, ...), custom_call_target="tpu_custom_call" | custom-call | flops 9395240960 | bytes 16777216 | tf_op jit(solution)/shard_map/pallas_call | solution.py:554
  132.1 3.7 %collective-permute-done.12.refs_12_ = bf16[8,4,16,1024]{3,2,1,0:T(8,128)(2,1)} collective-permute-done((bf16[8,4,16,1024]{3,2,1,0:T(8,128)(2,1)}, bf16[8,4,16,1024]{3,2,1,0:T(8,128)(2,1)}, u32[]{:S(2)}, u32[]{:S(2)}) %collective-permute-start.12) | collective-permute-done | bytes 1048608 | tf_op jit(solution)/shard_map/ppermute | solution.py:606
  135.8 18.0 %shard_map.89 = bf16[2,8,8,16,1024]{4,3,2,1,0:T(8,128)(2,1)} custom-call(s32[1,8,16]{2,1,0:T(8,128)} %bitcast.19, s32[1,8,16]{2,1,0:T(8,128)} %refs_1_.3, s32[16]{0:T(128)} %bitcast.21, s32[3]{0:T(128)} %get-tuple-element.34.half_ref.refs_3_, bf16[2,8,8,16,1024]{4,3,2,1,0:T(8,128)(2,1)} %bitcast.16, ...), custom_call_target="tpu_custom_call", output_to_operand_aliasing={{}: (20, {})} | custom-call | flops 5637144576 | bytes 12582912 | tf_op jit(solution)/shard_map/pallas_call | solution.py:554
  (16 shorter events, 1.0 us)
Async XLA Ops:
  2.1 7.0 %collective-permute-start.2 = (bf16[4,8,16,1024]{3,2,1,0:T(8,128)(2,1)}, bf16[4,8,16,1024]{3,2,1,0:T(8,128)(2,1)}, u32[]{:S(2)}, u32[]{:S(2)}) collective-permute-start(bf16[4,8,16,1024]{3,2,1,0:T(8,128)(2,1)} %shard_map.82), channel_id=1, source_target_pairs={{0,1},{1,0},{2,3},{3,2},{4,5},{5,4},{6,7},{7,6},{8,9},{9,8},{10,11... | collective-permute-start | bytes 3145736 | tf_op jit(solution)/shard_map/ppermute | solution.py:606
  2.8 57.5 %collective-permute-start.4 = (bf16[4,8,16,1024]{3,2,1,0:T(8,128)(2,1)}, bf16[4,8,16,1024]{3,2,1,0:T(8,128)(2,1)}, u32[]{:S(2)}, u32[]{:S(2)}) collective-permute-start(bf16[4,8,16,1024]{3,2,1,0:T(8,128)(2,1)} %shard_map.82), channel_id=1, source_target_pairs={{0,2},{1,3},{2,0},{3,1},{4,6},{5,7},{6,4},{7,5},{8,10},{9,11},{10,... | collective-permute-start | bytes 3145736 | tf_op jit(solution)/shard_map/ppermute | solution.py:606
  5.9 23.6 %copy-start = (s32[32]{0:T(128)S(1)}, s32[32]{0:T(128)}, u32[]{:S(2)}) copy-start(s32[32]{0:T(128)} %param.12) | copy-start | bytes 388
  5.9 54.4 %collective-permute-start.5 = (bf16[4,8,16,1024]{3,2,1,0:T(8,128)(2,1)}, bf16[4,8,16,1024]{3,2,1,0:T(8,128)(2,1)}, u32[]{:S(2)}, u32[]{:S(2)}) collective-permute-start(bf16[4,8,16,1024]{3,2,1,0:T(8,128)(2,1)} %get-tuple-element.42), channel_id=1, source_target_pairs={{0,4},{1,5},{2,6},{3,7},{4,0},{5,1},{6,2},{7,3},{8,12},{9,13},{10,... | collective-permute-start | bytes 3145736 | tf_op jit(solution)/shard_map/ppermute | solution.py:606
  7.2 24.8 %collective-permute-start.3 = (bf16[4,8,16,1024]{3,2,1,0:T(8,128)(2,1)}, bf16[4,8,16,1024]{3,2,1,0:T(8,128)(2,1)}, u32[]{:S(2)}, u32[]{:S(2)}) collective-permute-start(bf16[4,8,16,1024]{3,2,1,0:T(8,128)(2,1)} %get-tuple-element.42), channel_id=1, source_target_pairs={{0,1},{1,0},{2,3},{3,2},{4,5},{5,4},{6,7},{7,6},{8,9},{9,8},{10,11... | collective-permute-start | bytes 3145736 | tf_op jit(solution)/shard_map/ppermute | solution.py:606
  7.8 42.5 %collective-permute-start = (bf16[4,8,16,1024]{3,2,1,0:T(8,128)(2,1)}, bf16[4,8,16,1024]{3,2,1,0:T(8,128)(2,1)}, u32[]{:S(2)}, u32[]{:S(2)}) collective-permute-start(bf16[4,8,16,1024]{3,2,1,0:T(8,128)(2,1)} %get-tuple-element.39), channel_id=1, source_target_pairs={{0,2},{1,3},{2,0},{3,1},{4,6},{5,7},{6,4},{7,5},{8,10},{9,11},{10,... | collective-permute-start | bytes 3145736 | tf_op jit(solution)/shard_map/ppermute | solution.py:606
  9.0 44.1 %collective-permute-start.1 = (bf16[4,8,16,1024]{3,2,1,0:T(8,128)(2,1)}, bf16[4,8,16,1024]{3,2,1,0:T(8,128)(2,1)}, u32[]{:S(2)}, u32[]{:S(2)}) collective-permute-start(bf16[4,8,16,1024]{3,2,1,0:T(8,128)(2,1)} %get-tuple-element.40), channel_id=1, source_target_pairs={{0,4},{1,5},{2,6},{3,7},{4,0},{5,1},{6,2},{7,3},{8,12},{9,13},{10,... | collective-permute-start | bytes 3145736 | tf_op jit(solution)/shard_map/ppermute | solution.py:606
  53.1 17.0 %collective-permute-start.6 = (bf16[4,8,16,1024]{3,2,1,0:T(8,128)(2,1)}, bf16[4,8,16,1024]{3,2,1,0:T(8,128)(2,1)}, u32[]{:S(2)}, u32[]{:S(2)}) collective-permute-start(bf16[4,8,16,1024]{3,2,1,0:T(8,128)(2,1)} %collective-permute-done.rest_0_.refs_5_), channel_id=1, source_target_pairs={{3,2},{0,1},{1,4},{6,3},{7,6},{4,5},{5,8},{10,7},{11,10},{8,9},{9,... | collective-permute-start | bytes 3145736 | tf_op jit(solution)/shard_map/ppermute | solution.py:657
  56.2 17.9 %collective-permute-start.7 = (bf16[4,8,16,1024]{3,2,1,0:T(8,128)(2,1)}, bf16[4,8,16,1024]{3,2,1,0:T(8,128)(2,1)}, u32[]{:S(2)}, u32[]{:S(2)}) collective-permute-start(bf16[4,8,16,1024]{3,2,1,0:T(8,128)(2,1)} %collective-permute-done.1.rest_1_.refs_6_), channel_id=1, source_target_pairs={{7,4},{0,3},{3,8},{12,7},{15,12},{8,11},{11,16},{20,15},{23,20},{1... | collective-permute-start | bytes 3145736 | tf_op jit(solution)/shard_map/ppermute | solution.py:656
  66.3 47.5 %collective-permute-start.13 = (bf16[16,4,16,1024]{3,2,1,0:T(8,128)(2,1)}, bf16[16,4,16,1024]{3,2,1,0:T(8,128)(2,1)}, u32[]{:S(2)}, u32[]{:S(2)}) collective-permute-start(bf16[16,4,16,1024]{3,2,1,0:T(8,128)(2,1)} %get-tuple-element.60), channel_id=1, source_target_pairs={{0,1},{1,0},{2,3},{3,2},{4,5},{5,4},{6,7},{7,6},{8,9},{9,8},{10,11... | collective-permute-start | bytes 6291464 | tf_op jit(solution)/shard_map/ppermute | solution.py:606
  66.4 7.7 %collective-permute-start.9 = (bf16[4,8,16,1024]{3,2,1,0:T(8,128)(2,1)}, bf16[4,8,16,1024]{3,2,1,0:T(8,128)(2,1)}, u32[]{:S(2)}, u32[]{:S(2)}) collective-permute-start(bf16[4,8,16,1024]{3,2,1,0:T(8,128)(2,1)} %get-tuple-element.40), channel_id=1, source_target_pairs={{1,2},{2,1},{5,6},{6,5},{9,10},{10,9},{13,14},{14,13},{17,18},{18,... | collective-permute-start | bytes 3145736 | tf_op jit(solution)/shard_map/ppermute | solution.py:653
  68.1 44.5 %collective-permute-start.11 = (bf16[8,4,16,1024]{3,2,1,0:T(8,128)(2,1)}, bf16[8,4,16,1024]{3,2,1,0:T(8,128)(2,1)}, u32[]{:S(2)}, u32[]{:S(2)}) collective-permute-start(bf16[8,4,16,1024]{3,2,1,0:T(8,128)(2,1)} %get-tuple-element.58), channel_id=1, source_target_pairs={{0,4},{1,5},{2,6},{3,7},{4,0},{5,1},{6,2},{7,3},{8,12},{9,13},{10,... | collective-permute-start | bytes 3145736 | tf_op jit(solution)/shard_map/ppermute | solution.py:606
  74.1 39.7 %collective-permute-start.8 = (bf16[8,4,16,1024]{3,2,1,0:T(8,128)(2,1)}, bf16[8,4,16,1024]{3,2,1,0:T(8,128)(2,1)}, u32[]{:S(2)}, u32[]{:S(2)}) collective-permute-start(bf16[8,4,16,1024]{3,2,1,0:T(8,128)(2,1)} %get-tuple-element.51), channel_id=1, source_target_pairs={{0,2},{1,3},{2,0},{3,1},{4,6},{5,7},{6,4},{7,5},{8,10},{9,11},{10,... | collective-permute-start | bytes 3145736 | tf_op jit(solution)/shard_map/ppermute | solution.py:606
  92.3 39.8 %collective-permute-start.10 = (bf16[8,4,16,1024]{3,2,1,0:T(8,128)(2,1)}, bf16[8,4,16,1024]{3,2,1,0:T(8,128)(2,1)}, u32[]{:S(2)}, u32[]{:S(2)}) collective-permute-start(bf16[8,4,16,1024]{3,2,1,0:T(8,128)(2,1)} %get-tuple-element.57), channel_id=1, source_target_pairs={{0,3},{1,2},{2,1},{3,0},{4,7},{5,6},{6,5},{7,4},{8,11},{9,10},{10,... | collective-permute-start | bytes 3145736 | tf_op jit(solution)/shard_map/ppermute | solution.py:606
  92.9 42.8 %collective-permute-start.12 = (bf16[8,4,16,1024]{3,2,1,0:T(8,128)(2,1)}, bf16[8,4,16,1024]{3,2,1,0:T(8,128)(2,1)}, u32[]{:S(2)}, u32[]{:S(2)}) collective-permute-start(bf16[8,4,16,1024]{3,2,1,0:T(8,128)(2,1)} %get-tuple-element.59), channel_id=1, source_target_pairs={{0,5},{1,4},{2,7},{3,6},{4,1},{5,0},{6,3},{7,2},{8,13},{9,12},{10,... | collective-permute-start | bytes 3145736 | tf_op jit(solution)/shard_map/ppermute | solution.py:606
